TPU v7x, 32 devices: a whole 2x2x4 slice. The times are simulated.
32 devices in a mesh: dp: 32 (over z, y, x, core).
Axes of the slice: x: 2, y: 2, z: 4, core: 2. Of those that a mesh axis runs over, the one named last changes fastest.
Arguments:
- images: bfloat16 [64, 197, 384], P('dp'), may hold values from -6 to 6
- params: bfloat16 [1777664], P('dp'), may hold values from -1.2 to 1.4
- cotangent: bfloat16 [64, 197, 384], P('dp'), may hold values from -6 to 6
- counts: int32 [32], P('dp'), may hold values from 1 to 2, as said below
Outputs:
- block_out: bfloat16 [64, 197, 384], P('dp')
- image_grad: bfloat16 [64, 197, 384], P('dp')
- param_grad: float32 [1777664], P('dp')
Inputs may be any that keep to these rules, and one draw needn't show every extreme that they name: `counts`: every device has 1 to 2 live images; some device has exactly 2 and some exactly 1.
All inputs are finite; a program needn't handle non-finite values.
Results may differ from a plain program's by a relative error of at most 0.0075.
Values may be sent and summed in bfloat16 or wider, within the bound.
No kernel may reach another device: no remote copies, remote signals or barrier semaphores. Data moves between devices by JAX's collectives and lax.ppermute only.
A program may use at most 128 MiB of HBM per device.

v0:
```python
import jax
import jax.numpy as jnp
from jax import lax
from jax.sharding import PartitionSpec as P

D = 384
HEADS = 6
FF = 1536
TOK = 197
MB = 2
CAP = 1


EPSILON = 1e-06
SQRT_HALF = 0.7071067811865476
INV_ROOT_TAU = 0.3989422804014327


def param_layout():
    return [
        ("w_qkv", (D, 3 * D)),
        ("b_query", (D,)),
        ("b_value", (D,)),
        ("w_out", (D, D)),
        ("b_out", (D,)),
        ("w_up", (D, FF)),
        ("b_up", (FF,)),
        ("w_down", (FF, D)),
        ("b_down", (D,)),
        ("g_first", (D,)),
        ("b_first", (D,)),
        ("g_second", (D,)),
        ("b_second", (D,)),
    ]


def unpack_flat(flat_buffer):
    pieces = {}
    position = 0
    for entry_name, entry_shape in param_layout():
        entry_size = 1
        for extent_value in entry_shape:
            entry_size = entry_size * extent_value
        pieces[entry_name] = flat_buffer[position : position + entry_size].reshape(entry_shape)
        position = position + entry_size
    return pieces


def fetch_weights(params):
    return unpack_flat(lax.all_gather(params, "dp", axis=0, tiled=True))


def standardize(values):
    centre = values - jnp.mean(values, -1, keepdims=True)
    inverse = lax.rsqrt(jnp.mean(centre * centre, -1, keepdims=True) + EPSILON)
    return (centre * inverse, inverse)


def left_product(first, second):
    return lax.dot_general(
        first, second, (((0,), (0,)), ((), ())), preferred_element_type=jnp.float32
    )


def right_product(first, second):
    return lax.dot_general(
        first, second, (((1,), (1,)), ((), ())), preferred_element_type=jnp.float32
    )


def norm_back(grad_normed, normed_rows, inverse, gain):
    scaled = grad_normed * gain
    return inverse * (
        scaled
        - jnp.mean(scaled, -1, keepdims=True)
        - normed_rows * jnp.mean(scaled * normed_rows, -1, keepdims=True)
    )


def gelu_slope(values):
    return 0.5 * (1.0 + lax.erf(values * SQRT_HALF)) + values * INV_ROOT_TAU * jnp.exp(
        -0.5 * values * values
    )


def head_split(values, image_count):
    return values.reshape(image_count, TOK, HEADS, D // HEADS)


def as_float(values):
    return values.astype(jnp.float32)


def forward_pass(weights, image_block):
    image_count = image_block.shape[0]
    scale = float(D // HEADS) ** (-0.5)
    tokens_in = image_block.reshape(-1, D).astype(jnp.float32)
    first_hat, first_inv = standardize(tokens_in)
    normed = (first_hat * as_float(weights["g_first"]) + as_float(weights["b_first"])).astype(
        jnp.bfloat16
    )
    joined = jnp.dot(normed, weights["w_qkv"], preferred_element_type=jnp.float32)
    query = (joined[:, :D] + as_float(weights["b_query"])).astype(jnp.bfloat16)
    keys_all = joined[:, D : 2 * D].astype(jnp.bfloat16)
    values_all = (joined[:, 2 * D :] + as_float(weights["b_value"])).astype(jnp.bfloat16)
    raw_scores = (
        jnp.einsum(
            "bqhd,bkhd->bhqk",
            head_split(query, image_count),
            head_split(keys_all, image_count),
            preferred_element_type=jnp.float32,
        )
        * scale
    )
    peak = jnp.max(raw_scores, -1, keepdims=True)
    log_total = peak + jnp.log(jnp.sum(jnp.exp(raw_scores - peak), -1, keepdims=True))
    probs_low = jnp.exp(raw_scores - log_total).astype(jnp.bfloat16)
    mixed = (
        jnp.einsum(
            "bhqk,bkhd->bqhd",
            probs_low,
            head_split(values_all, image_count),
            preferred_element_type=jnp.float32,
        )
        .reshape(-1, D)
        .astype(jnp.bfloat16)
    )
    middle = tokens_in + (
        jnp.dot(mixed, weights["w_out"], preferred_element_type=jnp.float32)
        + as_float(weights["b_out"])
    )
    second_hat, second_inv = standardize(middle)
    second = (second_hat * as_float(weights["g_second"]) + as_float(weights["b_second"])).astype(
        jnp.bfloat16
    )
    hidden_pre = jnp.dot(second, weights["w_up"], preferred_element_type=jnp.float32) + as_float(
        weights["b_up"]
    )
    hidden = jax.nn.gelu(hidden_pre, approximate=False).astype(jnp.bfloat16)
    result = middle + (
        jnp.dot(hidden, weights["w_down"], preferred_element_type=jnp.float32)
        + as_float(weights["b_down"])
    )
    saved = (
        first_hat,
        first_inv,
        normed,
        query,
        keys_all,
        values_all,
        log_total,
        mixed,
        second_hat,
        second_inv,
        second,
        hidden_pre,
        hidden,
    )
    return (result.astype(jnp.bfloat16).reshape(image_block.shape), saved)


def backward_pass(weights, saved, grad_out):
    (
        first_hat,
        first_inv,
        normed,
        query,
        keys_all,
        values_all,
        log_total,
        mixed,
        second_hat,
        second_inv,
        second,
        hidden_pre,
        hidden,
    ) = saved
    image_count = query.shape[0] // TOK
    scale = float(D // HEADS) ** (-0.5)
    grads = {}
    grad_low = grad_out.astype(jnp.bfloat16)
    grads["w_down"] = left_product(hidden, grad_low)
    grads["b_down"] = jnp.sum(as_float(grad_low), 0)
    grad_pre = (right_product(grad_low, weights["w_down"]) * gelu_slope(hidden_pre)).astype(
        jnp.bfloat16
    )
    grads["w_up"] = left_product(second, grad_pre)
    grads["b_up"] = jnp.sum(as_float(grad_pre), 0)
    grad_second = right_product(grad_pre, weights["w_up"])
    grads["g_second"] = jnp.sum(grad_second * second_hat, 0)
    grads["b_second"] = jnp.sum(grad_second, 0)
    grad_middle = grad_out + norm_back(
        grad_second, second_hat, second_inv, as_float(weights["g_second"])
    )
    grad_attn = grad_middle.astype(jnp.bfloat16)
    grads["w_out"] = left_product(mixed, grad_attn)
    grads["b_out"] = jnp.sum(as_float(grad_attn), 0)
    grad_mixed = head_split(
        right_product(grad_attn, weights["w_out"]).astype(jnp.bfloat16), image_count
    )
    query_heads = head_split(query, image_count)
    key_heads = head_split(keys_all, image_count)
    value_heads = head_split(values_all, image_count)
    raw_scores = (
        jnp.einsum("bqhd,bkhd->bhqk", query_heads, key_heads, preferred_element_type=jnp.float32)
        * scale
    )
    probs = jnp.exp(raw_scores - log_total)
    probs_low = probs.astype(jnp.bfloat16)
    grad_values = jnp.einsum(
        "bhqk,bqhd->bkhd", probs_low, grad_mixed, preferred_element_type=jnp.float32
    )
    grad_probs = jnp.einsum(
        "bqhd,bkhd->bhqk", grad_mixed, value_heads, preferred_element_type=jnp.float32
    )
    grad_scores = (probs * (grad_probs - jnp.sum(grad_probs * probs, -1, keepdims=True))).astype(
        jnp.bfloat16
    )
    grad_query = (
        jnp.einsum("bhqk,bkhd->bqhd", grad_scores, key_heads, preferred_element_type=jnp.float32)
        * scale
    )
    grad_keys = (
        jnp.einsum("bhqk,bqhd->bkhd", grad_scores, query_heads, preferred_element_type=jnp.float32)
        * scale
    )
    grad_joined = jnp.concatenate(
        [grad_query.reshape(-1, D), grad_keys.reshape(-1, D), grad_values.reshape(-1, D)], 1
    ).astype(jnp.bfloat16)
    grads["w_qkv"] = left_product(normed, grad_joined)
    joined_sums = jnp.sum(as_float(grad_joined), 0)
    grads["b_query"] = joined_sums[:D]
    grads["b_value"] = joined_sums[2 * D :]
    grad_first = right_product(grad_joined, weights["w_qkv"])
    grads["g_first"] = jnp.sum(grad_first * first_hat, 0)
    grads["b_first"] = jnp.sum(grad_first, 0)
    grad_in = grad_middle + norm_back(
        grad_first, first_hat, first_inv, as_float(weights["g_first"])
    )
    return (grads, grad_in.astype(jnp.bfloat16))


def on_device(images, params, cotangent, counts):
    full_length = params.shape[0] * lax.axis_size("dp")
    live_total = counts[0]
    totals = {}
    outputs = []
    in_grads = []
    weights = None
    for micro_step in range(MB):
        weights = fetch_weights(params)
        block_in = images[micro_step * CAP : (micro_step + 1) * CAP]
        result, saved = forward_pass(weights, block_in)
        outputs.append(result)
        weights = unpack_flat(lax.all_gather(params, "dp", axis=0, tiled=True))
        live = (micro_step * CAP + jnp.arange(CAP, dtype=jnp.int32) < live_total).astype(
            jnp.float32
        )
        grad_out = (
            cotangent[micro_step * CAP : (micro_step + 1) * CAP].astype(jnp.float32)
            * live[:, None, None]
        ).reshape(-1, D)
        grads, grad_in = backward_pass(weights, saved, grad_out)
        in_grads.append(grad_in.reshape(block_in.shape))
        for entry_name, entry_shape in param_layout():
            if micro_step == 0:
                totals[entry_name] = grads[entry_name]
            else:
                totals[entry_name] = totals[entry_name] + grads[entry_name]
    pieces = [totals[entry_name].reshape(-1) for entry_name, entry_shape in param_layout()]
    used_length = sum([piece_part.shape[0] for piece_part in pieces])
    pieces.append(jnp.zeros((full_length - used_length,), jnp.float32))
    flat_grad = jnp.concatenate(pieces)
    owned = lax.psum_scatter(flat_grad, "dp", scatter_dimension=0, tiled=True)
    return (jnp.concatenate(outputs, 0), jnp.concatenate(in_grads, 0), owned)


def solution(mesh):
    placed = (P("dp", None, None), P("dp"), P("dp", None, None), P("dp"))
    return jax.shard_map(
        on_device,
        mesh=mesh,
        in_specs=placed,
        out_specs=(P("dp", None, None), P("dp", None, None), P("dp")),
        check_vma=False,
    )
```

profile of v0, /device:TPU:0, one launch (start us, length us, event | category | flops | bytes accessed | tf_op | source)
XLA Modules:
  0.0 429.4 jit_solution(1542696043808574378)
XLA Ops:
  7.2 1.7 reshape.453
  9.7 1.6 fusion.136
  16.0 70.9 %all-gather.3.cloned.1.call-done = bf16[32,1,55552]{2,1,0:T(2,128)(2,1)} async-done(((bf16[1,1,55552]{2,1,0:T(2,128)(2,1)}), bf16[32,1,55552]{2,1,0:T(2,128)(2,1)}) %all-gather.3.cloned.1.call-update) | async-done | bytes 3555344 | tf_op jit(solution)/shard_map/all_gather | solution.py:50
  86.9 21.0 %reduce.14 = bf16[32,55552]{1,0:T(8,128)(2,1)S(1)} reduce(bf16[32,1,55552]{2,1,0:T(2,128)(2,1)} %all-gather.3.cloned.1.call-done, bf16[]{:T(256)} %constant.101), dimensions={1}, to_apply=%all-gather.reduce_sub_computation | reduce | bytes 7110658 | tf_op jit(solution)/shard_map/all_gather | solution.py:50
  108.0 7.0 %reshape.454 = bf16[1777664]{0:T(1024)(128)(2,1)} reshape(bf16[32,55552]{1,0:T(8,128)(2,1)S(1)} %reduce.14) | data formatting | bytes 7110656
  116.4 1.7 slice.143
  119.4 3.7 fusion.134
  129.6 2.2 reshape.428
  133.3 1.6 reshape.429
  136.0 1.8 copy.61
  137.8 1.7 copy.62
  142.5 3.8 fusion.7
  146.4 3.8 fusion.4
  154.3 1.9 convert_reduce_fusion.9
  158.8 1.7 copy.75
  160.5 2.0 convolution_convert_fusion
  168.5 1.9 fusion.63
  175.6 1.8 convolution_add_fusion
  177.4 2.5 reshape.447
  179.9 3.0 constant_dynamic-update-slice_fusion.9
  186.6 1.9 reshape.448
  188.6 3.1 convolution_add_fusion.2
  191.6 2.4 reshape.449
  194.1 1.8 fusion.125
  195.8 2.0 convolution_add_fusion.1
  197.9 3.3 reshape.450
  201.1 2.2 constant_dynamic-update-slice_fusion.6
  204.7 20.3 %dynamic-update-slice.5 = f32[1777664]{0:T(1024)} dynamic-update-slice(f32[1777664]{0:T(1024)} %constant_dynamic-update-slice_fusion.5, f32[589824]{0:T(1024)S(1)} %reshape.449, s32[]{} %constant.107) | dynamic-update-slice | bytes 4718596
  226.3 21.2 %dynamic-update-slice.7 = f32[1777664]{0:T(1024)} dynamic-update-slice(f32[1777664]{0:T(1024)} %add_dynamic-update-slice_fusion, f32[589824]{0:T(1024)} %reshape.450, s32[]{} %constant.109) | dynamic-update-slice | bytes 4718596
  257.8 1.6 fusion.39
  262.1 158.3 %all-reduce.3.cloned.1.call-done = f32[1777664]{0:T(1024)} async-done(((f32[1777664]{0:T(1024)}), f32[1777664]{0:T(1024)}) %all-reduce.3.cloned.1.call-update) | async-done | bytes 7110672
  420.4 1.8 dynamic-slice
  (272 shorter events, 56.1 us)
Async XLA Ops:
  7.2 79.8 %all-gather.3.cloned.1.call-start = ((), (), s32[]{:S(2)}) async-start(), calls=%async_computation | async-start | bytes 7332864 | tf_op jit(solution)/shard_map/all_gather | solution.py:50
  8.9 411.5 %all-reduce.3.cloned.1.call-start = ((), (), s32[]{:S(2)}) async-start(), calls=%async_computation.1 | async-start | bytes 14221312
  9.6 3.4 copy-start.47
  116.4 15.8 %copy-start.64 = (f32[384]{0:T(512)}, f32[384]{0:T(512)S(1)}, u32[]{:S(2)}) copy-start(f32[384]{0:T(512)S(1)} %get-tuple-element.43) | copy-start | bytes 4612
  119.4 3.7 slice-start
  127.4 4.4 %copy-start.29 = (bf16[197,384]{0,1:T(8,128)(2,1)}, bf16[197,384]{0,1:T(8,128)(2,1)S(1)}, u32[]{:S(2)}) copy-start(bf16[197,384]{0,1:T(8,128)(2,1)S(1)} %copy.65) | copy-start | bytes 453892
  136.0 5.2 %copy-start.31 = (bf16[197,384]{0,1:T(8,128)(2,1)}, bf16[197,384]{0,1:T(8,128)(2,1)S(1)}, u32[]{:S(2)}) copy-start(bf16[197,384]{0,1:T(8,128)(2,1)S(1)} %copy.60) | copy-start | bytes 453892
  142.3 12.1 %copy-start.69 = (f32[197]{0:T(256)}, f32[197]{0:T(256)S(1)}, u32[]{:S(2)}) copy-start(f32[197]{0:T(256)S(1)} %broadcast_multiply_fusion.10) | copy-start | bytes 2368
  142.5 11.9 %copy-start.73 = (f32[197]{0:T(256)}, f32[197]{0:T(256)S(1)}, u32[]{:S(2)}) copy-start(f32[197]{0:T(256)S(1)} %add_rsqrt_fusion.2) | copy-start | bytes 2368
  146.4 3.8 copy-start
  146.4 3.8 copy-start.44
  164.2 8.3 %copy-start.23 = (bf16[6,64,197]{2,1,0:T(8,128)(2,1)}, bf16[6,64,197]{2,1,0:T(8,128)(2,1)S(1)}, u32[]{:S(2)}) copy-start(bf16[6,64,197]{2,1,0:T(8,128)(2,1)S(1)} %fusion.35) | copy-start | bytes 453892
  164.5 8.1 %copy-start.25 = (bf16[6,64,197]{2,1,0:T(8,128)(2,1)}, bf16[6,64,197]{2,1,0:T(8,128)(2,1)S(1)}, u32[]{:S(2)}) copy-start(bf16[6,64,197]{2,1,0:T(8,128)(2,1)S(1)} %fusion.34) | copy-start | bytes 453892
  179.9 5.6 %copy-start.11 = (f32[197,384]{1,0:T(8,128)S(1)}, f32[197,384]{1,0:T(8,128)}, u32[]{:S(2)}) copy-start(f32[197,384]{1,0:T(8,128)} %copy-done.10) | copy-start | bytes 907780
  179.9 5.6 %copy-start.21 = (f32[384,384]{1,0:T(8,128)S(1)}, f32[384,384]{1,0:T(8,128)}, u32[]{:S(2)}) copy-start(f32[384,384]{1,0:T(8,128)} %fusion.128) | copy-start | bytes 1769476
  179.9 5.6 %copy-start.28 = (bf16[6,64,197]{2,1,0:T(8,128)(2,1)S(1)}, bf16[6,64,197]{2,1,0:T(8,128)(2,1)}, u32[]{:S(2)}) copy-start(bf16[6,64,197]{2,1,0:T(8,128)(2,1)} %copy-done.27) | copy-start | bytes 453892
  185.5 3.1 copy-start.61
  185.5 3.1 copy-start.72
  197.9 5.5 %copy-start.77 = (f32[384]{0:T(512)S(1)}, f32[384]{0:T(512)}, u32[]{:S(2)}) copy-start(f32[384]{0:T(512)} %get-tuple-element.32) | copy-start | bytes 4612
  197.9 5.5 %copy-start.83 = (f32[384]{0:T(512)S(1)}, f32[384]{0:T(512)}, u32[]{:S(2)}) copy-start(f32[384]{0:T(512)} %get-tuple-element.34) | copy-start | bytes 4612
  204.7 20.3 %copy-start.78 = (f32[1536]{0:T(1024)S(1)}, f32[1536]{0:T(1024)}, u32[]{:S(2)}) copy-start(f32[1536]{0:T(1024)} %get-tuple-element.84) | copy-start | bytes 18436
  204.7 20.3 %copy-start.79 = (f32[1536]{0:T(1024)S(1)}, f32[1536]{0:T(1024)}, u32[]{:S(2)}) copy-start(f32[1536]{0:T(1024)} %get-tuple-element.86) | copy-start | bytes 18436
  226.2 21.3 %copy-start.75 = (f32[384]{0:T(512)S(1)}, f32[384]{0:T(512)}, u32[]{:S(2)}) copy-start(f32[384]{0:T(512)} %get-tuple-element.28) | copy-start | bytes 4612
  226.2 21.3 %copy-start.76 = (f32[384]{0:T(512)S(1)}, f32[384]{0:T(512)}, u32[]{:S(2)}) copy-start(f32[384]{0:T(512)} %get-tuple-element.90) | copy-start | bytes 4612
  226.2 22.6 %copy-start.14 = (f32[197,384]{1,0:T(8,128)S(1)}, f32[197,384]{1,0:T(8,128)}, u32[]{:S(2)}) copy-start(f32[197,384]{1,0:T(8,128)} %get-tuple-element.35) | copy-start | bytes 907780
  226.2 22.6 %copy-start.46 = (f32[197,384]{1,0:T(8,128)S(1)}, f32[197,384]{1,0:T(8,128)}, u32[]{:S(2)}) copy-start(f32[197,384]{1,0:T(8,128)} %fusion.131) | copy-start | bytes 907780
  226.2 22.6 %copy-start.50 = (f32[197,384]{1,0:T(8,128)S(1)}, f32[197,384]{1,0:T(8,128)}, u32[]{:S(2)}) copy-start(f32[197,384]{1,0:T(8,128)} %get-tuple-element.83) | copy-start | bytes 907780
  247.5 3.7 copy-start.88
  247.5 5.1 %copy-start.82 = (f32[384]{0:T(512)S(1)}, f32[384]{0:T(512)}, u32[]{:S(2)}) copy-start(f32[384]{0:T(512)} %get-tuple-element.64) | copy-start | bytes 4612
  247.5 5.1 %copy-start.87 = (f32[384]{0:T(512)S(1)}, f32[384]{0:T(512)}, u32[]{:S(2)}) copy-start(f32[384]{0:T(512)} %get-tuple-element.14) | copy-start | bytes 4612
  247.5 6.4 %copy-start.81 = (f32[384]{0:T(512)S(1)}, f32[384]{0:T(512)}, u32[]{:S(2)}) copy-start(f32[384]{0:T(512)} %get-tuple-element.61) | copy-start | bytes 4612
  247.5 6.4 %copy-start.86 = (f32[384]{0:T(512)S(1)}, f32[384]{0:T(512)}, u32[]{:S(2)}) copy-start(f32[384]{0:T(512)} %get-tuple-element.25) | copy-start | bytes 4612
  (61 other events, 82.8 us)
Sparse Core Ops, SparseCore 0:
  11.6 75.2 all-gather.2
  256.7 163.6 all-reduce.2
where the time goes:
time: 436 us; the launch traced here: 429 us
  waiting for transfers between devices  229 us (53%)
  local copies, waits for them, and re-layouts  99.4 us (23%)
  other arithmetic  43.9 us (10%)
  matrix products  40.7 us (9%)
  between operations  16.1 us (4%)
    unnamed x3, waiting for transfers between devices  158 us
    all_gather x1, waiting for transfers between devices, fetch_weights(): return unpack_flat(lax.all_gather(params, 'dp', axis=0, tiled=True))  70.9 us
    unnamed x189, local copies, waits for them, and re-layouts  66.8 us
    all_gather x1, other arithmetic, fetch_weights(): return unpack_flat(lax.all_gather(params, 'dp', axis=0, tiled=True))  21 us
    dot_general x8, matrix products, left_product(): lax.dot_general(first, second, (((0,), (0,)), ((), ())), preferred_elemen...  12 us
    unnamed x9, other arithmetic  11.8 us
    dot_general x8, matrix products, right_product(): lax.dot_general(first, second, (((1,), (1,)), ((), ())), preferred_elemen...  10.4 us
    reshape x4, local copies, waits for them, and re-layouts, on_device(): totals[entry_name].reshape(-1)  10.1 us
  transfers between devices with their start and end apart: 2, of which 2 were waited for; matrix products, arithmetic and copies ran while one was open for 2% of the time, Pallas kernels for 0%

commit v1 on v0

v1 whole, which is shorter than its diff:
```python
import jax
import jax.numpy as jnp
from jax import lax
from jax.experimental import pallas as pl
from jax.experimental.pallas import tpu as pltpu
from jax.sharding import PartitionSpec as P

D = 384
HEADS = 6
FF = 1536
LANES = 128
EPSILON = 1e-06
SQRT_HALF = 0.7071067811865476
INV_ROOT_TAU = 0.3989422804014327
BF = jnp.bfloat16
F32 = jnp.float32

R_QKV = 0
R_BQ = R_QKV + D * 3 * D // LANES
R_BV = R_BQ + D // LANES
R_OUT = R_BV + D // LANES
R_BO = R_OUT + D * D // LANES
R_UP = R_BO + D // LANES
R_BU = R_UP + D * FF // LANES
R_DOWN = R_BU + FF // LANES
R_BD = R_DOWN + D * FF // LANES
R_G1 = R_BD + D // LANES
R_B1 = R_G1 + D // LANES
R_G2 = R_B1 + D // LANES
R_B2 = R_G2 + D // LANES
R_END = R_B2 + D // LANES


def dot_nn(a, b):
    return lax.dot_general(a, b, (((1,), (0,)), ((), ())), preferred_element_type=F32)


def dot_nt(a, b):
    return lax.dot_general(a, b, (((1,), (1,)), ((), ())), preferred_element_type=F32)


def dot_tn(a, b):
    return lax.dot_general(a, b, (((0,), (0,)), ((), ())), preferred_element_type=F32)


def row_vector(ref, row, count):
    return jnp.concatenate([ref[row + i : row + i + 1, :] for i in range(count)], axis=1)


def put_row_vector(ref, row, value):
    for i in range(value.shape[1] // LANES):
        ref[row + i : row + i + 1, :] = value[:, i * LANES : (i + 1) * LANES]


def fold_rows(value):
    return jnp.sum(value.reshape(-1, 8, value.shape[-1]), axis=0)


def layer_body(
    me_ref,
    count_ref,
    image_ref,
    cot_ref,
    *refs,
    devices,
    rows,
    images,
    tok,
    pad,
):
    pieces = refs[:devices]
    (out_ref, gin_ref, send_ref, keep_ref) = refs[devices : devices + 4]
    (
        stage,
        wide,
        wq,
        wo,
        wu,
        wd,
        x_s,
        n1_s,
        r1_s,
        normed,
        qkv,
        probs,
        mixed,
        mid_s,
        n2_s,
        r2_s,
        second,
        hidden,
        gpre,
        acc,
        acc2,
        glow,
        gattn,
        gmix,
        gj,
        sems,
    ) = refs[devices + 4 :]
    me = me_ref[0]
    total = images * pad
    scale = float(D // HEADS) ** (-0.5)
    blk = 32
    steps = total // blk
    copies = [
        pltpu.make_async_copy(pieces[k], stage.at[me ^ k], sems.at[k]) for k in range(devices)
    ]
    for c in copies:
        c.start()

    for b in range(images):
        live = (count_ref[0] > b).astype(F32)
        zeros = jnp.zeros((pad - tok, D), F32)
        x_s[b * pad : (b + 1) * pad, :] = jnp.concatenate(
            [image_ref[b].astype(F32), zeros], axis=0
        )
        glow[b * pad : (b + 1) * pad, :] = jnp.concatenate(
            [cot_ref[b].astype(F32) * live, zeros], axis=0
        ).astype(BF)

    for c in copies:
        c.wait()
    for d in range(devices):
        wide[d * rows : (d + 1) * rows, :] = stage[d].astype(F32)

    def unpack(dst, start, height, width):
        per = width // LANES
        for j in range(per):
            dst[:, j * LANES : (j + 1) * LANES] = wide[
                pl.ds(start + j, height, stride=per), :
            ].astype(BF)

    unpack(wq, R_QKV, D, 3 * D)
    unpack(wo, R_OUT, D, D)
    unpack(wu, R_UP, D, FF)
    unpack(wd, R_DOWN, FF, D)
    b_query = row_vector(wide, R_BQ, 3)
    b_value = row_vector(wide, R_BV, 3)
    b_out = row_vector(wide, R_BO, 3)
    b_up = row_vector(wide, R_BU, 12)
    b_down = row_vector(wide, R_BD, 3)
    g_first = row_vector(wide, R_G1, 3)
    b_first = row_vector(wide, R_B1, 3)
    g_second = row_vector(wide, R_G2, 3)
    b_second = row_vector(wide, R_B2, 3)

    def blocks(body, init=None):
        def step(i, carry):
            return body(pl.ds(pl.multiple_of(i * blk, blk), blk), carry)

        return lax.fori_loop(0, steps, step, init)

    def standardize(v):
        centre = v - jnp.mean(v, axis=-1, keepdims=True)
        inverse = lax.rsqrt(jnp.mean(centre * centre, axis=-1, keepdims=True) + EPSILON)
        return centre * inverse, inverse

    def first_norm(at, carry):
        hat, inverse = standardize(x_s[at, :])
        n1_s[at, :] = hat
        r1_s[at, :] = inverse
        normed[at, :] = (hat * g_first + b_first).astype(BF)
        return carry

    blocks(first_norm)

    qkv[:, :D] = (dot_nn(normed[...], wq[:, :D]) + b_query).astype(BF)
    qkv[:, D : 2 * D] = dot_nn(normed[...], wq[:, D : 2 * D]).astype(BF)
    qkv[:, 2 * D :] = (dot_nn(normed[...], wq[:, 2 * D :]) + b_value).astype(BF)

    lane = lax.broadcasted_iota(jnp.int32, (1, LANES), 1)
    low_lane = lane < D // HEADS
    halves = (low_lane.astype(F32).astype(BF), (1.0 - low_lane.astype(F32)).astype(BF))
    key_ok = lax.broadcasted_iota(jnp.int32, (1, pad), 1) < tok

    def slab(ref, b, column):
        return ref[b * pad : (b + 1) * pad, column : column + LANES]

    for b in range(images):
        for h in range(HEADS // 2):
            query = slab(qkv, b, h * LANES)
            keys = slab(qkv, b, D + h * LANES)
            values = slab(qkv, b, 2 * D + h * LANES)
            outs = []
            for s in range(2):
                scores = jnp.where(key_ok, dot_nt(query * halves[s], keys) * scale, -1e30)
                top = jnp.max(scores, axis=-1, keepdims=True)
                weight = jnp.exp(scores - top)
                prob = weight * (1.0 / jnp.sum(weight, axis=-1, keepdims=True))
                probs[(b * HEADS // 2 + h) * 2 + s] = prob
                outs.append(dot_nn(prob.astype(BF), values))
            mixed[b * pad : (b + 1) * pad, h * LANES : (h + 1) * LANES] = jnp.where(
                low_lane, outs[0], outs[1]
            ).astype(BF)

    acc[...] = dot_nn(mixed[...], wo[...])

    def second_norm(at, carry):
        middle = x_s[at, :] + (acc[at, :] + b_out)
        mid_s[at, :] = middle
        hat, inverse = standardize(middle)
        n2_s[at, :] = hat
        r2_s[at, :] = inverse
        second[at, :] = (hat * g_second + b_second).astype(BF)
        return carry

    blocks(second_norm)

    wide[R_END:, :] = jnp.zeros((devices * rows - R_END, LANES), F32)

    def scatter(value, start, per):
        for j in range(value.shape[1] // LANES):
            wide[pl.ds(start + j, value.shape[0], stride=per), :] = value[
                :, j * LANES : (j + 1) * LANES
            ]

    for c in range(FF // D):
        cols = slice(c * D, (c + 1) * D)
        acc[...] = dot_nn(second[...], wu[:, cols])
        acc2[...] = dot_nt(glow[...], wd[cols, :])
        bias = b_up[:, cols]

        def activate(at, carry, cols=cols, bias=bias):
            pre = acc[at, :] + bias
            cdf = 0.5 * (1.0 + lax.erf(pre * SQRT_HALF))
            hidden[at, cols] = (pre * cdf).astype(BF)
            slope = cdf + pre * INV_ROOT_TAU * jnp.exp(-0.5 * pre * pre)
            back = (acc2[at, :] * slope).astype(BF)
            gpre[at, cols] = back
            return carry + fold_rows(back.astype(F32))

        sums = blocks(activate, jnp.zeros((8, D), F32))
        put_row_vector(wide, R_BU + 3 * c, jnp.sum(sums, axis=0, keepdims=True))
        scatter(dot_tn(second[...], gpre[:, cols]), R_UP + 3 * c, FF // LANES)
        scatter(dot_tn(hidden[:, cols], glow[...]), R_DOWN + 3 * D * c, D // LANES)

    acc[...] = dot_nn(hidden[...], wd[...])
    acc2[...] = dot_nt(gpre[...], wu[...])

    def second_back(at, carry):
        sum_g, sum_b, sum_low, sum_attn = carry
        grad = acc2[at, :]
        hat = n2_s[at, :]
        low = glow[at, :].astype(F32)
        mixed_block = mid_s[at, :] + (acc[at, :] + b_down)
        gmix[at, :] = mixed_block.astype(BF)
        s = grad * g_second
        middle_grad = low + r2_s[at, :] * (
            s
            - jnp.mean(s, axis=-1, keepdims=True)
            - hat * jnp.mean(s * hat, axis=-1, keepdims=True)
        )
        mid_s[at, :] = middle_grad
        attn = middle_grad.astype(BF)
        gattn[at, :] = attn
        return (
            sum_g + fold_rows(grad * hat),
            sum_b + fold_rows(grad),
            sum_low + fold_rows(low),
            sum_attn + fold_rows(attn.astype(F32)),
        )

    zero8 = jnp.zeros((8, D), F32)
    sum_g, sum_b, sum_low, sum_attn = blocks(second_back, (zero8, zero8, zero8, zero8))

    def put_sum(row, value):
        put_row_vector(wide, row, jnp.sum(value, axis=0, keepdims=True))

    put_sum(R_G2, sum_g)
    put_sum(R_B2, sum_b)
    put_sum(R_BD, sum_low)
    put_sum(R_BO, sum_attn)
    for b in range(images):
        out_ref[b] = gmix[b * pad : b * pad + tok, :]

    scatter(dot_tn(mixed[...], gattn[...]), R_OUT, D // LANES)
    gmix[...] = dot_nt(gattn[...], wo[...]).astype(BF)

    for b in range(images):
        for h in range(HEADS // 2):
            query = slab(qkv, b, h * LANES)
            keys = slab(qkv, b, D + h * LANES)
            values = slab(qkv, b, 2 * D + h * LANES)
            grads = slab(gmix, b, h * LANES)
            parts = []
            for s in range(2):
                prob = probs[(b * HEADS // 2 + h) * 2 + s]
                grad_prob = dot_nt(grads * halves[s], values)
                total_s = jnp.sum(grad_prob * prob, axis=-1, keepdims=True)
                grad_score = (prob * (grad_prob - total_s)).astype(BF)
                parts.append(
                    (
                        dot_nn(grad_score, keys) * scale,
                        dot_tn(grad_score, query) * scale,
                        dot_tn(prob.astype(BF), grads),
                    )
                )
            for t in range(3):
                column = t * D + h * LANES
                gj[b * pad : (b + 1) * pad, column : column + LANES] = jnp.where(
                    low_lane, parts[0][t], parts[1][t]
                ).astype(BF)

    for t in range(3):
        scatter(dot_tn(normed[...], gj[:, t * D : (t + 1) * D]), R_QKV + 3 * t, 3 * D // LANES)
    acc[...] = dot_nt(gj[...], wq[...])

    def first_back(at, carry):
        sum_g, sum_b, sum_q, sum_v = carry
        grad = acc[at, :]
        hat = n1_s[at, :]
        s = grad * g_first
        result = mid_s[at, :] + r1_s[at, :] * (
            s
            - jnp.mean(s, axis=-1, keepdims=True)
            - hat * jnp.mean(s * hat, axis=-1, keepdims=True)
        )
        gmix[at, :] = result.astype(BF)
        return (
            sum_g + fold_rows(grad * hat),
            sum_b + fold_rows(grad),
            sum_q + fold_rows(gj[at, :D].astype(F32)),
            sum_v + fold_rows(gj[at, 2 * D :].astype(F32)),
        )

    sum_g, sum_b, sum_q, sum_v = blocks(first_back, (zero8, zero8, zero8, zero8))
    put_sum(R_G1, sum_g)
    put_sum(R_B1, sum_b)
    put_sum(R_BQ, sum_q)
    put_sum(R_BV, sum_v)
    for b in range(images):
        gin_ref[b] = gmix[b * pad : b * pad + tok, :]

    for d in range(devices):
        stage[d] = wide[d * rows : (d + 1) * rows, :].astype(BF)
    copies = []
    for k in range(devices):
        target = (send_ref if k & 1 else keep_ref).at[k >> 1]
        copies.append(pltpu.make_async_copy(stage.at[me ^ k], target, sems.at[k]))
    for c in copies:
        c.start()
    for c in copies:
        c.wait()


def run_layer(me, counts, images, cotangent, pieces, interpret=False):
    devices = len(pieces)
    rows = pieces[0].shape[0]
    count, tok, _ = images.shape
    pad = (tok + 15) // 16 * 16
    total = count * pad
    body = lambda *refs: layer_body(
        *refs, devices=devices, rows=rows, images=count, tok=tok, pad=pad
    )
    vmem = pl.BlockSpec(memory_space=pltpu.VMEM)
    smem = pl.BlockSpec(memory_space=pltpu.SMEM)
    anyspace = pl.BlockSpec(memory_space=pl.ANY)
    half = jax.ShapeDtypeStruct((devices // 2, rows, LANES), BF)
    act = jax.ShapeDtypeStruct(images.shape, BF)
    V = pltpu.VMEM
    scratch = [
        V((devices, rows, LANES), BF),
        V((devices * rows, LANES), F32),
        V((D, 3 * D), BF),
        V((D, D), BF),
        V((D, FF), BF),
        V((FF, D), BF),
        V((total, D), F32),
        V((total, D), F32),
        V((total, 1), F32),
        V((total, D), BF),
        V((total, 3 * D), BF),
        V((count * HEADS, pad, pad), F32),
        V((total, D), BF),
        V((total, D), F32),
        V((total, D), F32),
        V((total, 1), F32),
        V((total, D), BF),
        V((total, FF), BF),
        V((total, FF), BF),
        V((total, D), F32),
        V((total, D), F32),
        V((total, D), BF),
        V((total, D), BF),
        V((total, D), BF),
        V((total, 3 * D), BF),
        pltpu.SemaphoreType.DMA((devices,)),
    ]
    return pl.pallas_call(
        body,
        name="layer",
        out_shape=(act, act, half, half),
        in_specs=[smem, smem, vmem, vmem] + [anyspace] * devices,
        out_specs=(vmem, vmem, anyspace, anyspace),
        scratch_shapes=scratch,
        compiler_params=pltpu.CompilerParams(vmem_limit_bytes=48 << 20),
        interpret=interpret,
    )(me, counts, images, cotangent, *pieces)


def swap(value, mask, devices):
    return lax.ppermute(value, "dp", [(i, i ^ mask) for i in range(devices)])


def gather_pieces(own, devices):
    pieces = {0: own}
    for s in range(8, devices, 8):
        pieces[s] = swap(own, s, devices)
    outer = sorted(pieces)
    for s in outer:
        pieces[s | 2] = swap(pieces[s], 2, devices)
        pieces[s | 4] = swap(pieces[s], 4, devices)
    for i, s in enumerate(outer):
        if i % 2 == 0:
            pieces[s | 6] = swap(pieces[s | 2], 4, devices)
        else:
            pieces[s | 6] = swap(pieces[s | 4], 2, devices)
    for s in sorted(pieces):
        pieces[s | 1] = swap(pieces[s], 1, devices)
    return [pieces[k] for k in range(devices)]


def reduce_pieces(keep, send, devices):
    held = keep.astype(F32) + swap(send, 1, devices).astype(F32)
    outer = devices // 8
    rows = keep.shape[1]
    held = held.reshape(outer, 2, 2, rows, LANES).astype(BF)
    cut = outer // 2
    up, down = held[:cut], held[cut:]
    up_got = swap(up[:, :, 1], 2, devices)
    down_got = swap(down[:, 1], 4, devices)
    up = (up[:, :, 0].astype(F32) + up_got.astype(F32)).astype(BF)
    down = (down[:, 0].astype(F32) + down_got.astype(F32)).astype(BF)
    up_got = swap(up[:, 1], 4, devices)
    down_got = swap(down[:, 1], 2, devices)
    up = up[:, 0].astype(F32) + up_got.astype(F32)
    down = down[:, 0].astype(F32) + down_got.astype(F32)
    mine = [up[i] for i in range(cut)] + [down[i] for i in range(outer - cut)]
    total = mine[0]
    for s in range(1, outer):
        total = total + swap(mine[s].astype(BF), 8 * s, devices).astype(F32)
    return total


def on_device(images, params, cotangent, counts):
    devices = lax.axis_size("dp")
    own = params.reshape(-1, LANES)
    pieces = gather_pieces(own, devices)
    me = lax.axis_index("dp").astype(jnp.int32).reshape(1)
    result, image_grad, send, keep = run_layer(me, counts, images, cotangent, pieces)
    owned = reduce_pieces(keep, send, devices)
    return (result, image_grad, owned.reshape(-1))


def solution(mesh):
    placed = (P("dp", None, None), P("dp"), P("dp", None, None), P("dp"))
    return jax.shard_map(
        on_device,
        mesh=mesh,
        in_specs=placed,
        out_specs=(P("dp", None, None), P("dp", None, None), P("dp")),
        check_vma=False,
    )
```

time: 436 us -> 112 us (0.26); the launches traced: 429 us -> 112 us
  waiting for transfers between devices: 229 us -> 34.5 us
  local copies, waits for them, and re-layouts: 99.4 us -> 6.84 us
  other arithmetic: 43.9 us -> 1.59 us
  matrix products: 40.7 us -> 0 us
  starting transfers between devices: 0.08 us -> 34.6 us
  Pallas kernels: 0 us -> 33.2 us
  between operations: 16.1 us -> 1.48 us
    unnamed x3 -> x0, waiting for transfers between devices: 158 us -> none
    all_gather x1 -> x0, waiting for transfers between devices: 70.9 us -> none  [fetch_weights(): return unpack_flat(lax.all_gather(params, 'dp', axis=0, tiled=True))]
    unnamed x189 -> x9, local copies, waits for them, and re-layouts: 66.8 us -> 4.83 us
    dot_general x36 -> x0, matrix products: 40.7 us -> none  [the longest x8 12 us: left_product(): lax.dot_general(first, second, (((0,), (0,)), ((), ())), preferred_elemen...]
    ppermute x0 -> x39, starting transfers between devices: none -> 34.6 us  [swap(): return lax.ppermute(value, 'dp', [(i, i ^ mask) for i in range(devices)])]
    ppermute x0 -> x39, waiting for transfers between devices: none -> 34.5 us  [swap(): return lax.ppermute(value, 'dp', [(i, i ^ mask) for i in range(devices)])]
    pallas_call x0 -> x1, Pallas kernels: none -> 33.2 us  [run_layer(): pl.pallas_call(body, name='layer', out_shape=(act, act, half, half), in_s...]
    all_gather x1 -> x0, other arithmetic: 21 us -> none  [fetch_weights(): return unpack_flat(lax.all_gather(params, 'dp', axis=0, tiled=True))]
  transfers between devices with their start and end apart: 2 -> 39, of which waited for: 2 -> 15; matrix products, arithmetic and copies ran while one was open for 2% -> 4% of each run, Pallas kernels for 0% -> 0%
where the time goes in v1:
time: 112 us
  starting transfers between devices  34.6 us (31%)
  waiting for transfers between devices  34.5 us (31%)
  Pallas kernels  33.2 us (30%)
  local copies, waits for them, and re-layouts  6.84 us (6%)
  other arithmetic  1.59 us (1%)
  between operations  1.48 us (1%)
    ppermute x39, starting transfers between devices, swap(): return lax.ppermute(value, 'dp', [(i, i ^ mask) for i in range(devices)])  34.6 us
    ppermute x39, waiting for transfers between devices, swap(): return lax.ppermute(value, 'dp', [(i, i ^ mask) for i in range(devices)])  34.5 us
    pallas_call x1, Pallas kernels, run_layer(): pl.pallas_call(body, name='layer', out_shape=(act, act, half, half), in_s...  33.2 us
    unnamed x9, local copies, waits for them, and re-layouts  4.83 us
  transfers between devices with their start and end apart: 39, of which 15 were waited for; matrix products, arithmetic and copies ran while one was open for 4% of the time, Pallas kernels for 0%

profile of v1, /device:TPU:0, one launch (start us, length us, event | category | flops | bytes accessed | tf_op | source)
XLA Modules:
  0.0 112.3 jit_solution(14149962926320683365)
XLA Ops:
  0.6 5.1 %collective-permute-start.23 = (bf16[434,128]{1,0:T(8,128)(2,1)}, bf16[434,128]{1,0:T(8,128)(2,1)S(1)}, u32[]{:S(2)}, u32[]{:S(2)}) collective-permute-start(bf16[434,128]{1,0:T(8,128)(2,1)} %bitcast.54), channel_id=1, source_target_pairs={{0,24},{1,25},{2,26},{3,27},{4,28},{5,29},{6,30},{7,31},{8,16},{9,... | collective-permute-start | bytes 333320 | tf_op jit(solution)/shard_map/ppermute | solution.py:403
  6.4 1.7 %collective-permute-start.3 = (bf16[434,128]{1,0:T(8,128)(2,1)}, bf16[434,128]{1,0:T(8,128)(2,1)S(1)}, u32[]{:S(2)}, u32[]{:S(2)}) collective-permute-start(bf16[434,128]{1,0:T(8,128)(2,1)} %bitcast.57), channel_id=1, source_target_pairs={{0,4},{1,5},{2,6},{3,7},{4,0},{5,1},{6,2},{7,3},{8,12},{9,13},{10,... | collective-permute-start | bytes 333320 | tf_op jit(solution)/shard_map/ppermute | solution.py:403
  8.1 1.5 %collective-permute-start.1 = (bf16[434,128]{1,0:T(8,128)(2,1)}, bf16[434,128]{1,0:T(8,128)(2,1)S(1)}, u32[]{:S(2)}, u32[]{:S(2)}) collective-permute-start(bf16[434,128]{1,0:T(8,128)(2,1)} %bitcast.58), channel_id=1, source_target_pairs={{0,2},{1,3},{2,0},{3,1},{4,6},{5,7},{6,4},{7,5},{8,10},{9,11},{10,... | collective-permute-start | bytes 333320 | tf_op jit(solution)/shard_map/ppermute | solution.py:403
  10.0 5.5 %collective-permute-done.15.refs_20_ = bf16[434,128]{1,0:T(8,128)(2,1)S(1)} collective-permute-done((bf16[434,128]{1,0:T(8,128)(2,1)}, bf16[434,128]{1,0:T(8,128)(2,1)S(1)}, u32[]{:S(2)}, u32[]{:S(2)}) %collective-permute-start.15) | collective-permute-done | bytes 111136 | tf_op jit(solution)/shard_map/ppermute | solution.py:403
  15.4 1.5 %collective-permute-start.27 = (bf16[434,128]{1,0:T(8,128)(2,1)S(1)}, bf16[434,128]{1,0:T(8,128)(2,1)S(1)}, u32[]{:S(2)}, u32[]{:S(2)}) collective-permute-start(bf16[434,128]{1,0:T(8,128)(2,1)S(1)} %collective-permute-done.23.refs_28_), channel_id=1, source_target_pairs={{0,4},{1,5},{2,6},{3,7},{4,0},{5,1},{6,2},{7,3},{8,12},{9,13},{10,... | collective-permute-start | bytes 333320 | tf_op jit(solution)/shard_map/ppermute | solution.py:403
  17.0 1.5 %collective-permute-start.25 = (bf16[434,128]{1,0:T(8,128)(2,1)S(1)}, bf16[434,128]{1,0:T(8,128)(2,1)S(1)}, u32[]{:S(2)}, u32[]{:S(2)}) collective-permute-start(bf16[434,128]{1,0:T(8,128)(2,1)S(1)} %collective-permute-done.23.refs_28_), channel_id=1, source_target_pairs={{0,2},{1,3},{2,0},{3,1},{4,6},{5,7},{6,4},{7,5},{8,10},{9,11},{10,... | collective-permute-start | bytes 333320 | tf_op jit(solution)/shard_map/ppermute | solution.py:403
  20.2 1.5 %collective-permute-done.25.refs_30_ = bf16[434,128]{1,0:T(8,128)(2,1)S(1)} collective-permute-done((bf16[434,128]{1,0:T(8,128)(2,1)S(1)}, bf16[434,128]{1,0:T(8,128)(2,1)S(1)}, u32[]{:S(2)}, u32[]{:S(2)}) %collective-permute-start.25) | collective-permute-done | bytes 111136 | tf_op jit(solution)/shard_map/ppermute | solution.py:403
  22.3 1.9 %collective-permute-start.9 = (bf16[434,128]{1,0:T(8,128)(2,1)S(1)}, bf16[434,128]{1,0:T(8,128)(2,1)S(1)}, u32[]{:S(2)}, u32[]{:S(2)}) collective-permute-start(bf16[434,128]{1,0:T(8,128)(2,1)S(1)} %collective-permute-done.7.refs_12_), channel_id=1, source_target_pairs={{0,2},{1,3},{2,0},{3,1},{4,6},{5,7},{6,4},{7,5},{8,10},{9,11},{10,... | collective-permute-start | bytes 333320 | tf_op jit(solution)/shard_map/ppermute | solution.py:403
  25.0 1.7 %collective-permute-start.5 = (bf16[434,128]{1,0:T(8,128)(2,1)S(1)}, bf16[434,128]{1,0:T(8,128)(2,1)S(1)}, u32[]{:S(2)}, u32[]{:S(2)}) collective-permute-start(bf16[434,128]{1,0:T(8,128)(2,1)S(1)} %collective-permute-done.1.refs_6_), channel_id=1, source_target_pairs={{0,4},{1,5},{2,6},{3,7},{4,0},{5,1},{6,2},{7,3},{8,12},{9,13},{10,... | collective-permute-start | bytes 333320 | tf_op jit(solution)/shard_map/ppermute | solution.py:403
  27.4 1.8 %collective-permute-start.29 = (bf16[434,128]{1,0:T(8,128)(2,1)S(1)}, bf16[434,128]{1,0:T(8,128)(2,1)S(1)}, u32[]{:S(2)}, u32[]{:S(2)}) collective-permute-start(bf16[434,128]{1,0:T(8,128)(2,1)S(1)} %collective-permute-done.27.refs_32_), channel_id=1, source_target_pairs={{0,2},{1,3},{2,0},{3,1},{4,6},{5,7},{6,4},{7,5},{8,10},{9,11},{10,... | collective-permute-start | bytes 333320 | tf_op jit(solution)/shard_map/ppermute | solution.py:403
  30.1 1.7 %collective-permute-start.21 = (bf16[434,128]{1,0:T(8,128)(2,1)S(1)}, bf16[434,128]{1,0:T(8,128)(2,1)S(1)}, u32[]{:S(2)}, u32[]{:S(2)}) collective-permute-start(bf16[434,128]{1,0:T(8,128)(2,1)S(1)} %collective-permute-done.17.refs_22_), channel_id=1, source_target_pairs={{0,4},{1,5},{2,6},{3,7},{4,0},{5,1},{6,2},{7,3},{8,12},{9,13},{10,... | collective-permute-start | bytes 333320 | tf_op jit(solution)/shard_map/ppermute | solution.py:403
  31.8 1.0 collective-permute-done.29.refs_34_
  32.8 1.7 %collective-permute-start.13 = (bf16[434,128]{1,0:T(8,128)(2,1)S(1)}, bf16[434,128]{1,0:T(8,128)(2,1)S(1)}, u32[]{:S(2)}, u32[]{:S(2)}) collective-permute-start(bf16[434,128]{1,0:T(8,128)(2,1)S(1)} %collective-permute-done.11.refs_16_), channel_id=1, source_target_pairs={{0,2},{1,3},{2,0},{3,1},{4,6},{5,7},{6,4},{7,5},{8,10},{9,11},{10,... | collective-permute-start | bytes 333320 | tf_op jit(solution)/shard_map/ppermute | solution.py:403
  36.1 2.2 %collective-permute-done.13.refs_18_ = bf16[434,128]{1,0:T(8,128)(2,1)S(1)} collective-permute-done((bf16[434,128]{1,0:T(8,128)(2,1)S(1)}, bf16[434,128]{1,0:T(8,128)(2,1)S(1)}, u32[]{:S(2)}, u32[]{:S(2)}) %collective-permute-start.13) | collective-permute-done | bytes 111136 | tf_op jit(solution)/shard_map/ppermute | solution.py:403
  39.5 1.0 copy.15.refs_2_
  40.5 1.0 copy.16.refs_3_
  41.6 0.9 copy-done
  42.5 33.2 %layer.1 = (bf16[2,197,384]{2,1,0:T(8,128)(2,1)S(1)}, bf16[2,197,384]{2,1,0:T(8,128)(2,1)S(1)}, bf16[16,434,128]{2,1,0:T(8,128)(2,1)}, bf16[16,434,128]{2,1,0:T(8,128)(2,1)}) custom-call(s32[1]{0:T(128)} %bitcast.refs_0_, s32[1]{0:T(128)S(6)} %copy.35.refs_1_, bf16[2,197,384]{2,1,0:T(8,128)(2,1)S(1)} %copy.15.refs_2_, ...), custom_call_target="tpu_custom_call" | custom-call | tf_op jit(solution)/shard_map/layer/pallas_call | solution.py:390
  75.6 1.9 %copy.17 = bf16[16,434,128]{2,0,1:T(8,128)(2,1)S(1)} copy(bf16[16,434,128]{2,1,0:T(8,128)(2,1)} %get-tuple-element.10) | data formatting | bytes 3555328 | tf_op jit(solution)/shard_map/layer/pallas_call | solution.py:390
  77.6 3.7 %collective-permute-done.31 = bf16[16,434,128]{2,0,1:T(8,128)(2,1)S(1)} collective-permute-done((bf16[16,434,128]{2,0,1:T(8,128)(2,1)S(1)}, bf16[16,434,128]{2,0,1:T(8,128)(2,1)S(1)}, u32[]{:S(2)}, u32[]{:S(2)}) %collective-permute-start.31) | collective-permute-done | bytes 1777696 | tf_op jit(solution)/shard_map/ppermute | solution.py:403
  81.8 1.2 %collective-permute-start.35 = (bf16[2,2,434,128]{3,2,1,0:T(8,128)(2,1)S(1)}, bf16[2,2,434,128]{3,2,1,0:T(8,128)(2,1)S(1)}, u32[]{:S(2)}, u32[]{:S(2)}) collective-permute-start(bf16[2,2,434,128]{3,2,1,0:T(8,128)(2,1)S(1)} %slice_bitcast_fusion), channel_id=1, source_target_pairs={{0,4},{1,5},{2,6},{3,7},{4,0},{5,1},{6,2},{7,3},{8,12},{9,13},{10,... | collective-permute-start | bytes 1333256 | tf_op jit(solution)/shard_map/ppermute | solution.py:403
  83.1 1.8 %collective-permute-start.32 = (bf16[2,2,434,128]{3,2,0,1:T(8,128)(2,1)S(1)}, bf16[2,2,434,128]{3,2,0,1:T(8,128)(2,1)S(1)}, u32[]{:S(2)}, u32[]{:S(2)}) collective-permute-start(bf16[2,2,434,128]{3,2,0,1:T(8,128)(2,1)S(1)} %bitcast.64), channel_id=1, source_target_pairs={{0,2},{1,3},{2,0},{3,1},{4,6},{5,7},{6,4},{7,5},{8,10},{9,11},{10,... | collective-permute-start | bytes 1333256 | tf_op jit(solution)/shard_map/ppermute | solution.py:403
  84.9 9.3 %collective-permute-done.35 = bf16[2,2,434,128]{3,2,1,0:T(8,128)(2,1)S(1)} collective-permute-done((bf16[2,2,434,128]{3,2,1,0:T(8,128)(2,1)S(1)}, bf16[2,2,434,128]{3,2,1,0:T(8,128)(2,1)S(1)}, u32[]{:S(2)}, u32[]{:S(2)}) %collective-permute-start.35) | collective-permute-done | bytes 444448 | tf_op jit(solution)/shard_map/ppermute | solution.py:403
  94.4 1.8 %collective-permute-start.36 = (bf16[2,434,128]{2,1,0:T(8,128)(2,1)S(1)}, bf16[2,434,128]{2,1,0:T(8,128)(2,1)S(1)}, u32[]{:S(2)}, u32[]{:S(2)}) collective-permute-start(bf16[2,434,128]{2,1,0:T(8,128)(2,1)S(1)} %slice_bitcast_fusion.2), channel_id=1, source_target_pairs={{0,2},{1,3},{2,0},{3,1},{4,6},{5,7},{6,4},{7,5},{8,10},{9,11},{10,... | collective-permute-start | bytes 666632 | tf_op jit(solution)/shard_map/ppermute | solution.py:403
  96.3 1.2 %collective-permute-start.33 = (bf16[2,434,128]{2,1,0:T(8,128)(2,1)S(1)}, bf16[2,434,128]{2,1,0:T(8,128)(2,1)S(1)}, u32[]{:S(2)}, u32[]{:S(2)}) collective-permute-start(bf16[2,434,128]{2,1,0:T(8,128)(2,1)S(1)} %slice_bitcast_fusion.5), channel_id=1, source_target_pairs={{0,4},{1,5},{2,6},{3,7},{4,0},{5,1},{6,2},{7,3},{8,12},{9,13},{10,... | collective-permute-start | bytes 666632 | tf_op jit(solution)/shard_map/ppermute | solution.py:403
  97.6 3.6 %collective-permute-done.36 = bf16[2,434,128]{2,1,0:T(8,128)(2,1)S(1)} collective-permute-done((bf16[2,434,128]{2,1,0:T(8,128)(2,1)S(1)}, bf16[2,434,128]{2,1,0:T(8,128)(2,1)S(1)}, u32[]{:S(2)}, u32[]{:S(2)}) %collective-permute-start.36) | collective-permute-done | bytes 222240 | tf_op jit(solution)/shard_map/ppermute | solution.py:403
  101.8 2.1 %collective-permute-start.38 = (bf16[434,128]{1,0:T(8,128)(2,1)S(1)}, bf16[434,128]{1,0:T(8,128)(2,1)S(1)}, u32[]{:S(2)}, u32[]{:S(2)}) collective-permute-start(bf16[434,128]{1,0:T(8,128)(2,1)S(1)} %get-tuple-element.20), channel_id=1, source_target_pairs={{0,24},{1,25},{2,26},{3,27},{4,28},{5,29},{6,30},{7,31},{8,16},{9,... | collective-permute-start | bytes 333320 | tf_op jit(solution)/shard_map/ppermute | solution.py:403
  104.0 1.0 collective-permute-start.34
  105.0 0.9 copy.23
  105.9 0.9 copy.24
  106.9 3.5 %collective-permute-done.37 = bf16[434,128]{1,0:T(8,128)(2,1)S(1)} collective-permute-done((bf16[434,128]{1,0:T(8,128)(2,1)S(1)}, bf16[434,128]{1,0:T(8,128)(2,1)S(1)}, u32[]{:S(2)}, u32[]{:S(2)}) %collective-permute-start.37) | collective-permute-done | bytes 111136 | tf_op jit(solution)/shard_map/ppermute | solution.py:403
  110.4 1.1 collective-permute-done.34
  (69 shorter events, 10.2 us)
Async XLA Ops:
  0.6 9.4 %collective-permute-start.23 = (bf16[434,128]{1,0:T(8,128)(2,1)}, bf16[434,128]{1,0:T(8,128)(2,1)S(1)}, u32[]{:S(2)}, u32[]{:S(2)}) collective-permute-start(bf16[434,128]{1,0:T(8,128)(2,1)} %bitcast.54), channel_id=1, source_target_pairs={{0,24},{1,25},{2,26},{3,27},{4,28},{5,29},{6,30},{7,31},{8,16},{9,... | collective-permute-start | bytes 333320 | tf_op jit(solution)/shard_map/ppermute | solution.py:403
  5.7 9.7 %collective-permute-start.15 = (bf16[434,128]{1,0:T(8,128)(2,1)}, bf16[434,128]{1,0:T(8,128)(2,1)S(1)}, u32[]{:S(2)}, u32[]{:S(2)}) collective-permute-start(bf16[434,128]{1,0:T(8,128)(2,1)} %bitcast.55), channel_id=1, source_target_pairs={{0,16},{1,17},{2,18},{3,19},{4,20},{5,21},{6,22},{7,23},{8,24},{9,... | collective-permute-start | bytes 333320 | tf_op jit(solution)/shard_map/ppermute | solution.py:403
  5.7 11.2 %collective-permute-start.7 = (bf16[434,128]{1,0:T(8,128)(2,1)}, bf16[434,128]{1,0:T(8,128)(2,1)S(1)}, u32[]{:S(2)}, u32[]{:S(2)}) collective-permute-start(bf16[434,128]{1,0:T(8,128)(2,1)} %bitcast.56), channel_id=1, source_target_pairs={{0,8},{1,9},{2,10},{3,11},{4,12},{5,13},{6,14},{7,15},{8,0},{9,1},... | collective-permute-start | bytes 333320 | tf_op jit(solution)/shard_map/ppermute | solution.py:403
  6.4 12.1 %collective-permute-start.3 = (bf16[434,128]{1,0:T(8,128)(2,1)}, bf16[434,128]{1,0:T(8,128)(2,1)S(1)}, u32[]{:S(2)}, u32[]{:S(2)}) collective-permute-start(bf16[434,128]{1,0:T(8,128)(2,1)} %bitcast.57), channel_id=1, source_target_pairs={{0,4},{1,5},{2,6},{3,7},{4,0},{5,1},{6,2},{7,3},{8,12},{9,13},{10,... | collective-permute-start | bytes 333320 | tf_op jit(solution)/shard_map/ppermute | solution.py:403
  8.1 10.4 %collective-permute-start.1 = (bf16[434,128]{1,0:T(8,128)(2,1)}, bf16[434,128]{1,0:T(8,128)(2,1)S(1)}, u32[]{:S(2)}, u32[]{:S(2)}) collective-permute-start(bf16[434,128]{1,0:T(8,128)(2,1)} %bitcast.58), channel_id=1, source_target_pairs={{0,2},{1,3},{2,0},{3,1},{4,6},{5,7},{6,4},{7,5},{8,10},{9,11},{10,... | collective-permute-start | bytes 333320 | tf_op jit(solution)/shard_map/ppermute | solution.py:403
  10.0 9.1 %collective-permute-start = (bf16[434,128]{1,0:T(8,128)(2,1)}, bf16[434,128]{1,0:T(8,128)(2,1)S(1)}, u32[]{:S(2)}, u32[]{:S(2)}) collective-permute-start(bf16[434,128]{1,0:T(8,128)(2,1)} %bitcast.59), channel_id=1, source_target_pairs={{0,1},{1,0},{2,3},{3,2},{4,5},{5,4},{6,7},{7,6},{8,9},{9,8},{10,11... | collective-permute-start | bytes 333320 | tf_op jit(solution)/shard_map/ppermute | solution.py:403
  15.4 4.8 %collective-permute-start.27 = (bf16[434,128]{1,0:T(8,128)(2,1)S(1)}, bf16[434,128]{1,0:T(8,128)(2,1)S(1)}, u32[]{:S(2)}, u32[]{:S(2)}) collective-permute-start(bf16[434,128]{1,0:T(8,128)(2,1)S(1)} %collective-permute-done.23.refs_28_), channel_id=1, source_target_pairs={{0,4},{1,5},{2,6},{3,7},{4,0},{5,1},{6,2},{7,3},{8,12},{9,13},{10,... | collective-permute-start | bytes 333320 | tf_op jit(solution)/shard_map/ppermute | solution.py:403
  17.0 4.8 %collective-permute-start.25 = (bf16[434,128]{1,0:T(8,128)(2,1)S(1)}, bf16[434,128]{1,0:T(8,128)(2,1)S(1)}, u32[]{:S(2)}, u32[]{:S(2)}) collective-permute-start(bf16[434,128]{1,0:T(8,128)(2,1)S(1)} %collective-permute-done.23.refs_28_), channel_id=1, source_target_pairs={{0,2},{1,3},{2,0},{3,1},{4,6},{5,7},{6,4},{7,5},{8,10},{9,11},{10,... | collective-permute-start | bytes 333320 | tf_op jit(solution)/shard_map/ppermute | solution.py:403
  18.5 3.8 %collective-permute-start.24 = (bf16[434,128]{1,0:T(8,128)(2,1)S(1)}, bf16[434,128]{1,0:T(8,128)(2,1)S(1)}, u32[]{:S(2)}, u32[]{:S(2)}) collective-permute-start(bf16[434,128]{1,0:T(8,128)(2,1)S(1)} %collective-permute-done.23.refs_28_), channel_id=1, source_target_pairs={{0,1},{1,0},{2,3},{3,2},{4,5},{5,4},{6,7},{7,6},{8,9},{9,8},{10,11... | collective-permute-start | bytes 333320 | tf_op jit(solution)/shard_map/ppermute | solution.py:403
  18.5 6.0 %collective-permute-start.19 = (bf16[434,128]{1,0:T(8,128)(2,1)S(1)}, bf16[434,128]{1,0:T(8,128)(2,1)S(1)}, u32[]{:S(2)}, u32[]{:S(2)}) collective-permute-start(bf16[434,128]{1,0:T(8,128)(2,1)S(1)} %collective-permute-done.15.refs_20_), channel_id=1, source_target_pairs={{0,4},{1,5},{2,6},{3,7},{4,0},{5,1},{6,2},{7,3},{8,12},{9,13},{10,... | collective-permute-start | bytes 333320 | tf_op jit(solution)/shard_map/ppermute | solution.py:403
  19.1 5.4 %collective-permute-start.17 = (bf16[434,128]{1,0:T(8,128)(2,1)S(1)}, bf16[434,128]{1,0:T(8,128)(2,1)S(1)}, u32[]{:S(2)}, u32[]{:S(2)}) collective-permute-start(bf16[434,128]{1,0:T(8,128)(2,1)S(1)} %collective-permute-done.15.refs_20_), channel_id=1, source_target_pairs={{0,2},{1,3},{2,0},{3,1},{4,6},{5,7},{6,4},{7,5},{8,10},{9,11},{10,... | collective-permute-start | bytes 333320 | tf_op jit(solution)/shard_map/ppermute | solution.py:403
  20.2 4.7 %collective-permute-start.16 = (bf16[434,128]{1,0:T(8,128)(2,1)S(1)}, bf16[434,128]{1,0:T(8,128)(2,1)S(1)}, u32[]{:S(2)}, u32[]{:S(2)}) collective-permute-start(bf16[434,128]{1,0:T(8,128)(2,1)S(1)} %collective-permute-done.15.refs_20_), channel_id=1, source_target_pairs={{0,1},{1,0},{2,3},{3,2},{4,5},{5,4},{6,7},{7,6},{8,9},{9,8},{10,11... | collective-permute-start | bytes 333320 | tf_op jit(solution)/shard_map/ppermute | solution.py:403
  21.7 4.9 %collective-permute-start.11 = (bf16[434,128]{1,0:T(8,128)(2,1)S(1)}, bf16[434,128]{1,0:T(8,128)(2,1)S(1)}, u32[]{:S(2)}, u32[]{:S(2)}) collective-permute-start(bf16[434,128]{1,0:T(8,128)(2,1)S(1)} %collective-permute-done.7.refs_12_), channel_id=1, source_target_pairs={{0,4},{1,5},{2,6},{3,7},{4,0},{5,1},{6,2},{7,3},{8,12},{9,13},{10,... | collective-permute-start | bytes 333320 | tf_op jit(solution)/shard_map/ppermute | solution.py:403
  22.3 5.1 %collective-permute-start.9 = (bf16[434,128]{1,0:T(8,128)(2,1)S(1)}, bf16[434,128]{1,0:T(8,128)(2,1)S(1)}, u32[]{:S(2)}, u32[]{:S(2)}) collective-permute-start(bf16[434,128]{1,0:T(8,128)(2,1)S(1)} %collective-permute-done.7.refs_12_), channel_id=1, source_target_pairs={{0,2},{1,3},{2,0},{3,1},{4,6},{5,7},{6,4},{7,5},{8,10},{9,11},{10,... | collective-permute-start | bytes 333320 | tf_op jit(solution)/shard_map/ppermute | solution.py:403
  24.5 4.7 %collective-permute-start.8 = (bf16[434,128]{1,0:T(8,128)(2,1)S(1)}, bf16[434,128]{1,0:T(8,128)(2,1)S(1)}, u32[]{:S(2)}, u32[]{:S(2)}) collective-permute-start(bf16[434,128]{1,0:T(8,128)(2,1)S(1)} %collective-permute-done.7.refs_12_), channel_id=1, source_target_pairs={{0,1},{1,0},{2,3},{3,2},{4,5},{5,4},{6,7},{7,6},{8,9},{9,8},{10,11... | collective-permute-start | bytes 333320 | tf_op jit(solution)/shard_map/ppermute | solution.py:403
  24.5 4.8 %collective-permute-start.4 = (bf16[434,128]{1,0:T(8,128)(2,1)S(1)}, bf16[434,128]{1,0:T(8,128)(2,1)S(1)}, u32[]{:S(2)}, u32[]{:S(2)}) collective-permute-start(bf16[434,128]{1,0:T(8,128)(2,1)S(1)} %collective-permute-done.3.refs_8_), channel_id=1, source_target_pairs={{0,1},{1,0},{2,3},{3,2},{4,5},{5,4},{6,7},{7,6},{8,9},{9,8},{10,11... | collective-permute-start | bytes 333320 | tf_op jit(solution)/shard_map/ppermute | solution.py:403
  25.0 5.1 %collective-permute-start.5 = (bf16[434,128]{1,0:T(8,128)(2,1)S(1)}, bf16[434,128]{1,0:T(8,128)(2,1)S(1)}, u32[]{:S(2)}, u32[]{:S(2)}) collective-permute-start(bf16[434,128]{1,0:T(8,128)(2,1)S(1)} %collective-permute-done.1.refs_6_), channel_id=1, source_target_pairs={{0,4},{1,5},{2,6},{3,7},{4,0},{5,1},{6,2},{7,3},{8,12},{9,13},{10,... | collective-permute-start | bytes 333320 | tf_op jit(solution)/shard_map/ppermute | solution.py:403
  27.4 5.4 %collective-permute-start.29 = (bf16[434,128]{1,0:T(8,128)(2,1)S(1)}, bf16[434,128]{1,0:T(8,128)(2,1)S(1)}, u32[]{:S(2)}, u32[]{:S(2)}) collective-permute-start(bf16[434,128]{1,0:T(8,128)(2,1)S(1)} %collective-permute-done.27.refs_32_), channel_id=1, source_target_pairs={{0,2},{1,3},{2,0},{3,1},{4,6},{5,7},{6,4},{7,5},{8,10},{9,11},{10,... | collective-permute-start | bytes 333320 | tf_op jit(solution)/shard_map/ppermute | solution.py:403
  29.3 5.3 %collective-permute-start.26 = (bf16[434,128]{1,0:T(8,128)(2,1)S(1)}, bf16[434,128]{1,0:T(8,128)(2,1)S(1)}, u32[]{:S(2)}, u32[]{:S(2)}) collective-permute-start(bf16[434,128]{1,0:T(8,128)(2,1)S(1)} %collective-permute-done.25.refs_30_), channel_id=1, source_target_pairs={{0,1},{1,0},{2,3},{3,2},{4,5},{5,4},{6,7},{7,6},{8,9},{9,8},{10,11... | collective-permute-start | bytes 333320 | tf_op jit(solution)/shard_map/ppermute | solution.py:403
  30.0 4.7 %collective-permute-start.20 = (bf16[434,128]{1,0:T(8,128)(2,1)S(1)}, bf16[434,128]{1,0:T(8,128)(2,1)S(1)}, u32[]{:S(2)}, u32[]{:S(2)}) collective-permute-start(bf16[434,128]{1,0:T(8,128)(2,1)S(1)} %collective-permute-done.19.refs_24_), channel_id=1, source_target_pairs={{0,1},{1,0},{2,3},{3,2},{4,5},{5,4},{6,7},{7,6},{8,9},{9,8},{10,11... | collective-permute-start | bytes 333320 | tf_op jit(solution)/shard_map/ppermute | solution.py:403
  30.1 5.5 %collective-permute-start.21 = (bf16[434,128]{1,0:T(8,128)(2,1)S(1)}, bf16[434,128]{1,0:T(8,128)(2,1)S(1)}, u32[]{:S(2)}, u32[]{:S(2)}) collective-permute-start(bf16[434,128]{1,0:T(8,128)(2,1)S(1)} %collective-permute-done.17.refs_22_), channel_id=1, source_target_pairs={{0,4},{1,5},{2,6},{3,7},{4,0},{5,1},{6,2},{7,3},{8,12},{9,13},{10,... | collective-permute-start | bytes 333320 | tf_op jit(solution)/shard_map/ppermute | solution.py:403
  32.8 5.5 %collective-permute-start.13 = (bf16[434,128]{1,0:T(8,128)(2,1)S(1)}, bf16[434,128]{1,0:T(8,128)(2,1)S(1)}, u32[]{:S(2)}, u32[]{:S(2)}) collective-permute-start(bf16[434,128]{1,0:T(8,128)(2,1)S(1)} %collective-permute-done.11.refs_16_), channel_id=1, source_target_pairs={{0,2},{1,3},{2,0},{3,1},{4,6},{5,7},{6,4},{7,5},{8,10},{9,11},{10,... | collective-permute-start | bytes 333320 | tf_op jit(solution)/shard_map/ppermute | solution.py:403
  34.8 6.7 %collective-permute-start.10 = (bf16[434,128]{1,0:T(8,128)(2,1)S(1)}, bf16[434,128]{1,0:T(8,128)(2,1)S(1)}, u32[]{:S(2)}, u32[]{:S(2)}) collective-permute-start(bf16[434,128]{1,0:T(8,128)(2,1)S(1)} %collective-permute-done.9.refs_14_), channel_id=1, source_target_pairs={{0,1},{1,0},{2,3},{3,2},{4,5},{5,4},{6,7},{7,6},{8,9},{9,8},{10,11... | collective-permute-start | bytes 333320 | tf_op jit(solution)/shard_map/ppermute | solution.py:403
  35.6 5.9 %collective-permute-start.6 = (bf16[434,128]{1,0:T(8,128)(2,1)S(1)}, bf16[434,128]{1,0:T(8,128)(2,1)S(1)}, u32[]{:S(2)}, u32[]{:S(2)}) collective-permute-start(bf16[434,128]{1,0:T(8,128)(2,1)S(1)} %collective-permute-done.5.refs_10_), channel_id=1, source_target_pairs={{0,1},{1,0},{2,3},{3,2},{4,5},{5,4},{6,7},{7,6},{8,9},{9,8},{10,11... | collective-permute-start | bytes 333320 | tf_op jit(solution)/shard_map/ppermute | solution.py:403
  35.6 6.0 %collective-permute-start.30 = (bf16[434,128]{1,0:T(8,128)(2,1)S(1)}, bf16[434,128]{1,0:T(8,128)(2,1)S(1)}, u32[]{:S(2)}, u32[]{:S(2)}) collective-permute-start(bf16[434,128]{1,0:T(8,128)(2,1)S(1)} %collective-permute-done.29.refs_34_), channel_id=1, source_target_pairs={{0,1},{1,0},{2,3},{3,2},{4,5},{5,4},{6,7},{7,6},{8,9},{9,8},{10,11... | collective-permute-start | bytes 333320 | tf_op jit(solution)/shard_map/ppermute | solution.py:403
  81.8 12.5 %collective-permute-start.35 = (bf16[2,2,434,128]{3,2,1,0:T(8,128)(2,1)S(1)}, bf16[2,2,434,128]{3,2,1,0:T(8,128)(2,1)S(1)}, u32[]{:S(2)}, u32[]{:S(2)}) collective-permute-start(bf16[2,2,434,128]{3,2,1,0:T(8,128)(2,1)S(1)} %slice_bitcast_fusion), channel_id=1, source_target_pairs={{0,4},{1,5},{2,6},{3,7},{4,0},{5,1},{6,2},{7,3},{8,12},{9,13},{10,... | collective-permute-start | bytes 1333256 | tf_op jit(solution)/shard_map/ppermute | solution.py:403
  83.1 13.1 %collective-permute-start.32 = (bf16[2,2,434,128]{3,2,0,1:T(8,128)(2,1)S(1)}, bf16[2,2,434,128]{3,2,0,1:T(8,128)(2,1)S(1)}, u32[]{:S(2)}, u32[]{:S(2)}) collective-permute-start(bf16[2,2,434,128]{3,2,0,1:T(8,128)(2,1)S(1)} %bitcast.64), channel_id=1, source_target_pairs={{0,2},{1,3},{2,0},{3,1},{4,6},{5,7},{6,4},{7,5},{8,10},{9,11},{10,... | collective-permute-start | bytes 1333256 | tf_op jit(solution)/shard_map/ppermute | solution.py:403
  94.4 6.8 %collective-permute-start.36 = (bf16[2,434,128]{2,1,0:T(8,128)(2,1)S(1)}, bf16[2,434,128]{2,1,0:T(8,128)(2,1)S(1)}, u32[]{:S(2)}, u32[]{:S(2)}) collective-permute-start(bf16[2,434,128]{2,1,0:T(8,128)(2,1)S(1)} %slice_bitcast_fusion.2), channel_id=1, source_target_pairs={{0,2},{1,3},{2,0},{3,1},{4,6},{5,7},{6,4},{7,5},{8,10},{9,11},{10,... | collective-permute-start | bytes 666632 | tf_op jit(solution)/shard_map/ppermute | solution.py:403
  96.3 7.6 %collective-permute-start.33 = (bf16[2,434,128]{2,1,0:T(8,128)(2,1)S(1)}, bf16[2,434,128]{2,1,0:T(8,128)(2,1)S(1)}, u32[]{:S(2)}, u32[]{:S(2)}) collective-permute-start(bf16[2,434,128]{2,1,0:T(8,128)(2,1)S(1)} %slice_bitcast_fusion.5), channel_id=1, source_target_pairs={{0,4},{1,5},{2,6},{3,7},{4,0},{5,1},{6,2},{7,3},{8,12},{9,13},{10,... | collective-permute-start | bytes 666632 | tf_op jit(solution)/shard_map/ppermute | solution.py:403
  101.3 9.1 %collective-permute-start.37 = (bf16[434,128]{1,0:T(8,128)(2,1)S(1)}, bf16[434,128]{1,0:T(8,128)(2,1)S(1)}, u32[]{:S(2)}, u32[]{:S(2)}) collective-permute-start(bf16[434,128]{1,0:T(8,128)(2,1)S(1)} %get-tuple-element.19), channel_id=1, source_target_pairs={{0,16},{1,17},{2,18},{3,19},{4,20},{5,21},{6,22},{7,23},{8,24},{9,... | collective-permute-start | bytes 333320 | tf_op jit(solution)/shard_map/ppermute | solution.py:403
  101.8 8.6 %collective-permute-start.38 = (bf16[434,128]{1,0:T(8,128)(2,1)S(1)}, bf16[434,128]{1,0:T(8,128)(2,1)S(1)}, u32[]{:S(2)}, u32[]{:S(2)}) collective-permute-start(bf16[434,128]{1,0:T(8,128)(2,1)S(1)} %get-tuple-element.20), channel_id=1, source_target_pairs={{0,24},{1,25},{2,26},{3,27},{4,28},{5,29},{6,30},{7,31},{8,16},{9,... | collective-permute-start | bytes 333320 | tf_op jit(solution)/shard_map/ppermute | solution.py:403
  104.0 7.5 %collective-permute-start.34 = (bf16[434,128]{1,0:T(8,128)(2,1)S(1)}, bf16[434,128]{1,0:T(8,128)(2,1)S(1)}, u32[]{:S(2)}, u32[]{:S(2)}) collective-permute-start(bf16[434,128]{1,0:T(8,128)(2,1)S(1)} %fusion.7), channel_id=1, source_target_pairs={{0,8},{1,9},{2,10},{3,11},{4,12},{5,13},{6,14},{7,15},{8,0},{9,1},... | collective-permute-start | bytes 333320 | tf_op jit(solution)/shard_map/ppermute | solution.py:403
  (9 other events, 30.3 us)

commit v2 on v1

--- a/solution.py
+++ b/solution.py
@@ -56,6 +56,17 @@
     return jnp.sum(value.reshape(-1, 8, value.shape[-1]), axis=0)
 
 
+def low_bits(me, c, b2, b1):
+    first = 2 + 2 * ((me & 1) ^ c)
+    return (me & 7) ^ c ^ (b1 * first) ^ (b2 * (6 - first))
+
+
+def group_keys(devices):
+    outer = devices // 8
+    near, far = tuple(range(outer // 2)), tuple(range(outer // 2, outer))
+    return [(c, b2, shifts) for shifts in (near, far) for c in range(2) for b2 in range(2)]
+
+
 def layer_body(
     me_ref,
     count_ref,
@@ -68,8 +79,11 @@
     tok,
     pad,
 ):
-    pieces = refs[:devices]
-    (out_ref, gin_ref, send_ref, keep_ref) = refs[devices : devices + 4]
+    order = group_keys(devices)
+    groups = refs[: len(order)]
+    refs = refs[len(order) :]
+    out_ref, gin_ref = refs[:2]
+    shares = refs[2 : 2 + len(order)]
     (
         stage,
         wide,
@@ -97,17 +111,19 @@
         gmix,
         gj,
         sems,
-    ) = refs[devices + 4 :]
+    ) = refs[2 + len(order) :]
     me = me_ref[0]
     total = images * pad
     scale = float(D // HEADS) ** (-0.5)
     blk = 32
     steps = total // blk
-    copies = [
-        pltpu.make_async_copy(pieces[k], stage.at[me ^ k], sems.at[k]) for k in range(devices)
-    ]
-    for c in copies:
-        c.start()
+    plane = me >> 3
+
+    def slots(refs):
+        for ref, (c, b2, shifts) in zip(refs, order):
+            for i in range(2 * len(shifts)):
+                b1, s = divmod(i, len(shifts))
+                yield ref.at[i], ((plane ^ shifts[s]) << 3) | low_bits(me, c, b2, b1)
 
     for b in range(images):
         live = (count_ref[0] > b).astype(F32)
@@ -119,10 +135,8 @@
             [cot_ref[b].astype(F32) * live, zeros], axis=0
         ).astype(BF)
 
-    for c in copies:
-        c.wait()
-    for d in range(devices):
-        wide[d * rows : (d + 1) * rows, :] = stage[d].astype(F32)
+    for ref, owner in slots(groups):
+        wide[pl.ds(owner * rows, rows), :] = ref[...].astype(F32)
 
     def unpack(dst, start, height, width):
         per = width // LANES
@@ -149,7 +163,7 @@
         def step(i, carry):
             return body(pl.ds(pl.multiple_of(i * blk, blk), blk), carry)
 
-        return lax.fori_loop(0, steps, step, init)
+        return lax.fori_loop(0, steps, step, init, unroll=True)
 
     def standardize(v):
         centre = v - jnp.mean(v, axis=-1, keepdims=True)
@@ -334,19 +348,18 @@
 
     for d in range(devices):
         stage[d] = wide[d * rows : (d + 1) * rows, :].astype(BF)
-    copies = []
-    for k in range(devices):
-        target = (send_ref if k & 1 else keep_ref).at[k >> 1]
-        copies.append(pltpu.make_async_copy(stage.at[me ^ k], target, sems.at[k]))
+    copies = [
+        pltpu.make_async_copy(stage.at[owner], ref, sems.at[k])
+        for k, (ref, owner) in enumerate(slots(shares))
+    ]
     for c in copies:
         c.start()
     for c in copies:
         c.wait()
 
 
-def run_layer(me, counts, images, cotangent, pieces, interpret=False):
-    devices = len(pieces)
-    rows = pieces[0].shape[0]
+def run_layer(me, counts, images, cotangent, groups, devices, interpret=False):
+    rows = groups[0].shape[1]
     count, tok, _ = images.shape
     pad = (tok + 15) // 16 * 16
     total = count * pad
@@ -356,7 +369,7 @@
     vmem = pl.BlockSpec(memory_space=pltpu.VMEM)
     smem = pl.BlockSpec(memory_space=pltpu.SMEM)
     anyspace = pl.BlockSpec(memory_space=pl.ANY)
-    half = jax.ShapeDtypeStruct((devices // 2, rows, LANES), BF)
+    parts = tuple(jax.ShapeDtypeStruct(g.shape, BF) for g in groups)
     act = jax.ShapeDtypeStruct(images.shape, BF)
     V = pltpu.VMEM
     scratch = [
@@ -390,66 +403,114 @@
     return pl.pallas_call(
         body,
         name="layer",
-        out_shape=(act, act, half, half),
-        in_specs=[smem, smem, vmem, vmem] + [anyspace] * devices,
-        out_specs=(vmem, vmem, anyspace, anyspace),
+        out_shape=(act, act) + parts,
+        in_specs=[smem, smem, vmem, vmem] + [vmem] * len(groups),
+        out_specs=(vmem, vmem) + (anyspace,) * len(groups),
         scratch_shapes=scratch,
         compiler_params=pltpu.CompilerParams(vmem_limit_bytes=48 << 20),
         interpret=interpret,
-    )(me, counts, images, cotangent, *pieces)
-
-
-def swap(value, mask, devices):
-    return lax.ppermute(value, "dp", [(i, i ^ mask) for i in range(devices)])
-
-
-def gather_pieces(own, devices):
-    pieces = {0: own}
-    for s in range(8, devices, 8):
-        pieces[s] = swap(own, s, devices)
-    outer = sorted(pieces)
-    for s in outer:
-        pieces[s | 2] = swap(pieces[s], 2, devices)
-        pieces[s | 4] = swap(pieces[s], 4, devices)
-    for i, s in enumerate(outer):
-        if i % 2 == 0:
-            pieces[s | 6] = swap(pieces[s | 2], 4, devices)
-        else:
-            pieces[s | 6] = swap(pieces[s | 4], 2, devices)
-    for s in sorted(pieces):
-        pieces[s | 1] = swap(pieces[s], 1, devices)
-    return [pieces[k] for k in range(devices)]
-
-
-def reduce_pieces(keep, send, devices):
-    held = keep.astype(F32) + swap(send, 1, devices).astype(F32)
-    outer = devices // 8
-    rows = keep.shape[1]
-    held = held.reshape(outer, 2, 2, rows, LANES).astype(BF)
-    cut = outer // 2
-    up, down = held[:cut], held[cut:]
-    up_got = swap(up[:, :, 1], 2, devices)
-    down_got = swap(down[:, 1], 4, devices)
-    up = (up[:, :, 0].astype(F32) + up_got.astype(F32)).astype(BF)
-    down = (down[:, 0].astype(F32) + down_got.astype(F32)).astype(BF)
-    up_got = swap(up[:, 1], 4, devices)
-    down_got = swap(down[:, 1], 2, devices)
-    up = up[:, 0].astype(F32) + up_got.astype(F32)
-    down = down[:, 0].astype(F32) + down_got.astype(F32)
-    mine = [up[i] for i in range(cut)] + [down[i] for i in range(outer - cut)]
-    total = mine[0]
-    for s in range(1, outer):
-        total = total + swap(mine[s].astype(BF), 8 * s, devices).astype(F32)
+    )(me, counts, images, cotangent, *groups)
+
+
+def permute(value, devices, partner):
+    return lax.ppermute(value, "dp", [(i, partner(i)) for i in range(devices)])
+
+
+def over_planes(value, devices, shift):
+    return permute(value, devices, lambda i: i ^ (8 * shift))
+
+
+def over_core(value, devices):
+    return permute(value, devices, lambda i: i ^ 1)
+
+
+def over_first(value, devices):
+    return permute(value, devices, lambda i: i ^ (4 if i & 1 else 2))
+
+
+def over_second(value, devices):
+    return permute(value, devices, lambda i: i ^ (2 if i & 1 else 4))
+
+
+def fence(*values):
+    return lax.optimization_barrier(values)
+
+
+def gather_groups(own, n):
+    outer = n // 8
+    half = outer // 2
+    got = {0: own, half: over_planes(own, n, half)}
+    if half > 1:
+        got[half // 2] = over_planes(own, n, half // 2)
+        names = sorted(got)
+        got = dict(zip(names, fence(*[got[s] for s in names])))
+    bit = half // 2
+    while bit:
+        for s in sorted(got):
+            if s ^ bit not in got:
+                got[s ^ bit] = over_planes(got[s], n, bit)
+        bit //= 2
+    got = [got[s] for s in range(outer)]
+    a = jnp.stack(got[: outer // 2])
+    a1 = over_first(a, n)
+    an = jnp.concatenate([a, a1], axis=0)
+    af = over_second(an, n)
+    *rest, an = fence(*got[outer // 2 :], an)
+    b = jnp.stack(rest)
+    b1 = over_first(b, n)
+    bn = jnp.concatenate([b, b1], axis=0)
+    bf = over_second(bn, n)
+    return [an, af, over_core(an, n), over_core(af, n), bn, bf, over_core(bn, n), over_core(bf, n)]
+
+
+def reduce_groups(parts, n):
+    near, far = parts[:4], parts[4:]
+
+    def add(held, got):
+        return held.astype(F32) + got.astype(F32)
+
+    fc = [over_core(far[2], n), over_core(far[3], n)]
+    nc = [over_core(near[2], n), over_core(near[3], n)]
+
+    def second_step(keep, got):
+        return add(keep[0], got[0]), over_second(add(keep[1], got[1]).astype(BF), n)
+
+    def first_step(held, got):
+        total = add(held, got)
+        cut = total.shape[0] // 2
+        return total[:cut], over_first(total[cut:].astype(BF), n)
+
+    outer = n // 8
+    f1 = second_step(far, fc)
+    n1 = second_step(near, nc)
+    f2 = first_step(*f1)
+    n2 = first_step(*n1)
+    f3 = add(*f2)
+    far = [f3[s] for s in range(outer - outer // 2)]
+    bit = outer // 4
+    while bit:
+        far = [far[s] + over_planes(far[s + bit].astype(BF), n, bit).astype(F32) for s in range(bit)]
+        bit //= 2
+    last = over_planes(far[0].astype(BF), n, outer // 2)
+    n3 = add(*n2)
+    near = [n3[s] for s in range(outer // 2)]
+    bit = outer // 4
+    while bit:
+        near = [
+            near[s] + over_planes(near[s + bit].astype(BF), n, bit).astype(F32) for s in range(bit)
+        ]
+        bit //= 2
+    total = near[0] + last.astype(F32)
     return total
 
 
 def on_device(images, params, cotangent, counts):
     devices = lax.axis_size("dp")
     own = params.reshape(-1, LANES)
-    pieces = gather_pieces(own, devices)
+    groups = gather_groups(own, devices)
     me = lax.axis_index("dp").astype(jnp.int32).reshape(1)
-    result, image_grad, send, keep = run_layer(me, counts, images, cotangent, pieces)
-    owned = reduce_pieces(keep, send, devices)
+    result, image_grad, *parts = run_layer(me, counts, images, cotangent, groups, devices)
+    owned = reduce_groups(parts, devices)
     return (result, image_grad, owned.reshape(-1))
 
 

time: 112 us -> 95.8 us (0.86)
  starting transfers between devices: 34.6 us -> 25.6 us
  Pallas kernels: 33.2 us -> 24.4 us
  waiting for transfers between devices: 34.5 us -> 37.9 us
  local copies, waits for them, and re-layouts: 6.84 us -> 3.7 us
    ppermute x39 -> x22, starting transfers between devices: 34.6 us -> 25.6 us  [permute(): return lax.ppermute(value, 'dp', [(i, partner(i)) for i in range(devices)])]
    pallas_call x1, Pallas kernels: 33.2 us -> 24.4 us  [run_layer(): pl.pallas_call(body, name='layer', out_shape=(act, act) + parts, in_specs...]
    ppermute x39 -> x22, waiting for transfers between devices: 34.5 us -> 37.9 us  [permute(): return lax.ppermute(value, 'dp', [(i, partner(i)) for i in range(devices)])]
    pallas_call x1 -> x0, local copies, waits for them, and re-layouts: 1.85 us -> none  [run_layer(): pl.pallas_call(body, name='layer', out_shape=(act, act, half, half), in_s...]
    unnamed x9 -> x18, local copies, waits for them, and re-layouts: 4.83 us -> 3.6 us
  transfers between devices with their start and end apart: 39 -> 22, of which waited for: 15 -> 12; matrix products, arithmetic and copies ran while one was open for 4% -> 3% of each run, Pallas kernels for 0% -> 0%
where the time goes in v2:
time: 95.8 us; the launch traced here: 95.6 us
  waiting for transfers between devices  37.9 us (40%)
  starting transfers between devices  25.6 us (27%)
  Pallas kernels  24.4 us (25%)
  local copies, waits for them, and re-layouts  3.7 us (4%)
  other arithmetic  2.55 us (3%)
  between operations  1.48 us (2%)
    ppermute x22, waiting for transfers between devices, permute(): return lax.ppermute(value, 'dp', [(i, partner(i)) for i in range(devices)])  37.9 us
    ppermute x22, starting transfers between devices, permute(): return lax.ppermute(value, 'dp', [(i, partner(i)) for i in range(devices)])  25.6 us
    pallas_call x1, Pallas kernels, run_layer(): pl.pallas_call(body, name='layer', out_shape=(act, act) + parts, in_specs...  24.4 us
    unnamed x18, local copies, waits for them, and re-layouts  3.6 us
  transfers between devices with their start and end apart: 22, of which 12 were waited for; matrix products, arithmetic and copies ran while one was open for 3% of the time, Pallas kernels for 0%

profile of v2, /device:TPU:0, one launch (start us, length us, event | category | flops | bytes accessed | tf_op | source)
XLA Modules:
  0.0 95.6 jit_solution(16055907417804590034)
XLA Ops:
  0.6 4.1 %collective-permute-start.1 = (bf16[434,128]{1,0:T(8,128)(2,1)}, bf16[434,128]{1,0:T(8,128)(2,1)S(1)}, u32[]{:S(2)}, u32[]{:S(2)}) collective-permute-start(bf16[434,128]{1,0:T(8,128)(2,1)} %bitcast.26), channel_id=1, source_target_pairs={{0,16},{1,17},{2,18},{3,19},{4,20},{5,21},{6,22},{7,23},{8,24},{9,... | collective-permute-start | bytes 333320 | tf_op jit(solution)/shard_map/ppermute | solution.py:416
  4.7 1.6 %collective-permute-start = (bf16[434,128]{1,0:T(8,128)(2,1)}, bf16[434,128]{1,0:T(8,128)(2,1)S(1)}, u32[]{:S(2)}, u32[]{:S(2)}) collective-permute-start(bf16[434,128]{1,0:T(8,128)(2,1)} %bitcast.27), channel_id=1, source_target_pairs={{0,8},{1,9},{2,10},{3,11},{4,12},{5,13},{6,14},{7,15},{8,0},{9,1},... | collective-permute-start | bytes 333320 | tf_op jit(solution)/shard_map/ppermute | solution.py:416
  6.3 4.3 %collective-permute-done.1 = bf16[434,128]{1,0:T(8,128)(2,1)S(1)} collective-permute-done((bf16[434,128]{1,0:T(8,128)(2,1)}, bf16[434,128]{1,0:T(8,128)(2,1)S(1)}, u32[]{:S(2)}, u32[]{:S(2)}) %collective-permute-start.1) | collective-permute-done | bytes 111136 | tf_op jit(solution)/shard_map/ppermute | solution.py:416
  10.8 1.0 %pad_maximum_fusion.2 = bf16[2,434,128]{2,1,0:T(8,128)(2,1)S(1)} fusion(bf16[1,434,128]{2,1,0:T(8,128)(2,1)S(1)} %bitcast.34, bf16[1,434,128]{2,1,0:T(8,128)(2,1)} %bitcast.28), kind=kLoop, calls=%fused_computation.19 | loop fusion | flops 111104 | bytes 444416 | tf_op jit(solution)/shard_map/stack | solution.py:454
  11.8 1.6 %collective-permute-start.3 = (bf16[2,434,128]{2,1,0:T(8,128)(2,1)S(1)}, bf16[2,434,128]{2,1,0:T(8,128)(2,1)S(1)}, u32[]{:S(2)}, u32[]{:S(2)}) collective-permute-start(bf16[2,434,128]{2,1,0:T(8,128)(2,1)S(1)} %pad_maximum_fusion.2), channel_id=1, source_target_pairs={{0,2},{1,5},{2,0},{3,7},{4,6},{5,1},{6,4},{7,3},{8,10},{9,13},{10,... | collective-permute-start | bytes 666632 | tf_op jit(solution)/shard_map/ppermute | solution.py:416
  13.4 1.4 %collective-permute-start.2 = (bf16[434,128]{1,0:T(8,128)(2,1)S(1)}, bf16[434,128]{1,0:T(8,128)(2,1)S(1)}, u32[]{:S(2)}, u32[]{:S(2)}) collective-permute-start(bf16[434,128]{1,0:T(8,128)(2,1)S(1)} %collective-permute-done.1), channel_id=1, source_target_pairs={{0,8},{1,9},{2,10},{3,11},{4,12},{5,13},{6,14},{7,15},{8,0},{9,1},... | collective-permute-start | bytes 333320 | tf_op jit(solution)/shard_map/ppermute | solution.py:416
  14.8 3.1 %collective-permute-done.3 = bf16[2,434,128]{2,1,0:T(8,128)(2,1)S(1)} collective-permute-done((bf16[2,434,128]{2,1,0:T(8,128)(2,1)S(1)}, bf16[2,434,128]{2,1,0:T(8,128)(2,1)S(1)}, u32[]{:S(2)}, u32[]{:S(2)}) %collective-permute-start.3) | collective-permute-done | bytes 222240 | tf_op jit(solution)/shard_map/ppermute | solution.py:416
  18.2 1.3 %collective-permute-start.7 = (bf16[2,434,128]{2,1,0:T(8,128)(2,1)S(1)}, bf16[2,434,128]{2,1,0:T(8,128)(2,1)S(1)}, u32[]{:S(2)}, u32[]{:S(2)}) collective-permute-start(bf16[2,434,128]{2,1,0:T(8,128)(2,1)S(1)} %pad_maximum_fusion.3), channel_id=1, source_target_pairs={{0,2},{1,5},{2,0},{3,7},{4,6},{5,1},{6,4},{7,3},{8,10},{9,13},{10,... | collective-permute-start | bytes 666632 | tf_op jit(solution)/shard_map/ppermute | solution.py:416
  19.5 1.5 %collective-permute-start.4 = (bf16[4,434,128]{2,1,0:T(8,128)(2,1)S(1)}, bf16[4,434,128]{2,1,0:T(8,128)(2,1)S(1)}, u32[]{:S(2)}, u32[]{:S(2)}) collective-permute-start(bf16[4,434,128]{2,1,0:T(8,128)(2,1)S(1)} %pad_maximum_fusion.refs_4_), channel_id=1, source_target_pairs={{0,4},{1,3},{2,6},{3,1},{4,0},{5,7},{6,2},{7,5},{8,12},{9,11},{10,... | collective-permute-start | bytes 1333256 | tf_op jit(solution)/shard_map/ppermute | solution.py:416
  21.1 5.7 %collective-permute-done.7 = bf16[2,434,128]{2,1,0:T(8,128)(2,1)S(1)} collective-permute-done((bf16[2,434,128]{2,1,0:T(8,128)(2,1)S(1)}, bf16[2,434,128]{2,1,0:T(8,128)(2,1)S(1)}, u32[]{:S(2)}, u32[]{:S(2)}) %collective-permute-start.7) | collective-permute-done | bytes 222240 | tf_op jit(solution)/shard_map/ppermute | solution.py:416
  26.8 1.6 %collective-permute-start.8 = (bf16[4,434,128]{2,1,0:T(8,128)(2,1)S(1)}, bf16[4,434,128]{2,1,0:T(8,128)(2,1)S(1)}, u32[]{:S(2)}, u32[]{:S(2)}) collective-permute-start(bf16[4,434,128]{2,1,0:T(8,128)(2,1)S(1)} %pad_maximum_fusion.1.refs_8_), channel_id=1, source_target_pairs={{0,4},{1,3},{2,6},{3,1},{4,0},{5,7},{6,2},{7,5},{8,12},{9,11},{10,... | collective-permute-start | bytes 1333256 | tf_op jit(solution)/shard_map/ppermute | solution.py:416
  28.4 0.5 collective-permute-start.9
  28.9 6.4 %collective-permute-done.8.refs_9_ = bf16[4,434,128]{2,1,0:T(8,128)(2,1)S(1)} collective-permute-done((bf16[4,434,128]{2,1,0:T(8,128)(2,1)S(1)}, bf16[4,434,128]{2,1,0:T(8,128)(2,1)S(1)}, u32[]{:S(2)}, u32[]{:S(2)}) %collective-permute-start.8) | collective-permute-done | bytes 444448 | tf_op jit(solution)/shard_map/ppermute | solution.py:416
  36.0 0.9 copy-done.6
  37.2 0.6 copy-done.2
  37.9 24.4 %layer.1 = (bf16[2,197,384]{2,1,0:T(8,128)(2,1)S(1)}, bf16[2,197,384]{2,1,0:T(8,128)(2,1)S(1)}, bf16[4,434,128]{2,1,0:T(8,128)(2,1)S(1)}, bf16[4,434,128]{2,1,0:...) custom-call(s32[1]{0:T(128)} %bitcast.refs_0_, ...), custom_call_target="tpu_custom_call" | custom-call | tf_op jit(solution)/shard_map/layer/pallas_call | solution.py:403
  62.3 0.6 collective-permute-start.17
  63.4 0.9 collective-permute-done.17
  64.5 1.6 %collective-permute-start.18 = (bf16[4,434,128]{2,1,0:T(8,128)(2,1)S(1)}, bf16[4,434,128]{2,1,0:T(8,128)(2,1)S(1)}, u32[]{:S(2)}, u32[]{:S(2)}) collective-permute-start(bf16[4,434,128]{2,1,0:T(8,128)(2,1)S(1)} %add_convert_fusion), channel_id=1, source_target_pairs={{0,4},{1,3},{2,6},{3,1},{4,0},{5,7},{6,2},{7,5},{8,12},{9,11},{10,... | collective-permute-start | bytes 1333256 | tf_op jit(solution)/shard_map/ppermute | solution.py:416
  66.2 1.4 %collective-permute-start.13 = (bf16[4,434,128]{2,1,0:T(8,128)(2,1)S(1)}, bf16[4,434,128]{2,1,0:T(8,128)(2,1)S(1)}, u32[]{:S(2)}, u32[]{:S(2)}) collective-permute-start(bf16[4,434,128]{2,1,0:T(8,128)(2,1)S(1)} %add_convert_fusion.1), channel_id=1, source_target_pairs={{0,4},{1,3},{2,6},{3,1},{4,0},{5,7},{6,2},{7,5},{8,12},{9,11},{10,... | collective-permute-start | bytes 1333256 | tf_op jit(solution)/shard_map/ppermute | solution.py:416
  67.6 5.3 %collective-permute-done.18 = bf16[4,434,128]{2,1,0:T(8,128)(2,1)S(1)} collective-permute-done((bf16[4,434,128]{2,1,0:T(8,128)(2,1)S(1)}, bf16[4,434,128]{2,1,0:T(8,128)(2,1)S(1)}, u32[]{:S(2)}, u32[]{:S(2)}) %collective-permute-start.18) | collective-permute-done | bytes 444448 | tf_op jit(solution)/shard_map/ppermute | solution.py:416
  73.1 1.3 %collective-permute-start.19 = (bf16[2,434,128]{2,1,0:T(8,128)(2,1)S(1)}, bf16[2,434,128]{2,1,0:T(8,128)(2,1)S(1)}, u32[]{:S(2)}, u32[]{:S(2)}) collective-permute-start(bf16[2,434,128]{2,1,0:T(8,128)(2,1)S(1)} %slice.66), channel_id=1, source_target_pairs={{0,2},{1,5},{2,0},{3,7},{4,6},{5,1},{6,4},{7,3},{8,10},{9,13},{10,... | collective-permute-start | bytes 666632 | tf_op jit(solution)/shard_map/ppermute | solution.py:416
  74.5 5.7 %collective-permute-done.13 = bf16[4,434,128]{2,1,0:T(8,128)(2,1)S(1)} collective-permute-done((bf16[4,434,128]{2,1,0:T(8,128)(2,1)S(1)}, bf16[4,434,128]{2,1,0:T(8,128)(2,1)S(1)}, u32[]{:S(2)}, u32[]{:S(2)}) %collective-permute-start.13) | collective-permute-done | bytes 444448 | tf_op jit(solution)/shard_map/ppermute | solution.py:416
  80.4 1.3 %collective-permute-start.14 = (bf16[2,434,128]{2,1,0:T(8,128)(2,1)S(1)}, bf16[2,434,128]{2,1,0:T(8,128)(2,1)S(1)}, u32[]{:S(2)}, u32[]{:S(2)}) collective-permute-start(bf16[2,434,128]{2,1,0:T(8,128)(2,1)S(1)} %slice.67), channel_id=1, source_target_pairs={{0,2},{1,5},{2,0},{3,7},{4,6},{5,1},{6,4},{7,3},{8,10},{9,13},{10,... | collective-permute-start | bytes 666632 | tf_op jit(solution)/shard_map/ppermute | solution.py:416
  81.8 1.4 %collective-permute-start.20 = (bf16[434,128]{1,0:T(8,128)(2,1)S(1)}, bf16[434,128]{1,0:T(8,128)(2,1)S(1)}, u32[]{:S(2)}, u32[]{:S(2)}) collective-permute-start(bf16[434,128]{1,0:T(8,128)(2,1)S(1)} %fusion.6), channel_id=1, source_target_pairs={{0,8},{1,9},{2,10},{3,11},{4,12},{5,13},{6,14},{7,15},{8,0},{9,1},... | collective-permute-start | bytes 333320 | tf_op jit(solution)/shard_map/ppermute | solution.py:416
  83.2 3.2 %collective-permute-done.14 = bf16[2,434,128]{2,1,0:T(8,128)(2,1)S(1)} collective-permute-done((bf16[2,434,128]{2,1,0:T(8,128)(2,1)S(1)}, bf16[2,434,128]{2,1,0:T(8,128)(2,1)S(1)}, u32[]{:S(2)}, u32[]{:S(2)}) %collective-permute-start.14) | collective-permute-done | bytes 222240 | tf_op jit(solution)/shard_map/ppermute | solution.py:416
  86.5 1.4 %collective-permute-start.15 = (bf16[434,128]{1,0:T(8,128)(2,1)S(1)}, bf16[434,128]{1,0:T(8,128)(2,1)S(1)}, u32[]{:S(2)}, u32[]{:S(2)}) collective-permute-start(bf16[434,128]{1,0:T(8,128)(2,1)S(1)} %fusion.5), channel_id=1, source_target_pairs={{0,8},{1,9},{2,10},{3,11},{4,12},{5,13},{6,14},{7,15},{8,0},{9,1},... | collective-permute-start | bytes 333320 | tf_op jit(solution)/shard_map/ppermute | solution.py:416
  87.9 2.3 %collective-permute-start.21 = (bf16[434,128]{1,0:T(8,128)(2,1)S(1)}, bf16[434,128]{1,0:T(8,128)(2,1)S(1)}, u32[]{:S(2)}, u32[]{:S(2)}) collective-permute-start(bf16[434,128]{1,0:T(8,128)(2,1)S(1)} %fusion.1), channel_id=1, source_target_pairs={{0,16},{1,17},{2,18},{3,19},{4,20},{5,21},{6,22},{7,23},{8,24},{9,... | collective-permute-start | bytes 333320 | tf_op jit(solution)/shard_map/ppermute | solution.py:416
  90.3 0.9 copy.9
  91.2 0.9 copy.10
  92.2 2.7 %collective-permute-done.21 = bf16[434,128]{1,0:T(8,128)(2,1)S(1)} collective-permute-done((bf16[434,128]{1,0:T(8,128)(2,1)S(1)}, bf16[434,128]{1,0:T(8,128)(2,1)S(1)}, u32[]{:S(2)}, u32[]{:S(2)}) %collective-permute-start.21) | collective-permute-done | bytes 111136 | tf_op jit(solution)/shard_map/ppermute | solution.py:416
  94.9 0.7 fusion.4
  (47 shorter events, 2.4 us)
Async XLA Ops:
  0.6 9.9 %collective-permute-start.1 = (bf16[434,128]{1,0:T(8,128)(2,1)}, bf16[434,128]{1,0:T(8,128)(2,1)S(1)}, u32[]{:S(2)}, u32[]{:S(2)}) collective-permute-start(bf16[434,128]{1,0:T(8,128)(2,1)} %bitcast.26), channel_id=1, source_target_pairs={{0,16},{1,17},{2,18},{3,19},{4,20},{5,21},{6,22},{7,23},{8,24},{9,... | collective-permute-start | bytes 333320 | tf_op jit(solution)/shard_map/ppermute | solution.py:416
  4.7 6.1 %collective-permute-start = (bf16[434,128]{1,0:T(8,128)(2,1)}, bf16[434,128]{1,0:T(8,128)(2,1)S(1)}, u32[]{:S(2)}, u32[]{:S(2)}) collective-permute-start(bf16[434,128]{1,0:T(8,128)(2,1)} %bitcast.27), channel_id=1, source_target_pairs={{0,8},{1,9},{2,10},{3,11},{4,12},{5,13},{6,14},{7,15},{8,0},{9,1},... | collective-permute-start | bytes 333320 | tf_op jit(solution)/shard_map/ppermute | solution.py:416
  10.8 7.0 %copy-start.4 = (bf16[55552]{0:T(1024)(128)(2,1)S(1)}, bf16[55552]{0:T(1024)(128)(2,1)}, u32[]{:S(2)}) copy-start(bf16[55552]{0:T(1024)(128)(2,1)} %param.5) | copy-start | bytes 333316
  11.8 6.0 %collective-permute-start.3 = (bf16[2,434,128]{2,1,0:T(8,128)(2,1)S(1)}, bf16[2,434,128]{2,1,0:T(8,128)(2,1)S(1)}, u32[]{:S(2)}, u32[]{:S(2)}) collective-permute-start(bf16[2,434,128]{2,1,0:T(8,128)(2,1)S(1)} %pad_maximum_fusion.2), channel_id=1, source_target_pairs={{0,2},{1,5},{2,0},{3,7},{4,6},{5,1},{6,4},{7,3},{8,10},{9,13},{10,... | collective-permute-start | bytes 666632 | tf_op jit(solution)/shard_map/ppermute | solution.py:416
  13.4 4.8 %collective-permute-start.2 = (bf16[434,128]{1,0:T(8,128)(2,1)S(1)}, bf16[434,128]{1,0:T(8,128)(2,1)S(1)}, u32[]{:S(2)}, u32[]{:S(2)}) collective-permute-start(bf16[434,128]{1,0:T(8,128)(2,1)S(1)} %collective-permute-done.1), channel_id=1, source_target_pairs={{0,8},{1,9},{2,10},{3,11},{4,12},{5,13},{6,14},{7,15},{8,0},{9,1},... | collective-permute-start | bytes 333320 | tf_op jit(solution)/shard_map/ppermute | solution.py:416
  18.2 17.7 %copy-start.5 = (bf16[2,197,384]{2,0,1:T(2,128)(2,1)S(1)}, bf16[2,197,384]{2,0,1:T(2,128)(2,1)}, u32[]{:S(2)}) copy-start(bf16[2,197,384]{2,0,1:T(2,128)(2,1)} %param.4) | copy-start | bytes 907780
  18.2 8.5 %collective-permute-start.7 = (bf16[2,434,128]{2,1,0:T(8,128)(2,1)S(1)}, bf16[2,434,128]{2,1,0:T(8,128)(2,1)S(1)}, u32[]{:S(2)}, u32[]{:S(2)}) collective-permute-start(bf16[2,434,128]{2,1,0:T(8,128)(2,1)S(1)} %pad_maximum_fusion.3), channel_id=1, source_target_pairs={{0,2},{1,5},{2,0},{3,7},{4,6},{5,1},{6,4},{7,3},{8,10},{9,13},{10,... | collective-permute-start | bytes 666632 | tf_op jit(solution)/shard_map/ppermute | solution.py:416
  19.5 9.3 %collective-permute-start.4 = (bf16[4,434,128]{2,1,0:T(8,128)(2,1)S(1)}, bf16[4,434,128]{2,1,0:T(8,128)(2,1)S(1)}, u32[]{:S(2)}, u32[]{:S(2)}) collective-permute-start(bf16[4,434,128]{2,1,0:T(8,128)(2,1)S(1)} %pad_maximum_fusion.refs_4_), channel_id=1, source_target_pairs={{0,4},{1,3},{2,6},{3,1},{4,0},{5,7},{6,2},{7,5},{8,12},{9,11},{10,... | collective-permute-start | bytes 1333256 | tf_op jit(solution)/shard_map/ppermute | solution.py:416
  26.8 10.1 %copy-start = (bf16[4,434,128]{2,1,0:T(8,128)(2,1)}, bf16[4,434,128]{2,1,0:T(8,128)(2,1)S(1)}, u32[]{:S(2)}) copy-start(bf16[4,434,128]{2,1,0:T(8,128)(2,1)S(1)} %pad_maximum_fusion.1.refs_8_) | copy-start | bytes 1333252
  26.8 8.5 %collective-permute-start.8 = (bf16[4,434,128]{2,1,0:T(8,128)(2,1)S(1)}, bf16[4,434,128]{2,1,0:T(8,128)(2,1)S(1)}, u32[]{:S(2)}, u32[]{:S(2)}) collective-permute-start(bf16[4,434,128]{2,1,0:T(8,128)(2,1)S(1)} %pad_maximum_fusion.1.refs_8_), channel_id=1, source_target_pairs={{0,4},{1,3},{2,6},{3,1},{4,0},{5,7},{6,2},{7,5},{8,12},{9,11},{10,... | collective-permute-start | bytes 1333256 | tf_op jit(solution)/shard_map/ppermute | solution.py:416
  28.4 8.6 %collective-permute-start.5 = (bf16[4,434,128]{2,1,0:T(8,128)(2,1)S(1)}, bf16[4,434,128]{2,1,0:T(8,128)(2,1)S(1)}, u32[]{:S(2)}, u32[]{:S(2)}) collective-permute-start(bf16[4,434,128]{2,1,0:T(8,128)(2,1)S(1)} %pad_maximum_fusion.refs_4_), channel_id=1, source_target_pairs={{0,1},{1,0},{2,3},{3,2},{4,5},{5,4},{6,7},{7,6},{8,9},{9,8},{10,11... | collective-permute-start | bytes 1333256 | tf_op jit(solution)/shard_map/ppermute | solution.py:416
  28.4 8.6 %collective-permute-start.9 = (bf16[4,434,128]{2,1,0:T(8,128)(2,1)S(1)}, bf16[4,434,128]{2,1,0:T(8,128)(2,1)S(1)}, u32[]{:S(2)}, u32[]{:S(2)}) collective-permute-start(bf16[4,434,128]{2,1,0:T(8,128)(2,1)S(1)} %pad_maximum_fusion.1.refs_8_), channel_id=1, source_target_pairs={{0,1},{1,0},{2,3},{3,2},{4,5},{5,4},{6,7},{7,6},{8,9},{9,8},{10,11... | collective-permute-start | bytes 1333256 | tf_op jit(solution)/shard_map/ppermute | solution.py:416
  28.9 8.1 %collective-permute-start.6 = (bf16[4,434,128]{2,1,0:T(8,128)(2,1)S(1)}, bf16[4,434,128]{2,1,0:T(8,128)(2,1)S(1)}, u32[]{:S(2)}, u32[]{:S(2)}) collective-permute-start(bf16[4,434,128]{2,1,0:T(8,128)(2,1)S(1)} %collective-permute-done.4.refs_5_), channel_id=1, source_target_pairs={{0,1},{1,0},{2,3},{3,2},{4,5},{5,4},{6,7},{7,6},{8,9},{9,8},{10,11... | collective-permute-start | bytes 1333256 | tf_op jit(solution)/shard_map/ppermute | solution.py:416
  35.2 1.7 %copy-start.1 = (bf16[4,434,128]{2,1,0:T(8,128)(2,1)}, bf16[4,434,128]{2,1,0:T(8,128)(2,1)S(1)}, u32[]{:S(2)}) copy-start(bf16[4,434,128]{2,1,0:T(8,128)(2,1)S(1)} %collective-permute-done.8.refs_9_) | copy-start | bytes 1333252
  35.2 1.9 %collective-permute-start.10 = (bf16[4,434,128]{2,1,0:T(8,128)(2,1)S(1)}, bf16[4,434,128]{2,1,0:T(8,128)(2,1)}, u32[]{:S(2)}, u32[]{:S(2)}) collective-permute-start(bf16[4,434,128]{2,1,0:T(8,128)(2,1)S(1)} %collective-permute-done.8.refs_9_), channel_id=1, source_target_pairs={{0,1},{1,0},{2,3},{3,2},{4,5},{5,4},{6,7},{7,6},{8,9},{9,8},{10,11... | collective-permute-start | bytes 1333256 | tf_op jit(solution)/shard_map/ppermute | solution.py:416
  35.9 1.0 %copy-start.6 = (bf16[2,197,384]{2,0,1:T(2,128)(2,1)S(1)}, bf16[2,197,384]{2,0,1:T(2,128)(2,1)}, u32[]{:S(2)}) copy-start(bf16[2,197,384]{2,0,1:T(2,128)(2,1)} %param.6) | copy-start | bytes 907780
  37.0 0.8 copy-start.2
  37.0 0.9 copy-start.3
  62.3 2.0 %collective-permute-start.17 = (bf16[4,434,128]{2,1,0:T(8,128)(2,1)S(1)}, bf16[4,434,128]{2,1,0:T(8,128)(2,1)S(1)}, u32[]{:S(2)}, u32[]{:S(2)}) collective-permute-start(bf16[4,434,128]{2,1,0:T(8,128)(2,1)S(1)} %get-tuple-element.34), channel_id=1, source_target_pairs={{0,1},{1,0},{2,3},{3,2},{4,5},{5,4},{6,7},{7,6},{8,9},{9,8},{10,11... | collective-permute-start | bytes 1333256 | tf_op jit(solution)/shard_map/ppermute | solution.py:416
  62.9 3.1 %collective-permute-start.12 = (bf16[4,434,128]{2,1,0:T(8,128)(2,1)S(1)}, bf16[4,434,128]{2,1,0:T(8,128)(2,1)S(1)}, u32[]{:S(2)}, u32[]{:S(2)}) collective-permute-start(bf16[4,434,128]{2,1,0:T(8,128)(2,1)S(1)} %get-tuple-element.30), channel_id=1, source_target_pairs={{0,1},{1,0},{2,3},{3,2},{4,5},{5,4},{6,7},{7,6},{8,9},{9,8},{10,11... | collective-permute-start | bytes 1333256 | tf_op jit(solution)/shard_map/ppermute | solution.py:416
  63.0 4.6 %collective-permute-start.16 = (bf16[4,434,128]{2,1,0:T(8,128)(2,1)S(1)}, bf16[4,434,128]{2,1,0:T(8,128)(2,1)S(1)}, u32[]{:S(2)}, u32[]{:S(2)}) collective-permute-start(bf16[4,434,128]{2,1,0:T(8,128)(2,1)S(1)} %get-tuple-element.32), channel_id=1, source_target_pairs={{0,1},{1,0},{2,3},{3,2},{4,5},{5,4},{6,7},{7,6},{8,9},{9,8},{10,11... | collective-permute-start | bytes 1333256 | tf_op jit(solution)/shard_map/ppermute | solution.py:416
  64.5 8.5 %collective-permute-start.18 = (bf16[4,434,128]{2,1,0:T(8,128)(2,1)S(1)}, bf16[4,434,128]{2,1,0:T(8,128)(2,1)S(1)}, u32[]{:S(2)}, u32[]{:S(2)}) collective-permute-start(bf16[4,434,128]{2,1,0:T(8,128)(2,1)S(1)} %add_convert_fusion), channel_id=1, source_target_pairs={{0,4},{1,3},{2,6},{3,1},{4,0},{5,7},{6,2},{7,5},{8,12},{9,11},{10,... | collective-permute-start | bytes 1333256 | tf_op jit(solution)/shard_map/ppermute | solution.py:416
  66.1 8.4 %collective-permute-start.11 = (bf16[4,434,128]{2,1,0:T(8,128)(2,1)S(1)}, bf16[4,434,128]{2,1,0:T(8,128)(2,1)S(1)}, u32[]{:S(2)}, u32[]{:S(2)}) collective-permute-start(bf16[4,434,128]{2,1,0:T(8,128)(2,1)S(1)} %get-tuple-element.28), channel_id=1, source_target_pairs={{0,1},{1,0},{2,3},{3,2},{4,5},{5,4},{6,7},{7,6},{8,9},{9,8},{10,11... | collective-permute-start | bytes 1333256 | tf_op jit(solution)/shard_map/ppermute | solution.py:416
  66.2 14.0 %collective-permute-start.13 = (bf16[4,434,128]{2,1,0:T(8,128)(2,1)S(1)}, bf16[4,434,128]{2,1,0:T(8,128)(2,1)S(1)}, u32[]{:S(2)}, u32[]{:S(2)}) collective-permute-start(bf16[4,434,128]{2,1,0:T(8,128)(2,1)S(1)} %add_convert_fusion.1), channel_id=1, source_target_pairs={{0,4},{1,3},{2,6},{3,1},{4,0},{5,7},{6,2},{7,5},{8,12},{9,11},{10,... | collective-permute-start | bytes 1333256 | tf_op jit(solution)/shard_map/ppermute | solution.py:416
  73.1 8.6 %collective-permute-start.19 = (bf16[2,434,128]{2,1,0:T(8,128)(2,1)S(1)}, bf16[2,434,128]{2,1,0:T(8,128)(2,1)S(1)}, u32[]{:S(2)}, u32[]{:S(2)}) collective-permute-start(bf16[2,434,128]{2,1,0:T(8,128)(2,1)S(1)} %slice.66), channel_id=1, source_target_pairs={{0,2},{1,5},{2,0},{3,7},{4,6},{5,1},{6,4},{7,3},{8,10},{9,13},{10,... | collective-permute-start | bytes 666632 | tf_op jit(solution)/shard_map/ppermute | solution.py:416
  80.4 6.0 %collective-permute-start.14 = (bf16[2,434,128]{2,1,0:T(8,128)(2,1)S(1)}, bf16[2,434,128]{2,1,0:T(8,128)(2,1)S(1)}, u32[]{:S(2)}, u32[]{:S(2)}) collective-permute-start(bf16[2,434,128]{2,1,0:T(8,128)(2,1)S(1)} %slice.67), channel_id=1, source_target_pairs={{0,2},{1,5},{2,0},{3,7},{4,6},{5,1},{6,4},{7,3},{8,10},{9,13},{10,... | collective-permute-start | bytes 666632 | tf_op jit(solution)/shard_map/ppermute | solution.py:416
  81.8 6.1 %collective-permute-start.20 = (bf16[434,128]{1,0:T(8,128)(2,1)S(1)}, bf16[434,128]{1,0:T(8,128)(2,1)S(1)}, u32[]{:S(2)}, u32[]{:S(2)}) collective-permute-start(bf16[434,128]{1,0:T(8,128)(2,1)S(1)} %fusion.6), channel_id=1, source_target_pairs={{0,8},{1,9},{2,10},{3,11},{4,12},{5,13},{6,14},{7,15},{8,0},{9,1},... | collective-permute-start | bytes 333320 | tf_op jit(solution)/shard_map/ppermute | solution.py:416
  86.5 5.7 %collective-permute-start.15 = (bf16[434,128]{1,0:T(8,128)(2,1)S(1)}, bf16[434,128]{1,0:T(8,128)(2,1)S(1)}, u32[]{:S(2)}, u32[]{:S(2)}) collective-permute-start(bf16[434,128]{1,0:T(8,128)(2,1)S(1)} %fusion.5), channel_id=1, source_target_pairs={{0,8},{1,9},{2,10},{3,11},{4,12},{5,13},{6,14},{7,15},{8,0},{9,1},... | collective-permute-start | bytes 333320 | tf_op jit(solution)/shard_map/ppermute | solution.py:416
  87.9 6.9 %collective-permute-start.21 = (bf16[434,128]{1,0:T(8,128)(2,1)S(1)}, bf16[434,128]{1,0:T(8,128)(2,1)S(1)}, u32[]{:S(2)}, u32[]{:S(2)}) collective-permute-start(bf16[434,128]{1,0:T(8,128)(2,1)S(1)} %fusion.1), channel_id=1, source_target_pairs={{0,16},{1,17},{2,18},{3,19},{4,20},{5,21},{6,22},{7,23},{8,24},{9,... | collective-permute-start | bytes 333320 | tf_op jit(solution)/shard_map/ppermute | solution.py:416

commit v3 on v2

--- a/solution.py
+++ b/solution.py
@@ -85,7 +85,6 @@
     out_ref, gin_ref = refs[:2]
     shares = refs[2 : 2 + len(order)]
     (
-        stage,
         wide,
         wq,
         wo,
@@ -110,7 +109,6 @@
         gattn,
         gmix,
         gj,
-        sems,
     ) = refs[2 + len(order) :]
     me = me_ref[0]
     total = images * pad
@@ -346,16 +344,8 @@
     for b in range(images):
         gin_ref[b] = gmix[b * pad : b * pad + tok, :]
 
-    for d in range(devices):
-        stage[d] = wide[d * rows : (d + 1) * rows, :].astype(BF)
-    copies = [
-        pltpu.make_async_copy(stage.at[owner], ref, sems.at[k])
-        for k, (ref, owner) in enumerate(slots(shares))
-    ]
-    for c in copies:
-        c.start()
-    for c in copies:
-        c.wait()
+    for ref, owner in slots(shares):
+        ref[...] = wide[pl.ds(owner * rows, rows), :].astype(BF)
 
 
 def run_layer(me, counts, images, cotangent, groups, devices, interpret=False):
@@ -368,12 +358,10 @@
     )
     vmem = pl.BlockSpec(memory_space=pltpu.VMEM)
     smem = pl.BlockSpec(memory_space=pltpu.SMEM)
-    anyspace = pl.BlockSpec(memory_space=pl.ANY)
     parts = tuple(jax.ShapeDtypeStruct(g.shape, BF) for g in groups)
     act = jax.ShapeDtypeStruct(images.shape, BF)
     V = pltpu.VMEM
     scratch = [
-        V((devices, rows, LANES), BF),
         V((devices * rows, LANES), F32),
         V((D, 3 * D), BF),
         V((D, D), BF),
@@ -398,16 +386,15 @@
         V((total, D), BF),
         V((total, D), BF),
         V((total, 3 * D), BF),
-        pltpu.SemaphoreType.DMA((devices,)),
     ]
     return pl.pallas_call(
         body,
         name="layer",
         out_shape=(act, act) + parts,
         in_specs=[smem, smem, vmem, vmem] + [vmem] * len(groups),
-        out_specs=(vmem, vmem) + (anyspace,) * len(groups),
+        out_specs=(vmem, vmem) + (vmem,) * len(groups),
         scratch_shapes=scratch,
-        compiler_params=pltpu.CompilerParams(vmem_limit_bytes=48 << 20),
+        compiler_params=pltpu.CompilerParams(vmem_limit_bytes=32 << 20),
         interpret=interpret,
     )(me, counts, images, cotangent, *groups)
 
@@ -440,31 +427,24 @@
     outer = n // 8
     half = outer // 2
     got = {0: own, half: over_planes(own, n, half)}
-    if half > 1:
-        got[half // 2] = over_planes(own, n, half // 2)
-        names = sorted(got)
-        got = dict(zip(names, fence(*[got[s] for s in names])))
     bit = half // 2
     while bit:
         for s in sorted(got):
             if s ^ bit not in got:
                 got[s ^ bit] = over_planes(got[s], n, bit)
         bit //= 2
-    got = [got[s] for s in range(outer)]
-    a = jnp.stack(got[: outer // 2])
-    a1 = over_first(a, n)
-    an = jnp.concatenate([a, a1], axis=0)
+    own_first = over_first(own, n)
+    others = jnp.stack([got[s] for s in range(1, half)])
+    an = jnp.concatenate([own[None], others, own_first[None], over_first(others, n)], axis=0)
     af = over_second(an, n)
-    *rest, an = fence(*got[outer // 2 :], an)
-    b = jnp.stack(rest)
-    b1 = over_first(b, n)
-    bn = jnp.concatenate([b, b1], axis=0)
+    b = jnp.stack([got[s] for s in range(half, outer)])
+    bn = jnp.concatenate([b, over_first(b, n)], axis=0)
     bf = over_second(bn, n)
     return [an, af, over_core(an, n), over_core(af, n), bn, bf, over_core(bn, n), over_core(bf, n)]
 
 
 def reduce_groups(parts, n):
-    near, far = parts[:4], parts[4:]
+    near, far = list(parts[:4]), parts[4:]
 
     def add(held, got):
         return held.astype(F32) + got.astype(F32)
@@ -482,6 +462,7 @@
 
     outer = n // 8
     f1 = second_step(far, fc)
+    *f1, near[0], near[1], nc[0], nc[1] = fence(*f1, near[0], near[1], *nc)
     n1 = second_step(near, nc)
     f2 = first_step(*f1)
     n2 = first_step(*n1)

time: 95.8 us -> 85.1 us (0.89)
  Pallas kernels: 24.4 us -> 17.8 us
  waiting for transfers between devices: 37.9 us -> 35.5 us
  other arithmetic: 2.55 us -> 1.57 us
    pallas_call x1, Pallas kernels: 24.4 us -> 17.8 us  [run_layer(): pl.pallas_call(body, name='layer', out_shape=(act, act) + parts, in_specs...]
    ppermute x22 -> x23, waiting for transfers between devices: 37.9 us -> 35.5 us  [permute(): return lax.ppermute(value, 'dp', [(i, partner(i)) for i in range(devices)])]
    another operation x2 -> x1, other arithmetic: 1.01 us -> 0.02 us  [gather_groups(): b = jnp.stack([got[s] for s in range(half, outer)])]
    unnamed x18 -> x10, local copies, waits for them, and re-layouts: 3.6 us -> 2.9 us
    ppermute x22 -> x23, starting transfers between devices: 25.6 us -> 25.5 us  [permute(): return lax.ppermute(value, 'dp', [(i, partner(i)) for i in range(devices)])]
  transfers between devices with their start and end apart: 22 -> 23, of which waited for: 12 -> 15; matrix products, arithmetic and copies ran while one was open for 3% -> 3% of each run, Pallas kernels for 0% -> 0%
where the time goes in v3:
time: 85.1 us; the launch traced here: 84.9 us
  waiting for transfers between devices  35.5 us (42%)
  starting transfers between devices  25.5 us (30%)
  Pallas kernels  17.8 us (21%)
  local copies, waits for them, and re-layouts  2.99 us (4%)
  other arithmetic  1.57 us (2%)
  between operations  1.45 us (2%)
    ppermute x23, waiting for transfers between devices, permute(): return lax.ppermute(value, 'dp', [(i, partner(i)) for i in range(devices)])  35.5 us
    ppermute x23, starting transfers between devices, permute(): return lax.ppermute(value, 'dp', [(i, partner(i)) for i in range(devices)])  25.5 us
    pallas_call x1, Pallas kernels, run_layer(): pl.pallas_call(body, name='layer', out_shape=(act, act) + parts, in_specs...  17.8 us
    unnamed x10, local copies, waits for them, and re-layouts  2.9 us
  transfers between devices with their start and end apart: 23, of which 15 were waited for; matrix products, arithmetic and copies ran while one was open for 3% of the time, Pallas kernels for 0%

profile of v3, /device:TPU:0, one launch (start us, length us, event | category | flops | bytes accessed | tf_op | source)
XLA Modules:
  0.0 84.9 jit_solution(16872632011698718691)
XLA Ops:
  0.6 4.1 %collective-permute-start.6 = (bf16[434,128]{1,0:T(8,128)(2,1)}, bf16[434,128]{1,0:T(8,128)(2,1)S(1)}, u32[]{:S(2)}, u32[]{:S(2)}) collective-permute-start(bf16[434,128]{1,0:T(8,128)(2,1)} %bitcast.31), channel_id=1, source_target_pairs={{0,16},{1,17},{2,18},{3,19},{4,20},{5,21},{6,22},{7,23},{8,24},{9,... | collective-permute-start | bytes 333320 | tf_op jit(solution)/shard_map/ppermute | solution.py:403
  4.7 1.6 %collective-permute-start = (bf16[434,128]{1,0:T(8,128)(2,1)}, bf16[434,128]{1,0:T(8,128)(2,1)S(1)}, u32[]{:S(2)}, u32[]{:S(2)}) collective-permute-start(bf16[434,128]{1,0:T(8,128)(2,1)} %bitcast.32), channel_id=1, source_target_pairs={{0,8},{1,9},{2,10},{3,11},{4,12},{5,13},{6,14},{7,15},{8,0},{9,1},... | collective-permute-start | bytes 333320 | tf_op jit(solution)/shard_map/ppermute | solution.py:403
  6.3 4.3 %collective-permute-done.6 = bf16[434,128]{1,0:T(8,128)(2,1)S(1)} collective-permute-done((bf16[434,128]{1,0:T(8,128)(2,1)}, bf16[434,128]{1,0:T(8,128)(2,1)S(1)}, u32[]{:S(2)}, u32[]{:S(2)}) %collective-permute-start.6) | collective-permute-done | bytes 111136 | tf_op jit(solution)/shard_map/ppermute | solution.py:403
  10.6 0.7 collective-permute-start.7
  11.3 1.5 %collective-permute-start.1 = (bf16[434,128]{1,0:T(8,128)(2,1)}, bf16[434,128]{1,0:T(8,128)(2,1)S(1)}, u32[]{:S(2)}, u32[]{:S(2)}) collective-permute-start(bf16[434,128]{1,0:T(8,128)(2,1)} %bitcast.33), channel_id=1, source_target_pairs={{0,2},{1,5},{2,0},{3,7},{4,6},{5,1},{6,4},{7,3},{8,10},{9,13},{10,... | collective-permute-start | bytes 333320 | tf_op jit(solution)/shard_map/ppermute | solution.py:403
  13.3 2.0 %collective-permute-done.7 = bf16[434,128]{1,0:T(8,128)(2,1)S(1)} collective-permute-done((bf16[434,128]{1,0:T(8,128)(2,1)S(1)}, bf16[434,128]{1,0:T(8,128)(2,1)S(1)}, u32[]{:S(2)}, u32[]{:S(2)}) %collective-permute-start.7) | collective-permute-done | bytes 111136 | tf_op jit(solution)/shard_map/ppermute | solution.py:403
  15.4 1.6 %collective-permute-start.8 = (bf16[2,434,128]{2,1,0:T(8,128)(2,1)S(1)}, bf16[2,434,128]{2,1,0:T(8,128)(2,1)S(1)}, u32[]{:S(2)}, u32[]{:S(2)}) collective-permute-start(bf16[2,434,128]{2,1,0:T(8,128)(2,1)S(1)} %pad_maximum_fusion.2), channel_id=1, source_target_pairs={{0,2},{1,5},{2,0},{3,7},{4,6},{5,1},{6,4},{7,3},{8,10},{9,13},{10,... | collective-permute-start | bytes 666632 | tf_op jit(solution)/shard_map/ppermute | solution.py:403
  17.0 0.6 collective-permute-done.2
  17.6 1.6 %collective-permute-start.3 = (bf16[4,434,128]{2,1,0:T(8,128)(2,1)S(1)}, bf16[4,434,128]{2,1,0:T(8,128)(2,1)S(1)}, u32[]{:S(2)}, u32[]{:S(2)}) collective-permute-start(bf16[4,434,128]{2,1,0:T(8,128)(2,1)S(1)} %pad_maximum_fusion.refs_4_), channel_id=1, source_target_pairs={{0,4},{1,3},{2,6},{3,1},{4,0},{5,7},{6,2},{7,5},{8,12},{9,11},{10,... | collective-permute-start | bytes 1333256 | tf_op jit(solution)/shard_map/ppermute | solution.py:403
  19.2 4.5 %collective-permute-done.8 = bf16[2,434,128]{2,1,0:T(8,128)(2,1)S(1)} collective-permute-done((bf16[2,434,128]{2,1,0:T(8,128)(2,1)S(1)}, bf16[2,434,128]{2,1,0:T(8,128)(2,1)S(1)}, u32[]{:S(2)}, u32[]{:S(2)}) %collective-permute-start.8) | collective-permute-done | bytes 222240 | tf_op jit(solution)/shard_map/ppermute | solution.py:403
  23.8 1.7 %collective-permute-start.9 = (bf16[4,434,128]{2,1,0:T(8,128)(2,1)S(1)}, bf16[4,434,128]{2,1,0:T(8,128)(2,1)S(1)}, u32[]{:S(2)}, u32[]{:S(2)}) collective-permute-start(bf16[4,434,128]{2,1,0:T(8,128)(2,1)S(1)} %pad_maximum_fusion.1.refs_8_), channel_id=1, source_target_pairs={{0,4},{1,3},{2,6},{3,1},{4,0},{5,7},{6,2},{7,5},{8,12},{9,11},{10,... | collective-permute-start | bytes 1333256 | tf_op jit(solution)/shard_map/ppermute | solution.py:403
  26.2 6.0 %collective-permute-done.9.refs_9_ = bf16[4,434,128]{2,1,0:T(8,128)(2,1)S(1)} collective-permute-done((bf16[4,434,128]{2,1,0:T(8,128)(2,1)S(1)}, bf16[4,434,128]{2,1,0:T(8,128)(2,1)S(1)}, u32[]{:S(2)}, u32[]{:S(2)}) %collective-permute-start.9) | collective-permute-done | bytes 444448 | tf_op jit(solution)/shard_map/ppermute | solution.py:403
  32.9 0.9 %copy-done.1 = bf16[2,197,384]{2,0,1:T(2,128)(2,1)S(1)} copy-done((bf16[2,197,384]{2,0,1:T(2,128)(2,1)S(1)}, bf16[2,197,384]{2,0,1:T(2,128)(2,1)}, u32[]{:S(2)}) %copy-start.1) | copy-done | bytes 302616
  34.2 17.8 %layer.1 = (bf16[2,197,384]{2,1,0:T(8,128)(2,1)S(1)}, bf16[2,197,384]{2,1,0:T(8,128)(2,1)S(1)}, bf16[4,434,128]{2,1,0:T(8,128)(2,1)S(1)}, bf16[4,434,128]{2,1,0:...) custom-call(s32[1]{0:T(128)} %bitcast.refs_0_, ...), custom_call_target="tpu_custom_call" | custom-call | tf_op jit(solution)/shard_map/layer/pallas_call | solution.py:390
  53.1 0.8 collective-permute-done.13
  54.0 1.7 %collective-permute-start.14 = (bf16[4,434,128]{2,1,0:T(8,128)(2,1)S(1)}, bf16[4,434,128]{2,1,0:T(8,128)(2,1)S(1)}, u32[]{:S(2)}, u32[]{:S(2)}) collective-permute-start(bf16[4,434,128]{2,1,0:T(8,128)(2,1)S(1)} %add_convert_fusion.1), channel_id=1, source_target_pairs={{0,4},{1,3},{2,6},{3,1},{4,0},{5,7},{6,2},{7,5},{8,12},{9,11},{10,... | collective-permute-start | bytes 1333256 | tf_op jit(solution)/shard_map/ppermute | solution.py:403
  55.8 6.6 %collective-permute-done.14 = bf16[4,434,128]{2,1,0:T(8,128)(2,1)S(1)} collective-permute-done((bf16[4,434,128]{2,1,0:T(8,128)(2,1)S(1)}, bf16[4,434,128]{2,1,0:T(8,128)(2,1)S(1)}, u32[]{:S(2)}, u32[]{:S(2)}) %collective-permute-start.14) | collective-permute-done | bytes 444448 | tf_op jit(solution)/shard_map/ppermute | solution.py:403
  62.6 1.7 %collective-permute-start.20 = (bf16[2,434,128]{2,1,0:T(8,128)(2,1)S(1)}, bf16[2,434,128]{2,1,0:T(8,128)(2,1)S(1)}, u32[]{:S(2)}, u32[]{:S(2)}) collective-permute-start(bf16[2,434,128]{2,1,0:T(8,128)(2,1)S(1)} %slice.66), channel_id=1, source_target_pairs={{0,2},{1,5},{2,0},{3,7},{4,6},{5,1},{6,4},{7,3},{8,10},{9,13},{10,... | collective-permute-start | bytes 666632 | tf_op jit(solution)/shard_map/ppermute | solution.py:403
  64.4 1.6 %collective-permute-start.17 = (bf16[4,434,128]{2,1,0:T(8,128)(2,1)S(1)}, bf16[4,434,128]{2,1,0:T(8,128)(2,1)S(1)}, u32[]{:S(2)}, u32[]{:S(2)}) collective-permute-start(bf16[4,434,128]{2,1,0:T(8,128)(2,1)S(1)} %add_convert_fusion), channel_id=1, source_target_pairs={{0,4},{1,3},{2,6},{3,1},{4,0},{5,7},{6,2},{7,5},{8,12},{9,11},{10,... | collective-permute-start | bytes 1333256 | tf_op jit(solution)/shard_map/ppermute | solution.py:403
  65.9 5.1 %collective-permute-done.20 = bf16[2,434,128]{2,1,0:T(8,128)(2,1)S(1)} collective-permute-done((bf16[2,434,128]{2,1,0:T(8,128)(2,1)S(1)}, bf16[2,434,128]{2,1,0:T(8,128)(2,1)S(1)}, u32[]{:S(2)}, u32[]{:S(2)}) %collective-permute-start.20) | collective-permute-done | bytes 222240 | tf_op jit(solution)/shard_map/ppermute | solution.py:403
  71.1 1.1 %collective-permute-start.21 = (bf16[434,128]{1,0:T(8,128)(2,1)S(1)}, bf16[434,128]{1,0:T(8,128)(2,1)S(1)}, u32[]{:S(2)}, u32[]{:S(2)}) collective-permute-start(bf16[434,128]{1,0:T(8,128)(2,1)S(1)} %fusion.6), channel_id=1, source_target_pairs={{0,8},{1,9},{2,10},{3,11},{4,12},{5,13},{6,14},{7,15},{8,0},{9,1},... | collective-permute-start | bytes 333320 | tf_op jit(solution)/shard_map/ppermute | solution.py:403
  72.2 0.7 collective-permute-done.17
  73.0 0.9 %collective-permute-start.18 = (bf16[2,434,128]{2,1,0:T(8,128)(2,1)S(1)}, bf16[2,434,128]{2,1,0:T(8,128)(2,1)S(1)}, u32[]{:S(2)}, u32[]{:S(2)}) collective-permute-start(bf16[2,434,128]{2,1,0:T(8,128)(2,1)S(1)} %slice.67), channel_id=1, source_target_pairs={{0,2},{1,5},{2,0},{3,7},{4,6},{5,1},{6,4},{7,3},{8,10},{9,13},{10,... | collective-permute-start | bytes 666632 | tf_op jit(solution)/shard_map/ppermute | solution.py:403
  73.9 2.0 %collective-permute-done.21 = bf16[434,128]{1,0:T(8,128)(2,1)S(1)} collective-permute-done((bf16[434,128]{1,0:T(8,128)(2,1)S(1)}, bf16[434,128]{1,0:T(8,128)(2,1)S(1)}, u32[]{:S(2)}, u32[]{:S(2)}) %collective-permute-start.21) | collective-permute-done | bytes 111136 | tf_op jit(solution)/shard_map/ppermute | solution.py:403
  76.0 2.3 %collective-permute-start.22 = (bf16[434,128]{1,0:T(8,128)(2,1)S(1)}, bf16[434,128]{1,0:T(8,128)(2,1)S(1)}, u32[]{:S(2)}, u32[]{:S(2)}) collective-permute-start(bf16[434,128]{1,0:T(8,128)(2,1)S(1)} %fusion.1), channel_id=1, source_target_pairs={{0,16},{1,17},{2,18},{3,19},{4,20},{5,21},{6,22},{7,23},{8,24},{9,... | collective-permute-start | bytes 333320 | tf_op jit(solution)/shard_map/ppermute | solution.py:403
  78.3 0.8 collective-permute-done.18
  79.1 1.3 %collective-permute-start.19 = (bf16[434,128]{1,0:T(8,128)(2,1)S(1)}, bf16[434,128]{1,0:T(8,128)(2,1)S(1)}, u32[]{:S(2)}, u32[]{:S(2)}) collective-permute-start(bf16[434,128]{1,0:T(8,128)(2,1)S(1)} %fusion.5), channel_id=1, source_target_pairs={{0,8},{1,9},{2,10},{3,11},{4,12},{5,13},{6,14},{7,15},{8,0},{9,1},... | collective-permute-start | bytes 333320 | tf_op jit(solution)/shard_map/ppermute | solution.py:403
  80.4 0.9 %copy.9 = bf16[2,197,384]{2,0,1:T(2,128)(2,1)} copy(bf16[2,197,384]{2,1,0:T(8,128)(2,1)S(1)} %get-tuple-element.35) | data formatting | bytes 605184
  81.4 0.9 %copy.10 = bf16[2,197,384]{2,0,1:T(2,128)(2,1)} copy(bf16[2,197,384]{2,1,0:T(8,128)(2,1)S(1)} %get-tuple-element.36) | data formatting | bytes 605184
  82.3 0.6 collective-permute-done.22
  82.9 1.2 %collective-permute-done.19 = bf16[434,128]{1,0:T(8,128)(2,1)S(1)} collective-permute-done((bf16[434,128]{1,0:T(8,128)(2,1)S(1)}, bf16[434,128]{1,0:T(8,128)(2,1)S(1)}, u32[]{:S(2)}, u32[]{:S(2)}) %collective-permute-start.19) | collective-permute-done | bytes 111136 | tf_op jit(solution)/shard_map/ppermute | solution.py:403
  84.1 0.7 fusion.4
  (41 shorter events, 3.7 us)
Async XLA Ops:
  0.6 9.9 %collective-permute-start.6 = (bf16[434,128]{1,0:T(8,128)(2,1)}, bf16[434,128]{1,0:T(8,128)(2,1)S(1)}, u32[]{:S(2)}, u32[]{:S(2)}) collective-permute-start(bf16[434,128]{1,0:T(8,128)(2,1)} %bitcast.31), channel_id=1, source_target_pairs={{0,16},{1,17},{2,18},{3,19},{4,20},{5,21},{6,22},{7,23},{8,24},{9,... | collective-permute-start | bytes 333320 | tf_op jit(solution)/shard_map/ppermute | solution.py:403
  4.7 8.0 %collective-permute-start = (bf16[434,128]{1,0:T(8,128)(2,1)}, bf16[434,128]{1,0:T(8,128)(2,1)S(1)}, u32[]{:S(2)}, u32[]{:S(2)}) collective-permute-start(bf16[434,128]{1,0:T(8,128)(2,1)} %bitcast.32), channel_id=1, source_target_pairs={{0,8},{1,9},{2,10},{3,11},{4,12},{5,13},{6,14},{7,15},{8,0},{9,1},... | collective-permute-start | bytes 333320 | tf_op jit(solution)/shard_map/ppermute | solution.py:403
  10.6 4.8 %collective-permute-start.7 = (bf16[434,128]{1,0:T(8,128)(2,1)S(1)}, bf16[434,128]{1,0:T(8,128)(2,1)S(1)}, u32[]{:S(2)}, u32[]{:S(2)}) collective-permute-start(bf16[434,128]{1,0:T(8,128)(2,1)S(1)} %collective-permute-done.6), channel_id=1, source_target_pairs={{0,8},{1,9},{2,10},{3,11},{4,12},{5,13},{6,14},{7,15},{8,0},{9,1},... | collective-permute-start | bytes 333320 | tf_op jit(solution)/shard_map/ppermute | solution.py:403
  11.3 5.7 %collective-permute-start.1 = (bf16[434,128]{1,0:T(8,128)(2,1)}, bf16[434,128]{1,0:T(8,128)(2,1)S(1)}, u32[]{:S(2)}, u32[]{:S(2)}) collective-permute-start(bf16[434,128]{1,0:T(8,128)(2,1)} %bitcast.33), channel_id=1, source_target_pairs={{0,2},{1,5},{2,0},{3,7},{4,6},{5,1},{6,4},{7,3},{8,10},{9,13},{10,... | collective-permute-start | bytes 333320 | tf_op jit(solution)/shard_map/ppermute | solution.py:403
  12.8 4.8 %collective-permute-start.2 = (bf16[1,434,128]{2,1,0:T(8,128)(2,1)S(1)}, bf16[1,434,128]{2,1,0:T(8,128)(2,1)S(1)}, u32[]{:S(2)}, u32[]{:S(2)}) collective-permute-start(bf16[1,434,128]{2,1,0:T(8,128)(2,1)S(1)} %bitcast.35), channel_id=1, source_target_pairs={{0,2},{1,5},{2,0},{3,7},{4,6},{5,1},{6,4},{7,3},{8,10},{9,13},{10,... | collective-permute-start | bytes 333320 | tf_op jit(solution)/shard_map/ppermute | solution.py:403
  15.3 2.2 %copy-start.2 = (bf16[55552]{0:T(1024)(128)(2,1)S(1)}, bf16[55552]{0:T(1024)(128)(2,1)}, u32[]{:S(2)}) copy-start(bf16[55552]{0:T(1024)(128)(2,1)} %param.5) | copy-start | bytes 333316
  15.4 8.4 %collective-permute-start.8 = (bf16[2,434,128]{2,1,0:T(8,128)(2,1)S(1)}, bf16[2,434,128]{2,1,0:T(8,128)(2,1)S(1)}, u32[]{:S(2)}, u32[]{:S(2)}) collective-permute-start(bf16[2,434,128]{2,1,0:T(8,128)(2,1)S(1)} %pad_maximum_fusion.2), channel_id=1, source_target_pairs={{0,2},{1,5},{2,0},{3,7},{4,6},{5,1},{6,4},{7,3},{8,10},{9,13},{10,... | collective-permute-start | bytes 666632 | tf_op jit(solution)/shard_map/ppermute | solution.py:403
  17.6 15.3 %copy-start = (bf16[2,197,384]{2,0,1:T(2,128)(2,1)S(1)}, bf16[2,197,384]{2,0,1:T(2,128)(2,1)}, u32[]{:S(2)}) copy-start(bf16[2,197,384]{2,0,1:T(2,128)(2,1)} %param.4) | copy-start | bytes 907780
  17.6 8.5 %collective-permute-start.3 = (bf16[4,434,128]{2,1,0:T(8,128)(2,1)S(1)}, bf16[4,434,128]{2,1,0:T(8,128)(2,1)S(1)}, u32[]{:S(2)}, u32[]{:S(2)}) collective-permute-start(bf16[4,434,128]{2,1,0:T(8,128)(2,1)S(1)} %pad_maximum_fusion.refs_4_), channel_id=1, source_target_pairs={{0,4},{1,3},{2,6},{3,1},{4,0},{5,7},{6,2},{7,5},{8,12},{9,11},{10,... | collective-permute-start | bytes 1333256 | tf_op jit(solution)/shard_map/ppermute | solution.py:403
  23.8 8.5 %collective-permute-start.9 = (bf16[4,434,128]{2,1,0:T(8,128)(2,1)S(1)}, bf16[4,434,128]{2,1,0:T(8,128)(2,1)S(1)}, u32[]{:S(2)}, u32[]{:S(2)}) collective-permute-start(bf16[4,434,128]{2,1,0:T(8,128)(2,1)S(1)} %pad_maximum_fusion.1.refs_8_), channel_id=1, source_target_pairs={{0,4},{1,3},{2,6},{3,1},{4,0},{5,7},{6,2},{7,5},{8,12},{9,11},{10,... | collective-permute-start | bytes 1333256 | tf_op jit(solution)/shard_map/ppermute | solution.py:403
  25.5 8.4 %collective-permute-start.4 = (bf16[4,434,128]{2,1,0:T(8,128)(2,1)S(1)}, bf16[4,434,128]{2,1,0:T(8,128)(2,1)S(1)}, u32[]{:S(2)}, u32[]{:S(2)}) collective-permute-start(bf16[4,434,128]{2,1,0:T(8,128)(2,1)S(1)} %pad_maximum_fusion.refs_4_), channel_id=1, source_target_pairs={{0,1},{1,0},{2,3},{3,2},{4,5},{5,4},{6,7},{7,6},{8,9},{9,8},{10,11... | collective-permute-start | bytes 1333256 | tf_op jit(solution)/shard_map/ppermute | solution.py:403
  25.5 8.5 %collective-permute-start.10 = (bf16[4,434,128]{2,1,0:T(8,128)(2,1)S(1)}, bf16[4,434,128]{2,1,0:T(8,128)(2,1)S(1)}, u32[]{:S(2)}, u32[]{:S(2)}) collective-permute-start(bf16[4,434,128]{2,1,0:T(8,128)(2,1)S(1)} %pad_maximum_fusion.1.refs_8_), channel_id=1, source_target_pairs={{0,1},{1,0},{2,3},{3,2},{4,5},{5,4},{6,7},{7,6},{8,9},{9,8},{10,11... | collective-permute-start | bytes 1333256 | tf_op jit(solution)/shard_map/ppermute | solution.py:403
  26.1 7.8 %collective-permute-start.5 = (bf16[4,434,128]{2,1,0:T(8,128)(2,1)S(1)}, bf16[4,434,128]{2,1,0:T(8,128)(2,1)S(1)}, u32[]{:S(2)}, u32[]{:S(2)}) collective-permute-start(bf16[4,434,128]{2,1,0:T(8,128)(2,1)S(1)} %collective-permute-done.3.refs_5_), channel_id=1, source_target_pairs={{0,1},{1,0},{2,3},{3,2},{4,5},{5,4},{6,7},{7,6},{8,9},{9,8},{10,11... | collective-permute-start | bytes 1333256 | tf_op jit(solution)/shard_map/ppermute | solution.py:403
  32.2 1.9 %collective-permute-start.11 = (bf16[4,434,128]{2,1,0:T(8,128)(2,1)S(1)}, bf16[4,434,128]{2,1,0:T(8,128)(2,1)}, u32[]{:S(2)}, u32[]{:S(2)}) collective-permute-start(bf16[4,434,128]{2,1,0:T(8,128)(2,1)S(1)} %collective-permute-done.9.refs_9_), channel_id=1, source_target_pairs={{0,1},{1,0},{2,3},{3,2},{4,5},{5,4},{6,7},{7,6},{8,9},{9,8},{10,11... | collective-permute-start | bytes 1333256 | tf_op jit(solution)/shard_map/ppermute | solution.py:403
  32.9 1.0 %copy-start.1 = (bf16[2,197,384]{2,0,1:T(2,128)(2,1)S(1)}, bf16[2,197,384]{2,0,1:T(2,128)(2,1)}, u32[]{:S(2)}) copy-start(bf16[2,197,384]{2,0,1:T(2,128)(2,1)} %param.6) | copy-start | bytes 907780
  52.0 1.9 %collective-permute-start.13 = (bf16[4,434,128]{2,1,0:T(8,128)(2,1)S(1)}, bf16[4,434,128]{2,1,0:T(8,128)(2,1)S(1)}, u32[]{:S(2)}, u32[]{:S(2)}) collective-permute-start(bf16[4,434,128]{2,1,0:T(8,128)(2,1)S(1)} %get-tuple-element.24), channel_id=1, source_target_pairs={{0,1},{1,0},{2,3},{3,2},{4,5},{5,4},{6,7},{7,6},{8,9},{9,8},{10,11... | collective-permute-start | bytes 1333256 | tf_op jit(solution)/shard_map/ppermute | solution.py:403
  52.4 3.3 %collective-permute-start.12 = (bf16[4,434,128]{2,1,0:T(8,128)(2,1)S(1)}, bf16[4,434,128]{2,1,0:T(8,128)(2,1)S(1)}, u32[]{:S(2)}, u32[]{:S(2)}) collective-permute-start(bf16[4,434,128]{2,1,0:T(8,128)(2,1)S(1)} %get-tuple-element.22), channel_id=1, source_target_pairs={{0,1},{1,0},{2,3},{3,2},{4,5},{5,4},{6,7},{7,6},{8,9},{9,8},{10,11... | collective-permute-start | bytes 1333256 | tf_op jit(solution)/shard_map/ppermute | solution.py:403
  52.6 3.2 %collective-permute-start.15 = (bf16[4,434,128]{2,1,0:T(8,128)(2,1)S(1)}, bf16[4,434,128]{2,1,0:T(8,128)(2,1)S(1)}, u32[]{:S(2)}, u32[]{:S(2)}) collective-permute-start(bf16[4,434,128]{2,1,0:T(8,128)(2,1)S(1)} %get-tuple-element.27), channel_id=1, source_target_pairs={{0,1},{1,0},{2,3},{3,2},{4,5},{5,4},{6,7},{7,6},{8,9},{9,8},{10,11... | collective-permute-start | bytes 1333256 | tf_op jit(solution)/shard_map/ppermute | solution.py:403
  52.9 2.9 %collective-permute-start.16 = (bf16[4,434,128]{2,1,0:T(8,128)(2,1)S(1)}, bf16[4,434,128]{2,1,0:T(8,128)(2,1)S(1)}, u32[]{:S(2)}, u32[]{:S(2)}) collective-permute-start(bf16[4,434,128]{2,1,0:T(8,128)(2,1)S(1)} %get-tuple-element.28), channel_id=1, source_target_pairs={{0,1},{1,0},{2,3},{3,2},{4,5},{5,4},{6,7},{7,6},{8,9},{9,8},{10,11... | collective-permute-start | bytes 1333256 | tf_op jit(solution)/shard_map/ppermute | solution.py:403
  54.0 8.5 %collective-permute-start.14 = (bf16[4,434,128]{2,1,0:T(8,128)(2,1)S(1)}, bf16[4,434,128]{2,1,0:T(8,128)(2,1)S(1)}, u32[]{:S(2)}, u32[]{:S(2)}) collective-permute-start(bf16[4,434,128]{2,1,0:T(8,128)(2,1)S(1)} %add_convert_fusion.1), channel_id=1, source_target_pairs={{0,4},{1,3},{2,6},{3,1},{4,0},{5,7},{6,2},{7,5},{8,12},{9,11},{10,... | collective-permute-start | bytes 1333256 | tf_op jit(solution)/shard_map/ppermute | solution.py:403
  62.6 8.5 %collective-permute-start.20 = (bf16[2,434,128]{2,1,0:T(8,128)(2,1)S(1)}, bf16[2,434,128]{2,1,0:T(8,128)(2,1)S(1)}, u32[]{:S(2)}, u32[]{:S(2)}) collective-permute-start(bf16[2,434,128]{2,1,0:T(8,128)(2,1)S(1)} %slice.66), channel_id=1, source_target_pairs={{0,2},{1,5},{2,0},{3,7},{4,6},{5,1},{6,4},{7,3},{8,10},{9,13},{10,... | collective-permute-start | bytes 666632 | tf_op jit(solution)/shard_map/ppermute | solution.py:403
  64.4 8.5 %collective-permute-start.17 = (bf16[4,434,128]{2,1,0:T(8,128)(2,1)S(1)}, bf16[4,434,128]{2,1,0:T(8,128)(2,1)S(1)}, u32[]{:S(2)}, u32[]{:S(2)}) collective-permute-start(bf16[4,434,128]{2,1,0:T(8,128)(2,1)S(1)} %add_convert_fusion), channel_id=1, source_target_pairs={{0,4},{1,3},{2,6},{3,1},{4,0},{5,7},{6,2},{7,5},{8,12},{9,11},{10,... | collective-permute-start | bytes 1333256 | tf_op jit(solution)/shard_map/ppermute | solution.py:403
  71.1 4.8 %collective-permute-start.21 = (bf16[434,128]{1,0:T(8,128)(2,1)S(1)}, bf16[434,128]{1,0:T(8,128)(2,1)S(1)}, u32[]{:S(2)}, u32[]{:S(2)}) collective-permute-start(bf16[434,128]{1,0:T(8,128)(2,1)S(1)} %fusion.6), channel_id=1, source_target_pairs={{0,8},{1,9},{2,10},{3,11},{4,12},{5,13},{6,14},{7,15},{8,0},{9,1},... | collective-permute-start | bytes 333320 | tf_op jit(solution)/shard_map/ppermute | solution.py:403
  73.0 6.0 %collective-permute-start.18 = (bf16[2,434,128]{2,1,0:T(8,128)(2,1)S(1)}, bf16[2,434,128]{2,1,0:T(8,128)(2,1)S(1)}, u32[]{:S(2)}, u32[]{:S(2)}) collective-permute-start(bf16[2,434,128]{2,1,0:T(8,128)(2,1)S(1)} %slice.67), channel_id=1, source_target_pairs={{0,2},{1,5},{2,0},{3,7},{4,6},{5,1},{6,4},{7,3},{8,10},{9,13},{10,... | collective-permute-start | bytes 666632 | tf_op jit(solution)/shard_map/ppermute | solution.py:403
  76.0 7.0 %collective-permute-start.22 = (bf16[434,128]{1,0:T(8,128)(2,1)S(1)}, bf16[434,128]{1,0:T(8,128)(2,1)S(1)}, u32[]{:S(2)}, u32[]{:S(2)}) collective-permute-start(bf16[434,128]{1,0:T(8,128)(2,1)S(1)} %fusion.1), channel_id=1, source_target_pairs={{0,16},{1,17},{2,18},{3,19},{4,20},{5,21},{6,22},{7,23},{8,24},{9,... | collective-permute-start | bytes 333320 | tf_op jit(solution)/shard_map/ppermute | solution.py:403
  79.1 5.0 %collective-permute-start.19 = (bf16[434,128]{1,0:T(8,128)(2,1)S(1)}, bf16[434,128]{1,0:T(8,128)(2,1)S(1)}, u32[]{:S(2)}, u32[]{:S(2)}) collective-permute-start(bf16[434,128]{1,0:T(8,128)(2,1)S(1)} %fusion.5), channel_id=1, source_target_pairs={{0,8},{1,9},{2,10},{3,11},{4,12},{5,13},{6,14},{7,15},{8,0},{9,1},... | collective-permute-start | bytes 333320 | tf_op jit(solution)/shard_map/ppermute | solution.py:403

commit v4 on v3

--- a/solution.py
+++ b/solution.py
@@ -125,13 +125,8 @@
 
     for b in range(images):
         live = (count_ref[0] > b).astype(F32)
-        zeros = jnp.zeros((pad - tok, D), F32)
-        x_s[b * pad : (b + 1) * pad, :] = jnp.concatenate(
-            [image_ref[b].astype(F32), zeros], axis=0
-        )
-        glow[b * pad : (b + 1) * pad, :] = jnp.concatenate(
-            [cot_ref[b].astype(F32) * live, zeros], axis=0
-        ).astype(BF)
+        x_s[b * pad : (b + 1) * pad, :] = image_ref[b].astype(F32)
+        glow[b * pad : (b + 1) * pad, :] = (cot_ref[b].astype(F32) * live).astype(BF)
 
     for ref, owner in slots(groups):
         wide[pl.ds(owner * rows, rows), :] = ref[...].astype(F32)
@@ -194,16 +189,15 @@
             query = slab(qkv, b, h * LANES)
             keys = slab(qkv, b, D + h * LANES)
             values = slab(qkv, b, 2 * D + h * LANES)
-            outs = []
-            for s in range(2):
-                scores = jnp.where(key_ok, dot_nt(query * halves[s], keys) * scale, -1e30)
-                top = jnp.max(scores, axis=-1, keepdims=True)
-                weight = jnp.exp(scores - top)
-                prob = weight * (1.0 / jnp.sum(weight, axis=-1, keepdims=True))
-                probs[(b * HEADS // 2 + h) * 2 + s] = prob
-                outs.append(dot_nn(prob.astype(BF), values))
+            both = jnp.concatenate([query * halves[0], query * halves[1]], axis=0)
+            scores = jnp.where(key_ok, dot_nt(both, keys) * scale, -1e30)
+            top = jnp.max(scores, axis=-1, keepdims=True)
+            weight = jnp.exp(scores - top)
+            prob = weight * (1.0 / jnp.sum(weight, axis=-1, keepdims=True))
+            probs[b * HEADS // 2 + h] = prob
+            outs = dot_nn(prob.astype(BF), values)
             mixed[b * pad : (b + 1) * pad, h * LANES : (h + 1) * LANES] = jnp.where(
-                low_lane, outs[0], outs[1]
+                low_lane, outs[:pad], outs[pad:]
             ).astype(BF)
 
     acc[...] = dot_nn(mixed[...], wo[...])
@@ -295,24 +289,21 @@
             keys = slab(qkv, b, D + h * LANES)
             values = slab(qkv, b, 2 * D + h * LANES)
             grads = slab(gmix, b, h * LANES)
-            parts = []
-            for s in range(2):
-                prob = probs[(b * HEADS // 2 + h) * 2 + s]
-                grad_prob = dot_nt(grads * halves[s], values)
-                total_s = jnp.sum(grad_prob * prob, axis=-1, keepdims=True)
-                grad_score = (prob * (grad_prob - total_s)).astype(BF)
-                parts.append(
-                    (
-                        dot_nn(grad_score, keys) * scale,
-                        dot_tn(grad_score, query) * scale,
-                        dot_tn(prob.astype(BF), grads),
-                    )
-                )
+            both = jnp.concatenate([grads * halves[0], grads * halves[1]], axis=0)
+            both_query = jnp.concatenate([query * halves[0], query * halves[1]], axis=0)
+            prob = probs[b * HEADS // 2 + h]
+            grad_prob = dot_nt(both, values)
+            total_s = jnp.sum(grad_prob * prob, axis=-1, keepdims=True)
+            grad_score = (prob * (grad_prob - total_s)).astype(BF)
+            grad_query = dot_nn(grad_score, keys) * scale
+            found = (
+                jnp.where(low_lane, grad_query[:pad], grad_query[pad:]),
+                dot_tn(grad_score, both_query) * scale,
+                dot_tn(prob.astype(BF), both),
+            )
             for t in range(3):
                 column = t * D + h * LANES
-                gj[b * pad : (b + 1) * pad, column : column + LANES] = jnp.where(
-                    low_lane, parts[0][t], parts[1][t]
-                ).astype(BF)
+                gj[b * pad : (b + 1) * pad, column : column + LANES] = found[t].astype(BF)
 
     for t in range(3):
         scatter(dot_tn(normed[...], gj[:, t * D : (t + 1) * D]), R_QKV + 3 * t, 3 * D // LANES)
@@ -348,10 +339,9 @@
         ref[...] = wide[pl.ds(owner * rows, rows), :].astype(BF)
 
 
-def run_layer(me, counts, images, cotangent, groups, devices, interpret=False):
+def run_layer(me, counts, images, cotangent, tok, groups, devices, interpret=False):
     rows = groups[0].shape[1]
-    count, tok, _ = images.shape
-    pad = (tok + 15) // 16 * 16
+    count, pad, _ = images.shape
     total = count * pad
     body = lambda *refs: layer_body(
         *refs, devices=devices, rows=rows, images=count, tok=tok, pad=pad
@@ -359,7 +349,7 @@
     vmem = pl.BlockSpec(memory_space=pltpu.VMEM)
     smem = pl.BlockSpec(memory_space=pltpu.SMEM)
     parts = tuple(jax.ShapeDtypeStruct(g.shape, BF) for g in groups)
-    act = jax.ShapeDtypeStruct(images.shape, BF)
+    act = jax.ShapeDtypeStruct((count, tok, D), BF)
     V = pltpu.VMEM
     scratch = [
         V((devices * rows, LANES), F32),
@@ -372,7 +362,7 @@
         V((total, 1), F32),
         V((total, D), BF),
         V((total, 3 * D), BF),
-        V((count * HEADS, pad, pad), F32),
+        V((count * HEADS // 2, 2 * pad, pad), F32),
         V((total, D), BF),
         V((total, D), F32),
         V((total, D), F32),
@@ -423,7 +413,7 @@
     return lax.optimization_barrier(values)
 
 
-def gather_groups(own, n):
+def gather_groups(own, n, *ready):
     outer = n // 8
     half = outer // 2
     got = {0: own, half: over_planes(own, n, half)}
@@ -439,8 +429,11 @@
     af = over_second(an, n)
     b = jnp.stack([got[s] for s in range(half, outer)])
     bn = jnp.concatenate([b, over_first(b, n)], axis=0)
+    bn, *ready = fence(bn, *ready)
     bf = over_second(bn, n)
-    return [an, af, over_core(an, n), over_core(af, n), bn, bf, over_core(bn, n), over_core(bf, n)]
+    groups = [an, af, over_core(an, n), over_core(af, n)]
+    groups += [bn, bf, over_core(bn, n), over_core(bf, n)]
+    return groups, *ready
 
 
 def reduce_groups(parts, n):
@@ -462,9 +455,10 @@
 
     outer = n // 8
     f1 = second_step(far, fc)
-    *f1, near[0], near[1], nc[0], nc[1] = fence(*f1, near[0], near[1], *nc)
     n1 = second_step(near, nc)
     f2 = first_step(*f1)
+    n1 = list(n1)
+    *f2, n1[1] = fence(*f2, n1[1])
     n2 = first_step(*n1)
     f3 = add(*f2)
     far = [f3[s] for s in range(outer - outer // 2)]
@@ -488,9 +482,13 @@
 def on_device(images, params, cotangent, counts):
     devices = lax.axis_size("dp")
     own = params.reshape(-1, LANES)
-    groups = gather_groups(own, devices)
+    tok = images.shape[1]
+    blank = ((0, 0), (0, (tok + 15) // 16 * 16 - tok), (0, 0))
+    groups, images, cotangent = gather_groups(
+        own, devices, jnp.pad(images, blank), jnp.pad(cotangent, blank)
+    )
     me = lax.axis_index("dp").astype(jnp.int32).reshape(1)
-    result, image_grad, *parts = run_layer(me, counts, images, cotangent, groups, devices)
+    result, image_grad, *parts = run_layer(me, counts, images, cotangent, tok, groups, devices)
     owned = reduce_groups(parts, devices)
     return (result, image_grad, owned.reshape(-1))
 

time: 85.1 us -> 82.6 us (0.971)
  Pallas kernels: 17.8 us -> 16.3 us
  starting transfers between devices: 25.5 us -> 24.5 us
    pallas_call x1, Pallas kernels: 17.8 us -> 16.3 us  [run_layer(): pl.pallas_call(body, name='layer', out_shape=(act, act) + parts, in_specs...]
    ppermute x23, starting transfers between devices: 25.5 us -> 24.5 us  [permute(): return lax.ppermute(value, 'dp', [(i, partner(i)) for i in range(devices)])]
  transfers between devices with their start and end apart: 23 -> 23, of which waited for: 15 -> 13; matrix products, arithmetic and copies ran while one was open for 3% -> 4% of each run, Pallas kernels for 0% -> 0%
where the time goes in v4:
time: 82.6 us; the launch traced here: 82.5 us
  waiting for transfers between devices  35.9 us (43%)
  starting transfers between devices  24.5 us (30%)
  Pallas kernels  16.3 us (20%)
  local copies, waits for them, and re-layouts  2.65 us (3%)
  other arithmetic  1.54 us (2%)
  between operations  1.47 us (2%)
    ppermute x23, waiting for transfers between devices, permute(): return lax.ppermute(value, 'dp', [(i, partner(i)) for i in range(devices)])  35.9 us
    ppermute x23, starting transfers between devices, permute(): return lax.ppermute(value, 'dp', [(i, partner(i)) for i in range(devices)])  24.5 us
    pallas_call x1, Pallas kernels, run_layer(): pl.pallas_call(body, name='layer', out_shape=(act, act) + parts, in_specs...  16.3 us
    unnamed x10, local copies, waits for them, and re-layouts  2.46 us
  transfers between devices with their start and end apart: 23, of which 13 were waited for; matrix products, arithmetic and copies ran while one was open for 4% of the time, Pallas kernels for 0%

profile of v4, /device:TPU:0, one launch (start us, length us, event | category | flops | bytes accessed | tf_op | source)
XLA Modules:
  0.0 82.5 jit_solution(2487518173006796713)
XLA Ops:
  0.6 4.1 %collective-permute-start = (bf16[434,128]{1,0:T(8,128)(2,1)}, bf16[434,128]{1,0:T(8,128)(2,1)S(1)}, u32[]{:S(2)}, u32[]{:S(2)}) collective-permute-start(bf16[434,128]{1,0:T(8,128)(2,1)} %bitcast.31), channel_id=1, source_target_pairs={{0,16},{1,17},{2,18},{3,19},{4,20},{5,21},{6,22},{7,23},{8,24},{9,... | collective-permute-start | bytes 333320 | tf_op jit(solution)/shard_map/ppermute | solution.py:393
  4.7 1.6 %collective-permute-start.3 = (bf16[434,128]{1,0:T(8,128)(2,1)}, bf16[434,128]{1,0:T(8,128)(2,1)S(1)}, u32[]{:S(2)}, u32[]{:S(2)}) collective-permute-start(bf16[434,128]{1,0:T(8,128)(2,1)} %bitcast.32), channel_id=1, source_target_pairs={{0,8},{1,9},{2,10},{3,11},{4,12},{5,13},{6,14},{7,15},{8,0},{9,1},... | collective-permute-start | bytes 333320 | tf_op jit(solution)/shard_map/ppermute | solution.py:393
  6.3 4.3 %collective-permute-done = bf16[434,128]{1,0:T(8,128)(2,1)S(1)} collective-permute-done((bf16[434,128]{1,0:T(8,128)(2,1)}, bf16[434,128]{1,0:T(8,128)(2,1)S(1)}, u32[]{:S(2)}, u32[]{:S(2)}) %collective-permute-start) | collective-permute-done | bytes 111136 | tf_op jit(solution)/shard_map/ppermute | solution.py:393
  10.6 0.7 collective-permute-start.1
  11.3 1.5 %collective-permute-start.4 = (bf16[434,128]{1,0:T(8,128)(2,1)}, bf16[434,128]{1,0:T(8,128)(2,1)S(1)}, u32[]{:S(2)}, u32[]{:S(2)}) collective-permute-start(bf16[434,128]{1,0:T(8,128)(2,1)} %bitcast.33), channel_id=1, source_target_pairs={{0,2},{1,5},{2,0},{3,7},{4,6},{5,1},{6,4},{7,3},{8,10},{9,13},{10,... | collective-permute-start | bytes 333320 | tf_op jit(solution)/shard_map/ppermute | solution.py:393
  12.8 0.5 collective-permute-start.5
  13.3 2.0 %collective-permute-done.1 = bf16[434,128]{1,0:T(8,128)(2,1)S(1)} collective-permute-done((bf16[434,128]{1,0:T(8,128)(2,1)S(1)}, bf16[434,128]{1,0:T(8,128)(2,1)S(1)}, u32[]{:S(2)}, u32[]{:S(2)}) %collective-permute-start.1) | collective-permute-done | bytes 111136 | tf_op jit(solution)/shard_map/ppermute | solution.py:393
  15.4 1.6 %collective-permute-start.2 = (bf16[2,434,128]{2,1,0:T(8,128)(2,1)S(1)}, bf16[2,434,128]{2,1,0:T(8,128)(2,1)S(1)}, u32[]{:S(2)}, u32[]{:S(2)}) collective-permute-start(bf16[2,434,128]{2,1,0:T(8,128)(2,1)S(1)} %pad_maximum_fusion.2), channel_id=1, source_target_pairs={{0,2},{1,5},{2,0},{3,7},{4,6},{5,1},{6,4},{7,3},{8,10},{9,13},{10,... | collective-permute-start | bytes 666632 | tf_op jit(solution)/shard_map/ppermute | solution.py:393
  18.1 1.6 %collective-permute-start.6 = (bf16[4,434,128]{2,1,0:T(8,128)(2,1)S(1)}, bf16[4,434,128]{2,1,0:T(8,128)(2,1)S(1)}, u32[]{:S(2)}, u32[]{:S(2)}) collective-permute-start(bf16[4,434,128]{2,1,0:T(8,128)(2,1)S(1)} %pad_maximum_fusion.1.refs_4_), channel_id=1, source_target_pairs={{0,4},{1,3},{2,6},{3,1},{4,0},{5,7},{6,2},{7,5},{8,12},{9,11},{10,... | collective-permute-start | bytes 1333256 | tf_op jit(solution)/shard_map/ppermute | solution.py:393
  19.7 4.1 %collective-permute-done.2 = bf16[2,434,128]{2,1,0:T(8,128)(2,1)S(1)} collective-permute-done((bf16[2,434,128]{2,1,0:T(8,128)(2,1)S(1)}, bf16[2,434,128]{2,1,0:T(8,128)(2,1)S(1)}, u32[]{:S(2)}, u32[]{:S(2)}) %collective-permute-start.2) | collective-permute-done | bytes 222240 | tf_op jit(solution)/shard_map/ppermute | solution.py:393
  23.8 1.7 %collective-permute-start.9 = (bf16[4,434,128]{2,1,0:T(8,128)(2,1)S(1)}, bf16[4,434,128]{2,1,0:T(8,128)(2,1)S(1)}, u32[]{:S(2)}, u32[]{:S(2)}) collective-permute-start(bf16[4,434,128]{2,1,0:T(8,128)(2,1)S(1)} %pad_maximum_fusion.refs_8_), channel_id=1, source_target_pairs={{0,4},{1,3},{2,6},{3,1},{4,0},{5,7},{6,2},{7,5},{8,12},{9,11},{10,... | collective-permute-start | bytes 1333256 | tf_op jit(solution)/shard_map/ppermute | solution.py:393
  25.5 0.5 collective-permute-start.10
  26.0 0.5 collective-permute-done.6.refs_5_
  26.6 5.7 %collective-permute-done.9.refs_9_ = bf16[4,434,128]{2,1,0:T(8,128)(2,1)S(1)} collective-permute-done((bf16[4,434,128]{2,1,0:T(8,128)(2,1)S(1)}, bf16[4,434,128]{2,1,0:T(8,128)(2,1)S(1)}, u32[]{:S(2)}, u32[]{:S(2)}) %collective-permute-start.9) | collective-permute-done | bytes 444448 | tf_op jit(solution)/shard_map/ppermute | solution.py:393
  33.0 1.2 %collective-permute-done.11.refs_11_ = bf16[4,434,128]{2,1,0:T(8,128)(2,1)} collective-permute-done((bf16[4,434,128]{2,1,0:T(8,128)(2,1)S(1)}, bf16[4,434,128]{2,1,0:T(8,128)(2,1)}, u32[]{:S(2)}, u32[]{:S(2)}) %collective-permute-start.11) | collective-permute-done | bytes 444448 | tf_op jit(solution)/shard_map/ppermute | solution.py:393
  34.2 16.3 %layer.1 = (bf16[2,197,384]{2,1,0:T(8,128)(2,1)S(1)}, bf16[2,197,384]{2,1,0:T(8,128)(2,1)S(1)}, bf16[4,434,128]{2,1,0:T(8,128)(2,1)S(1)}, bf16[4,434,128]{2,1,0:...) custom-call(s32[1]{0:T(128)} %bitcast.refs_0_, ...), custom_call_target="tpu_custom_call" | custom-call | tf_op jit(solution)/shard_map/layer/pallas_call | solution.py:380
  51.3 1.2 %collective-permute-done.14 = bf16[4,434,128]{2,1,0:T(8,128)(2,1)S(1)} collective-permute-done((bf16[4,434,128]{2,1,0:T(8,128)(2,1)S(1)}, bf16[4,434,128]{2,1,0:T(8,128)(2,1)S(1)}, u32[]{:S(2)}, u32[]{:S(2)}) %collective-permute-start.14) | collective-permute-done | bytes 444448 | tf_op jit(solution)/shard_map/ppermute | solution.py:393
  52.6 1.7 %collective-permute-start.15 = (bf16[4,434,128]{2,1,0:T(8,128)(2,1)S(1)}, bf16[4,434,128]{2,1,0:T(8,128)(2,1)S(1)}, u32[]{:S(2)}, u32[]{:S(2)}) collective-permute-start(bf16[4,434,128]{2,1,0:T(8,128)(2,1)S(1)} %add_convert_fusion.1), channel_id=1, source_target_pairs={{0,4},{1,3},{2,6},{3,1},{4,0},{5,7},{6,2},{7,5},{8,12},{9,11},{10,... | collective-permute-start | bytes 1333256 | tf_op jit(solution)/shard_map/ppermute | solution.py:393
  54.4 0.5 collective-permute-start.18
  54.9 6.1 %collective-permute-done.15 = bf16[4,434,128]{2,1,0:T(8,128)(2,1)S(1)} collective-permute-done((bf16[4,434,128]{2,1,0:T(8,128)(2,1)S(1)}, bf16[4,434,128]{2,1,0:T(8,128)(2,1)S(1)}, u32[]{:S(2)}, u32[]{:S(2)}) %collective-permute-start.15) | collective-permute-done | bytes 444448 | tf_op jit(solution)/shard_map/ppermute | solution.py:393
  61.2 1.7 %collective-permute-start.16 = (bf16[2,434,128]{2,1,0:T(8,128)(2,1)S(1)}, bf16[2,434,128]{2,1,0:T(8,128)(2,1)S(1)}, u32[]{:S(2)}, u32[]{:S(2)}) collective-permute-start(bf16[2,434,128]{2,1,0:T(8,128)(2,1)S(1)} %slice.66), channel_id=1, source_target_pairs={{0,2},{1,5},{2,0},{3,7},{4,6},{5,1},{6,4},{7,3},{8,10},{9,13},{10,... | collective-permute-start | bytes 666632 | tf_op jit(solution)/shard_map/ppermute | solution.py:393
  62.9 5.3 %collective-permute-done.18 = bf16[4,434,128]{2,1,0:T(8,128)(2,1)S(1)} collective-permute-done((bf16[4,434,128]{2,1,0:T(8,128)(2,1)S(1)}, bf16[4,434,128]{2,1,0:T(8,128)(2,1)S(1)}, u32[]{:S(2)}, u32[]{:S(2)}) %collective-permute-start.18) | collective-permute-done | bytes 444448 | tf_op jit(solution)/shard_map/ppermute | solution.py:393
  68.3 0.6 collective-permute-start.21
  69.1 1.6 %collective-permute-start.19 = (bf16[2,434,128]{2,1,0:T(8,128)(2,1)S(1)}, bf16[2,434,128]{2,1,0:T(8,128)(2,1)S(1)}, u32[]{:S(2)}, u32[]{:S(2)}) collective-permute-start(bf16[2,434,128]{2,1,0:T(8,128)(2,1)S(1)} %slice.65), channel_id=1, source_target_pairs={{0,2},{1,5},{2,0},{3,7},{4,6},{5,1},{6,4},{7,3},{8,10},{9,13},{10,... | collective-permute-start | bytes 666632 | tf_op jit(solution)/shard_map/ppermute | solution.py:393
  70.7 2.7 %collective-permute-done.21 = bf16[434,128]{1,0:T(8,128)(2,1)S(1)} collective-permute-done((bf16[434,128]{1,0:T(8,128)(2,1)S(1)}, bf16[434,128]{1,0:T(8,128)(2,1)S(1)}, u32[]{:S(2)}, u32[]{:S(2)}) %collective-permute-start.21) | collective-permute-done | bytes 111136 | tf_op jit(solution)/shard_map/ppermute | solution.py:393
  73.3 2.2 %collective-permute-start.22 = (bf16[434,128]{1,0:T(8,128)(2,1)S(1)}, bf16[434,128]{1,0:T(8,128)(2,1)S(1)}, u32[]{:S(2)}, u32[]{:S(2)}) collective-permute-start(bf16[434,128]{1,0:T(8,128)(2,1)S(1)} %fusion.1), channel_id=1, source_target_pairs={{0,16},{1,17},{2,18},{3,19},{4,20},{5,21},{6,22},{7,23},{8,24},{9,... | collective-permute-start | bytes 333320 | tf_op jit(solution)/shard_map/ppermute | solution.py:393
  75.6 1.8 %collective-permute-start.20 = (bf16[434,128]{1,0:T(8,128)(2,1)S(1)}, bf16[434,128]{1,0:T(8,128)(2,1)S(1)}, u32[]{:S(2)}, u32[]{:S(2)}) collective-permute-start(bf16[434,128]{1,0:T(8,128)(2,1)S(1)} %fusion.5), channel_id=1, source_target_pairs={{0,8},{1,9},{2,10},{3,11},{4,12},{5,13},{6,14},{7,15},{8,0},{9,1},... | collective-permute-start | bytes 333320 | tf_op jit(solution)/shard_map/ppermute | solution.py:393
  77.4 0.9 %copy.9 = bf16[2,197,384]{2,0,1:T(2,128)(2,1)} copy(bf16[2,197,384]{2,1,0:T(8,128)(2,1)S(1)} %get-tuple-element.35) | data formatting | bytes 605184
  78.4 0.9 %copy.10 = bf16[2,197,384]{2,0,1:T(2,128)(2,1)} copy(bf16[2,197,384]{2,1,0:T(8,128)(2,1)S(1)} %get-tuple-element.36) | data formatting | bytes 605184
  79.3 1.5 %collective-permute-done.22 = bf16[434,128]{1,0:T(8,128)(2,1)S(1)} collective-permute-done((bf16[434,128]{1,0:T(8,128)(2,1)S(1)}, bf16[434,128]{1,0:T(8,128)(2,1)S(1)}, u32[]{:S(2)}, u32[]{:S(2)}) %collective-permute-start.22) | collective-permute-done | bytes 111136 | tf_op jit(solution)/shard_map/ppermute | solution.py:393
  80.9 0.9 %collective-permute-done.20 = bf16[434,128]{1,0:T(8,128)(2,1)S(1)} collective-permute-done((bf16[434,128]{1,0:T(8,128)(2,1)S(1)}, bf16[434,128]{1,0:T(8,128)(2,1)S(1)}, u32[]{:S(2)}, u32[]{:S(2)}) %collective-permute-start.20) | collective-permute-done | bytes 111136 | tf_op jit(solution)/shard_map/ppermute | solution.py:393
  81.7 0.7 fusion.4
  (43 shorter events, 2.7 us)
Async XLA Ops:
  0.6 16.4 %copy-start = (bf16[2,197,384]{2,0,1:T(2,128)(2,1)S(1)}, bf16[2,197,384]{2,0,1:T(2,128)(2,1)}, u32[]{:S(2)}) copy-start(bf16[2,197,384]{2,0,1:T(2,128)(2,1)} %param.4) | copy-start | bytes 907780
  0.6 9.9 %collective-permute-start = (bf16[434,128]{1,0:T(8,128)(2,1)}, bf16[434,128]{1,0:T(8,128)(2,1)S(1)}, u32[]{:S(2)}, u32[]{:S(2)}) collective-permute-start(bf16[434,128]{1,0:T(8,128)(2,1)} %bitcast.31), channel_id=1, source_target_pairs={{0,16},{1,17},{2,18},{3,19},{4,20},{5,21},{6,22},{7,23},{8,24},{9,... | collective-permute-start | bytes 333320 | tf_op jit(solution)/shard_map/ppermute | solution.py:393
  4.7 8.0 %collective-permute-start.3 = (bf16[434,128]{1,0:T(8,128)(2,1)}, bf16[434,128]{1,0:T(8,128)(2,1)S(1)}, u32[]{:S(2)}, u32[]{:S(2)}) collective-permute-start(bf16[434,128]{1,0:T(8,128)(2,1)} %bitcast.32), channel_id=1, source_target_pairs={{0,8},{1,9},{2,10},{3,11},{4,12},{5,13},{6,14},{7,15},{8,0},{9,1},... | collective-permute-start | bytes 333320 | tf_op jit(solution)/shard_map/ppermute | solution.py:393
  10.6 4.8 %collective-permute-start.1 = (bf16[434,128]{1,0:T(8,128)(2,1)S(1)}, bf16[434,128]{1,0:T(8,128)(2,1)S(1)}, u32[]{:S(2)}, u32[]{:S(2)}) collective-permute-start(bf16[434,128]{1,0:T(8,128)(2,1)S(1)} %collective-permute-done), channel_id=1, source_target_pairs={{0,8},{1,9},{2,10},{3,11},{4,12},{5,13},{6,14},{7,15},{8,0},{9,1},... | collective-permute-start | bytes 333320 | tf_op jit(solution)/shard_map/ppermute | solution.py:393
  11.3 5.9 %collective-permute-start.4 = (bf16[434,128]{1,0:T(8,128)(2,1)}, bf16[434,128]{1,0:T(8,128)(2,1)S(1)}, u32[]{:S(2)}, u32[]{:S(2)}) collective-permute-start(bf16[434,128]{1,0:T(8,128)(2,1)} %bitcast.33), channel_id=1, source_target_pairs={{0,2},{1,5},{2,0},{3,7},{4,6},{5,1},{6,4},{7,3},{8,10},{9,13},{10,... | collective-permute-start | bytes 333320 | tf_op jit(solution)/shard_map/ppermute | solution.py:393
  12.8 4.8 %collective-permute-start.5 = (bf16[1,434,128]{2,1,0:T(8,128)(2,1)S(1)}, bf16[1,434,128]{2,1,0:T(8,128)(2,1)S(1)}, u32[]{:S(2)}, u32[]{:S(2)}) collective-permute-start(bf16[1,434,128]{2,1,0:T(8,128)(2,1)S(1)} %bitcast.35), channel_id=1, source_target_pairs={{0,2},{1,5},{2,0},{3,7},{4,6},{5,1},{6,4},{7,3},{8,10},{9,13},{10,... | collective-permute-start | bytes 333320 | tf_op jit(solution)/shard_map/ppermute | solution.py:393
  15.4 1.7 %copy-start.1 = (bf16[2,197,384]{2,0,1:T(2,128)(2,1)S(1)}, bf16[2,197,384]{2,0,1:T(2,128)(2,1)}, u32[]{:S(2)}) copy-start(bf16[2,197,384]{2,0,1:T(2,128)(2,1)} %param.6) | copy-start | bytes 907780
  15.4 8.4 %collective-permute-start.2 = (bf16[2,434,128]{2,1,0:T(8,128)(2,1)S(1)}, bf16[2,434,128]{2,1,0:T(8,128)(2,1)S(1)}, u32[]{:S(2)}, u32[]{:S(2)}) collective-permute-start(bf16[2,434,128]{2,1,0:T(8,128)(2,1)S(1)} %pad_maximum_fusion.2), channel_id=1, source_target_pairs={{0,2},{1,5},{2,0},{3,7},{4,6},{5,1},{6,4},{7,3},{8,10},{9,13},{10,... | collective-permute-start | bytes 666632 | tf_op jit(solution)/shard_map/ppermute | solution.py:393
  17.1 0.9 %copy-start.2 = (bf16[55552]{0:T(1024)(128)(2,1)S(1)}, bf16[55552]{0:T(1024)(128)(2,1)}, u32[]{:S(2)}) copy-start(bf16[55552]{0:T(1024)(128)(2,1)} %param.5) | copy-start | bytes 333316
  18.1 8.5 %collective-permute-start.6 = (bf16[4,434,128]{2,1,0:T(8,128)(2,1)S(1)}, bf16[4,434,128]{2,1,0:T(8,128)(2,1)S(1)}, u32[]{:S(2)}, u32[]{:S(2)}) collective-permute-start(bf16[4,434,128]{2,1,0:T(8,128)(2,1)S(1)} %pad_maximum_fusion.1.refs_4_), channel_id=1, source_target_pairs={{0,4},{1,3},{2,6},{3,1},{4,0},{5,7},{6,2},{7,5},{8,12},{9,11},{10,... | collective-permute-start | bytes 1333256 | tf_op jit(solution)/shard_map/ppermute | solution.py:393
  23.8 8.5 %collective-permute-start.9 = (bf16[4,434,128]{2,1,0:T(8,128)(2,1)S(1)}, bf16[4,434,128]{2,1,0:T(8,128)(2,1)S(1)}, u32[]{:S(2)}, u32[]{:S(2)}) collective-permute-start(bf16[4,434,128]{2,1,0:T(8,128)(2,1)S(1)} %pad_maximum_fusion.refs_8_), channel_id=1, source_target_pairs={{0,4},{1,3},{2,6},{3,1},{4,0},{5,7},{6,2},{7,5},{8,12},{9,11},{10,... | collective-permute-start | bytes 1333256 | tf_op jit(solution)/shard_map/ppermute | solution.py:393
  25.5 7.4 %collective-permute-start.7 = (bf16[4,434,128]{2,1,0:T(8,128)(2,1)S(1)}, bf16[4,434,128]{2,1,0:T(8,128)(2,1)S(1)}, u32[]{:S(2)}, u32[]{:S(2)}) collective-permute-start(bf16[4,434,128]{2,1,0:T(8,128)(2,1)S(1)} %pad_maximum_fusion.1.refs_4_), channel_id=1, source_target_pairs={{0,1},{1,0},{2,3},{3,2},{4,5},{5,4},{6,7},{7,6},{8,9},{9,8},{10,11... | collective-permute-start | bytes 1333256 | tf_op jit(solution)/shard_map/ppermute | solution.py:393
  25.5 7.4 %collective-permute-start.10 = (bf16[4,434,128]{2,1,0:T(8,128)(2,1)S(1)}, bf16[4,434,128]{2,1,0:T(8,128)(2,1)S(1)}, u32[]{:S(2)}, u32[]{:S(2)}) collective-permute-start(bf16[4,434,128]{2,1,0:T(8,128)(2,1)S(1)} %pad_maximum_fusion.refs_8_), channel_id=1, source_target_pairs={{0,1},{1,0},{2,3},{3,2},{4,5},{5,4},{6,7},{7,6},{8,9},{9,8},{10,11... | collective-permute-start | bytes 1333256 | tf_op jit(solution)/shard_map/ppermute | solution.py:393
  26.6 6.4 %collective-permute-start.8 = (bf16[4,434,128]{2,1,0:T(8,128)(2,1)S(1)}, bf16[4,434,128]{2,1,0:T(8,128)(2,1)}, u32[]{:S(2)}, u32[]{:S(2)}) collective-permute-start(bf16[4,434,128]{2,1,0:T(8,128)(2,1)S(1)} %collective-permute-done.6.refs_5_), channel_id=1, source_target_pairs={{0,1},{1,0},{2,3},{3,2},{4,5},{5,4},{6,7},{7,6},{8,9},{9,8},{10,11... | collective-permute-start | bytes 1333256 | tf_op jit(solution)/shard_map/ppermute | solution.py:393
  32.3 1.9 %collective-permute-start.11 = (bf16[4,434,128]{2,1,0:T(8,128)(2,1)S(1)}, bf16[4,434,128]{2,1,0:T(8,128)(2,1)}, u32[]{:S(2)}, u32[]{:S(2)}) collective-permute-start(bf16[4,434,128]{2,1,0:T(8,128)(2,1)S(1)} %collective-permute-done.9.refs_9_), channel_id=1, source_target_pairs={{0,1},{1,0},{2,3},{3,2},{4,5},{5,4},{6,7},{7,6},{8,9},{9,8},{10,11... | collective-permute-start | bytes 1333256 | tf_op jit(solution)/shard_map/ppermute | solution.py:393
  50.6 1.9 %collective-permute-start.14 = (bf16[4,434,128]{2,1,0:T(8,128)(2,1)S(1)}, bf16[4,434,128]{2,1,0:T(8,128)(2,1)S(1)}, u32[]{:S(2)}, u32[]{:S(2)}) collective-permute-start(bf16[4,434,128]{2,1,0:T(8,128)(2,1)S(1)} %get-tuple-element.29), channel_id=1, source_target_pairs={{0,1},{1,0},{2,3},{3,2},{4,5},{5,4},{6,7},{7,6},{8,9},{9,8},{10,11... | collective-permute-start | bytes 1333256 | tf_op jit(solution)/shard_map/ppermute | solution.py:393
  50.8 3.5 %collective-permute-start.17 = (bf16[4,434,128]{2,1,0:T(8,128)(2,1)S(1)}, bf16[4,434,128]{2,1,0:T(8,128)(2,1)S(1)}, u32[]{:S(2)}, u32[]{:S(2)}) collective-permute-start(bf16[4,434,128]{2,1,0:T(8,128)(2,1)S(1)} %get-tuple-element.31), channel_id=1, source_target_pairs={{0,1},{1,0},{2,3},{3,2},{4,5},{5,4},{6,7},{7,6},{8,9},{9,8},{10,11... | collective-permute-start | bytes 1333256 | tf_op jit(solution)/shard_map/ppermute | solution.py:393
  51.1 3.8 %collective-permute-start.13 = (bf16[4,434,128]{2,1,0:T(8,128)(2,1)S(1)}, bf16[4,434,128]{2,1,0:T(8,128)(2,1)S(1)}, u32[]{:S(2)}, u32[]{:S(2)}) collective-permute-start(bf16[4,434,128]{2,1,0:T(8,128)(2,1)S(1)} %get-tuple-element.27), channel_id=1, source_target_pairs={{0,1},{1,0},{2,3},{3,2},{4,5},{5,4},{6,7},{7,6},{8,9},{9,8},{10,11... | collective-permute-start | bytes 1333256 | tf_op jit(solution)/shard_map/ppermute | solution.py:393
  52.6 8.5 %collective-permute-start.15 = (bf16[4,434,128]{2,1,0:T(8,128)(2,1)S(1)}, bf16[4,434,128]{2,1,0:T(8,128)(2,1)S(1)}, u32[]{:S(2)}, u32[]{:S(2)}) collective-permute-start(bf16[4,434,128]{2,1,0:T(8,128)(2,1)S(1)} %add_convert_fusion.1), channel_id=1, source_target_pairs={{0,4},{1,3},{2,6},{3,1},{4,0},{5,7},{6,2},{7,5},{8,12},{9,11},{10,... | collective-permute-start | bytes 1333256 | tf_op jit(solution)/shard_map/ppermute | solution.py:393
  54.4 13.9 %collective-permute-start.18 = (bf16[4,434,128]{2,1,0:T(8,128)(2,1)S(1)}, bf16[4,434,128]{2,1,0:T(8,128)(2,1)S(1)}, u32[]{:S(2)}, u32[]{:S(2)}) collective-permute-start(bf16[4,434,128]{2,1,0:T(8,128)(2,1)S(1)} %add_convert_fusion), channel_id=1, source_target_pairs={{0,4},{1,3},{2,6},{3,1},{4,0},{5,7},{6,2},{7,5},{8,12},{9,11},{10,... | collective-permute-start | bytes 1333256 | tf_op jit(solution)/shard_map/ppermute | solution.py:393
  61.2 7.0 %collective-permute-start.16 = (bf16[2,434,128]{2,1,0:T(8,128)(2,1)S(1)}, bf16[2,434,128]{2,1,0:T(8,128)(2,1)S(1)}, u32[]{:S(2)}, u32[]{:S(2)}) collective-permute-start(bf16[2,434,128]{2,1,0:T(8,128)(2,1)S(1)} %slice.66), channel_id=1, source_target_pairs={{0,2},{1,5},{2,0},{3,7},{4,6},{5,1},{6,4},{7,3},{8,10},{9,13},{10,... | collective-permute-start | bytes 666632 | tf_op jit(solution)/shard_map/ppermute | solution.py:393
  62.9 6.0 %collective-permute-start.12 = (bf16[4,434,128]{2,1,0:T(8,128)(2,1)S(1)}, bf16[4,434,128]{2,1,0:T(8,128)(2,1)S(1)}, u32[]{:S(2)}, u32[]{:S(2)}) collective-permute-start(bf16[4,434,128]{2,1,0:T(8,128)(2,1)S(1)} %get-tuple-element.25), channel_id=1, source_target_pairs={{0,1},{1,0},{2,3},{3,2},{4,5},{5,4},{6,7},{7,6},{8,9},{9,8},{10,11... | collective-permute-start | bytes 1333256 | tf_op jit(solution)/shard_map/ppermute | solution.py:393
  68.3 5.0 %collective-permute-start.21 = (bf16[434,128]{1,0:T(8,128)(2,1)S(1)}, bf16[434,128]{1,0:T(8,128)(2,1)S(1)}, u32[]{:S(2)}, u32[]{:S(2)}) collective-permute-start(bf16[434,128]{1,0:T(8,128)(2,1)S(1)} %fusion.6), channel_id=1, source_target_pairs={{0,8},{1,9},{2,10},{3,11},{4,12},{5,13},{6,14},{7,15},{8,0},{9,1},... | collective-permute-start | bytes 333320 | tf_op jit(solution)/shard_map/ppermute | solution.py:393
  69.1 6.5 %collective-permute-start.19 = (bf16[2,434,128]{2,1,0:T(8,128)(2,1)S(1)}, bf16[2,434,128]{2,1,0:T(8,128)(2,1)S(1)}, u32[]{:S(2)}, u32[]{:S(2)}) collective-permute-start(bf16[2,434,128]{2,1,0:T(8,128)(2,1)S(1)} %slice.65), channel_id=1, source_target_pairs={{0,2},{1,5},{2,0},{3,7},{4,6},{5,1},{6,4},{7,3},{8,10},{9,13},{10,... | collective-permute-start | bytes 666632 | tf_op jit(solution)/shard_map/ppermute | solution.py:393
  73.3 7.5 %collective-permute-start.22 = (bf16[434,128]{1,0:T(8,128)(2,1)S(1)}, bf16[434,128]{1,0:T(8,128)(2,1)S(1)}, u32[]{:S(2)}, u32[]{:S(2)}) collective-permute-start(bf16[434,128]{1,0:T(8,128)(2,1)S(1)} %fusion.1), channel_id=1, source_target_pairs={{0,16},{1,17},{2,18},{3,19},{4,20},{5,21},{6,22},{7,23},{8,24},{9,... | collective-permute-start | bytes 333320 | tf_op jit(solution)/shard_map/ppermute | solution.py:393
  75.6 6.1 %collective-permute-start.20 = (bf16[434,128]{1,0:T(8,128)(2,1)S(1)}, bf16[434,128]{1,0:T(8,128)(2,1)S(1)}, u32[]{:S(2)}, u32[]{:S(2)}) collective-permute-start(bf16[434,128]{1,0:T(8,128)(2,1)S(1)} %fusion.5), channel_id=1, source_target_pairs={{0,8},{1,9},{2,10},{3,11},{4,12},{5,13},{6,14},{7,15},{8,0},{9,1},... | collective-permute-start | bytes 333320 | tf_op jit(solution)/shard_map/ppermute | solution.py:393

commit v5 on v4

--- a/solution.py
+++ b/solution.py
@@ -113,7 +113,7 @@
     me = me_ref[0]
     total = images * pad
     scale = float(D // HEADS) ** (-0.5)
-    blk = 32
+    blk = 16
     steps = total // blk
     plane = me >> 3
 

time: 82.6 us -> 82.7 us (level)
  no operation moved by 1% of the time
where the time goes in v5:
time: 82.7 us; the launch traced here: 82.5 us
  waiting for transfers between devices  36 us (44%)
  starting transfers between devices  24.5 us (30%)
  Pallas kernels  16.4 us (20%)
  local copies, waits for them, and re-layouts  2.65 us (3%)
  other arithmetic  1.54 us (2%)
  between operations  1.47 us (2%)
    ppermute x23, waiting for transfers between devices, permute(): return lax.ppermute(value, 'dp', [(i, partner(i)) for i in range(devices)])  36 us
    ppermute x23, starting transfers between devices, permute(): return lax.ppermute(value, 'dp', [(i, partner(i)) for i in range(devices)])  24.5 us
    pallas_call x1, Pallas kernels, run_layer(): pl.pallas_call(body, name='layer', out_shape=(act, act) + parts, in_specs...  16.4 us
    unnamed x10, local copies, waits for them, and re-layouts  2.46 us
  transfers between devices with their start and end apart: 23, of which 13 were waited for; matrix products, arithmetic and copies ran while one was open for 4% of the time, Pallas kernels for 0%

profile of v5, /device:TPU:0, one launch (start us, length us, event | category | flops | bytes accessed | tf_op | source)
XLA Modules:
  0.0 82.5 jit_solution(10855574269064260263)
XLA Ops:
  0.6 4.1 %collective-permute-start = (bf16[434,128]{1,0:T(8,128)(2,1)}, bf16[434,128]{1,0:T(8,128)(2,1)S(1)}, u32[]{:S(2)}, u32[]{:S(2)}) collective-permute-start(bf16[434,128]{1,0:T(8,128)(2,1)} %bitcast.31), channel_id=1, source_target_pairs={{0,16},{1,17},{2,18},{3,19},{4,20},{5,21},{6,22},{7,23},{8,24},{9,... | collective-permute-start | bytes 333320 | tf_op jit(solution)/shard_map/ppermute | solution.py:393
  4.7 1.6 %collective-permute-start.3 = (bf16[434,128]{1,0:T(8,128)(2,1)}, bf16[434,128]{1,0:T(8,128)(2,1)S(1)}, u32[]{:S(2)}, u32[]{:S(2)}) collective-permute-start(bf16[434,128]{1,0:T(8,128)(2,1)} %bitcast.32), channel_id=1, source_target_pairs={{0,8},{1,9},{2,10},{3,11},{4,12},{5,13},{6,14},{7,15},{8,0},{9,1},... | collective-permute-start | bytes 333320 | tf_op jit(solution)/shard_map/ppermute | solution.py:393
  6.3 4.3 %collective-permute-done = bf16[434,128]{1,0:T(8,128)(2,1)S(1)} collective-permute-done((bf16[434,128]{1,0:T(8,128)(2,1)}, bf16[434,128]{1,0:T(8,128)(2,1)S(1)}, u32[]{:S(2)}, u32[]{:S(2)}) %collective-permute-start) | collective-permute-done | bytes 111136 | tf_op jit(solution)/shard_map/ppermute | solution.py:393
  10.6 0.7 collective-permute-start.1
  11.3 1.5 %collective-permute-start.4 = (bf16[434,128]{1,0:T(8,128)(2,1)}, bf16[434,128]{1,0:T(8,128)(2,1)S(1)}, u32[]{:S(2)}, u32[]{:S(2)}) collective-permute-start(bf16[434,128]{1,0:T(8,128)(2,1)} %bitcast.33), channel_id=1, source_target_pairs={{0,2},{1,5},{2,0},{3,7},{4,6},{5,1},{6,4},{7,3},{8,10},{9,13},{10,... | collective-permute-start | bytes 333320 | tf_op jit(solution)/shard_map/ppermute | solution.py:393
  12.8 0.5 collective-permute-start.5
  13.3 2.0 %collective-permute-done.1 = bf16[434,128]{1,0:T(8,128)(2,1)S(1)} collective-permute-done((bf16[434,128]{1,0:T(8,128)(2,1)S(1)}, bf16[434,128]{1,0:T(8,128)(2,1)S(1)}, u32[]{:S(2)}, u32[]{:S(2)}) %collective-permute-start.1) | collective-permute-done | bytes 111136 | tf_op jit(solution)/shard_map/ppermute | solution.py:393
  15.4 1.6 %collective-permute-start.2 = (bf16[2,434,128]{2,1,0:T(8,128)(2,1)S(1)}, bf16[2,434,128]{2,1,0:T(8,128)(2,1)S(1)}, u32[]{:S(2)}, u32[]{:S(2)}) collective-permute-start(bf16[2,434,128]{2,1,0:T(8,128)(2,1)S(1)} %pad_maximum_fusion.2), channel_id=1, source_target_pairs={{0,2},{1,5},{2,0},{3,7},{4,6},{5,1},{6,4},{7,3},{8,10},{9,13},{10,... | collective-permute-start | bytes 666632 | tf_op jit(solution)/shard_map/ppermute | solution.py:393
  18.1 1.6 %collective-permute-start.6 = (bf16[4,434,128]{2,1,0:T(8,128)(2,1)S(1)}, bf16[4,434,128]{2,1,0:T(8,128)(2,1)S(1)}, u32[]{:S(2)}, u32[]{:S(2)}) collective-permute-start(bf16[4,434,128]{2,1,0:T(8,128)(2,1)S(1)} %pad_maximum_fusion.1.refs_4_), channel_id=1, source_target_pairs={{0,4},{1,3},{2,6},{3,1},{4,0},{5,7},{6,2},{7,5},{8,12},{9,11},{10,... | collective-permute-start | bytes 1333256 | tf_op jit(solution)/shard_map/ppermute | solution.py:393
  19.7 4.1 %collective-permute-done.2 = bf16[2,434,128]{2,1,0:T(8,128)(2,1)S(1)} collective-permute-done((bf16[2,434,128]{2,1,0:T(8,128)(2,1)S(1)}, bf16[2,434,128]{2,1,0:T(8,128)(2,1)S(1)}, u32[]{:S(2)}, u32[]{:S(2)}) %collective-permute-start.2) | collective-permute-done | bytes 222240 | tf_op jit(solution)/shard_map/ppermute | solution.py:393
  23.8 1.7 %collective-permute-start.9 = (bf16[4,434,128]{2,1,0:T(8,128)(2,1)S(1)}, bf16[4,434,128]{2,1,0:T(8,128)(2,1)S(1)}, u32[]{:S(2)}, u32[]{:S(2)}) collective-permute-start(bf16[4,434,128]{2,1,0:T(8,128)(2,1)S(1)} %pad_maximum_fusion.refs_8_), channel_id=1, source_target_pairs={{0,4},{1,3},{2,6},{3,1},{4,0},{5,7},{6,2},{7,5},{8,12},{9,11},{10,... | collective-permute-start | bytes 1333256 | tf_op jit(solution)/shard_map/ppermute | solution.py:393
  25.5 0.5 collective-permute-start.10
  26.0 0.5 collective-permute-done.6.refs_5_
  26.6 5.7 %collective-permute-done.9.refs_9_ = bf16[4,434,128]{2,1,0:T(8,128)(2,1)S(1)} collective-permute-done((bf16[4,434,128]{2,1,0:T(8,128)(2,1)S(1)}, bf16[4,434,128]{2,1,0:T(8,128)(2,1)S(1)}, u32[]{:S(2)}, u32[]{:S(2)}) %collective-permute-start.9) | collective-permute-done | bytes 444448 | tf_op jit(solution)/shard_map/ppermute | solution.py:393
  33.0 1.2 %collective-permute-done.11.refs_11_ = bf16[4,434,128]{2,1,0:T(8,128)(2,1)} collective-permute-done((bf16[4,434,128]{2,1,0:T(8,128)(2,1)S(1)}, bf16[4,434,128]{2,1,0:T(8,128)(2,1)}, u32[]{:S(2)}, u32[]{:S(2)}) %collective-permute-start.11) | collective-permute-done | bytes 444448 | tf_op jit(solution)/shard_map/ppermute | solution.py:393
  34.2 16.4 %layer.1 = (bf16[2,197,384]{2,1,0:T(8,128)(2,1)S(1)}, bf16[2,197,384]{2,1,0:T(8,128)(2,1)S(1)}, bf16[4,434,128]{2,1,0:T(8,128)(2,1)S(1)}, bf16[4,434,128]{2,1,0:...) custom-call(s32[1]{0:T(128)} %bitcast.refs_0_, ...), custom_call_target="tpu_custom_call" | custom-call | tf_op jit(solution)/shard_map/layer/pallas_call | solution.py:380
  51.3 1.2 %collective-permute-done.14 = bf16[4,434,128]{2,1,0:T(8,128)(2,1)S(1)} collective-permute-done((bf16[4,434,128]{2,1,0:T(8,128)(2,1)S(1)}, bf16[4,434,128]{2,1,0:T(8,128)(2,1)S(1)}, u32[]{:S(2)}, u32[]{:S(2)}) %collective-permute-start.14) | collective-permute-done | bytes 444448 | tf_op jit(solution)/shard_map/ppermute | solution.py:393
  52.6 1.7 %collective-permute-start.15 = (bf16[4,434,128]{2,1,0:T(8,128)(2,1)S(1)}, bf16[4,434,128]{2,1,0:T(8,128)(2,1)S(1)}, u32[]{:S(2)}, u32[]{:S(2)}) collective-permute-start(bf16[4,434,128]{2,1,0:T(8,128)(2,1)S(1)} %add_convert_fusion.1), channel_id=1, source_target_pairs={{0,4},{1,3},{2,6},{3,1},{4,0},{5,7},{6,2},{7,5},{8,12},{9,11},{10,... | collective-permute-start | bytes 1333256 | tf_op jit(solution)/shard_map/ppermute | solution.py:393
  54.4 0.5 collective-permute-start.18
  54.9 6.1 %collective-permute-done.15 = bf16[4,434,128]{2,1,0:T(8,128)(2,1)S(1)} collective-permute-done((bf16[4,434,128]{2,1,0:T(8,128)(2,1)S(1)}, bf16[4,434,128]{2,1,0:T(8,128)(2,1)S(1)}, u32[]{:S(2)}, u32[]{:S(2)}) %collective-permute-start.15) | collective-permute-done | bytes 444448 | tf_op jit(solution)/shard_map/ppermute | solution.py:393
  61.2 1.7 %collective-permute-start.16 = (bf16[2,434,128]{2,1,0:T(8,128)(2,1)S(1)}, bf16[2,434,128]{2,1,0:T(8,128)(2,1)S(1)}, u32[]{:S(2)}, u32[]{:S(2)}) collective-permute-start(bf16[2,434,128]{2,1,0:T(8,128)(2,1)S(1)} %slice.66), channel_id=1, source_target_pairs={{0,2},{1,5},{2,0},{3,7},{4,6},{5,1},{6,4},{7,3},{8,10},{9,13},{10,... | collective-permute-start | bytes 666632 | tf_op jit(solution)/shard_map/ppermute | solution.py:393
  62.9 5.3 %collective-permute-done.18 = bf16[4,434,128]{2,1,0:T(8,128)(2,1)S(1)} collective-permute-done((bf16[4,434,128]{2,1,0:T(8,128)(2,1)S(1)}, bf16[4,434,128]{2,1,0:T(8,128)(2,1)S(1)}, u32[]{:S(2)}, u32[]{:S(2)}) %collective-permute-start.18) | collective-permute-done | bytes 444448 | tf_op jit(solution)/shard_map/ppermute | solution.py:393
  68.3 0.6 collective-permute-start.21
  69.1 1.6 %collective-permute-start.19 = (bf16[2,434,128]{2,1,0:T(8,128)(2,1)S(1)}, bf16[2,434,128]{2,1,0:T(8,128)(2,1)S(1)}, u32[]{:S(2)}, u32[]{:S(2)}) collective-permute-start(bf16[2,434,128]{2,1,0:T(8,128)(2,1)S(1)} %slice.65), channel_id=1, source_target_pairs={{0,2},{1,5},{2,0},{3,7},{4,6},{5,1},{6,4},{7,3},{8,10},{9,13},{10,... | collective-permute-start | bytes 666632 | tf_op jit(solution)/shard_map/ppermute | solution.py:393
  70.7 2.7 %collective-permute-done.21 = bf16[434,128]{1,0:T(8,128)(2,1)S(1)} collective-permute-done((bf16[434,128]{1,0:T(8,128)(2,1)S(1)}, bf16[434,128]{1,0:T(8,128)(2,1)S(1)}, u32[]{:S(2)}, u32[]{:S(2)}) %collective-permute-start.21) | collective-permute-done | bytes 111136 | tf_op jit(solution)/shard_map/ppermute | solution.py:393
  73.4 2.2 %collective-permute-start.22 = (bf16[434,128]{1,0:T(8,128)(2,1)S(1)}, bf16[434,128]{1,0:T(8,128)(2,1)S(1)}, u32[]{:S(2)}, u32[]{:S(2)}) collective-permute-start(bf16[434,128]{1,0:T(8,128)(2,1)S(1)} %fusion.1), channel_id=1, source_target_pairs={{0,16},{1,17},{2,18},{3,19},{4,20},{5,21},{6,22},{7,23},{8,24},{9,... | collective-permute-start | bytes 333320 | tf_op jit(solution)/shard_map/ppermute | solution.py:393
  75.7 1.8 %collective-permute-start.20 = (bf16[434,128]{1,0:T(8,128)(2,1)S(1)}, bf16[434,128]{1,0:T(8,128)(2,1)S(1)}, u32[]{:S(2)}, u32[]{:S(2)}) collective-permute-start(bf16[434,128]{1,0:T(8,128)(2,1)S(1)} %fusion.5), channel_id=1, source_target_pairs={{0,8},{1,9},{2,10},{3,11},{4,12},{5,13},{6,14},{7,15},{8,0},{9,1},... | collective-permute-start | bytes 333320 | tf_op jit(solution)/shard_map/ppermute | solution.py:393
  77.5 0.9 %copy.9 = bf16[2,197,384]{2,0,1:T(2,128)(2,1)} copy(bf16[2,197,384]{2,1,0:T(8,128)(2,1)S(1)} %get-tuple-element.35) | data formatting | bytes 605184
  78.4 0.9 %copy.10 = bf16[2,197,384]{2,0,1:T(2,128)(2,1)} copy(bf16[2,197,384]{2,1,0:T(8,128)(2,1)S(1)} %get-tuple-element.36) | data formatting | bytes 605184
  79.4 1.5 %collective-permute-done.22 = bf16[434,128]{1,0:T(8,128)(2,1)S(1)} collective-permute-done((bf16[434,128]{1,0:T(8,128)(2,1)S(1)}, bf16[434,128]{1,0:T(8,128)(2,1)S(1)}, u32[]{:S(2)}, u32[]{:S(2)}) %collective-permute-start.22) | collective-permute-done | bytes 111136 | tf_op jit(solution)/shard_map/ppermute | solution.py:393
  80.9 0.9 %collective-permute-done.20 = bf16[434,128]{1,0:T(8,128)(2,1)S(1)} collective-permute-done((bf16[434,128]{1,0:T(8,128)(2,1)S(1)}, bf16[434,128]{1,0:T(8,128)(2,1)S(1)}, u32[]{:S(2)}, u32[]{:S(2)}) %collective-permute-start.20) | collective-permute-done | bytes 111136 | tf_op jit(solution)/shard_map/ppermute | solution.py:393
  81.8 0.7 fusion.4
  (43 shorter events, 2.7 us)
Async XLA Ops:
  0.6 16.4 %copy-start = (bf16[2,197,384]{2,0,1:T(2,128)(2,1)S(1)}, bf16[2,197,384]{2,0,1:T(2,128)(2,1)}, u32[]{:S(2)}) copy-start(bf16[2,197,384]{2,0,1:T(2,128)(2,1)} %param.4) | copy-start | bytes 907780
  0.6 9.9 %collective-permute-start = (bf16[434,128]{1,0:T(8,128)(2,1)}, bf16[434,128]{1,0:T(8,128)(2,1)S(1)}, u32[]{:S(2)}, u32[]{:S(2)}) collective-permute-start(bf16[434,128]{1,0:T(8,128)(2,1)} %bitcast.31), channel_id=1, source_target_pairs={{0,16},{1,17},{2,18},{3,19},{4,20},{5,21},{6,22},{7,23},{8,24},{9,... | collective-permute-start | bytes 333320 | tf_op jit(solution)/shard_map/ppermute | solution.py:393
  4.7 8.0 %collective-permute-start.3 = (bf16[434,128]{1,0:T(8,128)(2,1)}, bf16[434,128]{1,0:T(8,128)(2,1)S(1)}, u32[]{:S(2)}, u32[]{:S(2)}) collective-permute-start(bf16[434,128]{1,0:T(8,128)(2,1)} %bitcast.32), channel_id=1, source_target_pairs={{0,8},{1,9},{2,10},{3,11},{4,12},{5,13},{6,14},{7,15},{8,0},{9,1},... | collective-permute-start | bytes 333320 | tf_op jit(solution)/shard_map/ppermute | solution.py:393
  10.6 4.8 %collective-permute-start.1 = (bf16[434,128]{1,0:T(8,128)(2,1)S(1)}, bf16[434,128]{1,0:T(8,128)(2,1)S(1)}, u32[]{:S(2)}, u32[]{:S(2)}) collective-permute-start(bf16[434,128]{1,0:T(8,128)(2,1)S(1)} %collective-permute-done), channel_id=1, source_target_pairs={{0,8},{1,9},{2,10},{3,11},{4,12},{5,13},{6,14},{7,15},{8,0},{9,1},... | collective-permute-start | bytes 333320 | tf_op jit(solution)/shard_map/ppermute | solution.py:393
  11.3 5.9 %collective-permute-start.4 = (bf16[434,128]{1,0:T(8,128)(2,1)}, bf16[434,128]{1,0:T(8,128)(2,1)S(1)}, u32[]{:S(2)}, u32[]{:S(2)}) collective-permute-start(bf16[434,128]{1,0:T(8,128)(2,1)} %bitcast.33), channel_id=1, source_target_pairs={{0,2},{1,5},{2,0},{3,7},{4,6},{5,1},{6,4},{7,3},{8,10},{9,13},{10,... | collective-permute-start | bytes 333320 | tf_op jit(solution)/shard_map/ppermute | solution.py:393
  12.8 4.8 %collective-permute-start.5 = (bf16[1,434,128]{2,1,0:T(8,128)(2,1)S(1)}, bf16[1,434,128]{2,1,0:T(8,128)(2,1)S(1)}, u32[]{:S(2)}, u32[]{:S(2)}) collective-permute-start(bf16[1,434,128]{2,1,0:T(8,128)(2,1)S(1)} %bitcast.35), channel_id=1, source_target_pairs={{0,2},{1,5},{2,0},{3,7},{4,6},{5,1},{6,4},{7,3},{8,10},{9,13},{10,... | collective-permute-start | bytes 333320 | tf_op jit(solution)/shard_map/ppermute | solution.py:393
  15.4 1.7 %copy-start.1 = (bf16[2,197,384]{2,0,1:T(2,128)(2,1)S(1)}, bf16[2,197,384]{2,0,1:T(2,128)(2,1)}, u32[]{:S(2)}) copy-start(bf16[2,197,384]{2,0,1:T(2,128)(2,1)} %param.6) | copy-start | bytes 907780
  15.4 8.4 %collective-permute-start.2 = (bf16[2,434,128]{2,1,0:T(8,128)(2,1)S(1)}, bf16[2,434,128]{2,1,0:T(8,128)(2,1)S(1)}, u32[]{:S(2)}, u32[]{:S(2)}) collective-permute-start(bf16[2,434,128]{2,1,0:T(8,128)(2,1)S(1)} %pad_maximum_fusion.2), channel_id=1, source_target_pairs={{0,2},{1,5},{2,0},{3,7},{4,6},{5,1},{6,4},{7,3},{8,10},{9,13},{10,... | collective-permute-start | bytes 666632 | tf_op jit(solution)/shard_map/ppermute | solution.py:393
  17.1 0.9 %copy-start.2 = (bf16[55552]{0:T(1024)(128)(2,1)S(1)}, bf16[55552]{0:T(1024)(128)(2,1)}, u32[]{:S(2)}) copy-start(bf16[55552]{0:T(1024)(128)(2,1)} %param.5) | copy-start | bytes 333316
  18.1 8.5 %collective-permute-start.6 = (bf16[4,434,128]{2,1,0:T(8,128)(2,1)S(1)}, bf16[4,434,128]{2,1,0:T(8,128)(2,1)S(1)}, u32[]{:S(2)}, u32[]{:S(2)}) collective-permute-start(bf16[4,434,128]{2,1,0:T(8,128)(2,1)S(1)} %pad_maximum_fusion.1.refs_4_), channel_id=1, source_target_pairs={{0,4},{1,3},{2,6},{3,1},{4,0},{5,7},{6,2},{7,5},{8,12},{9,11},{10,... | collective-permute-start | bytes 1333256 | tf_op jit(solution)/shard_map/ppermute | solution.py:393
  23.8 8.5 %collective-permute-start.9 = (bf16[4,434,128]{2,1,0:T(8,128)(2,1)S(1)}, bf16[4,434,128]{2,1,0:T(8,128)(2,1)S(1)}, u32[]{:S(2)}, u32[]{:S(2)}) collective-permute-start(bf16[4,434,128]{2,1,0:T(8,128)(2,1)S(1)} %pad_maximum_fusion.refs_8_), channel_id=1, source_target_pairs={{0,4},{1,3},{2,6},{3,1},{4,0},{5,7},{6,2},{7,5},{8,12},{9,11},{10,... | collective-permute-start | bytes 1333256 | tf_op jit(solution)/shard_map/ppermute | solution.py:393
  25.5 7.4 %collective-permute-start.7 = (bf16[4,434,128]{2,1,0:T(8,128)(2,1)S(1)}, bf16[4,434,128]{2,1,0:T(8,128)(2,1)S(1)}, u32[]{:S(2)}, u32[]{:S(2)}) collective-permute-start(bf16[4,434,128]{2,1,0:T(8,128)(2,1)S(1)} %pad_maximum_fusion.1.refs_4_), channel_id=1, source_target_pairs={{0,1},{1,0},{2,3},{3,2},{4,5},{5,4},{6,7},{7,6},{8,9},{9,8},{10,11... | collective-permute-start | bytes 1333256 | tf_op jit(solution)/shard_map/ppermute | solution.py:393
  25.5 7.4 %collective-permute-start.10 = (bf16[4,434,128]{2,1,0:T(8,128)(2,1)S(1)}, bf16[4,434,128]{2,1,0:T(8,128)(2,1)S(1)}, u32[]{:S(2)}, u32[]{:S(2)}) collective-permute-start(bf16[4,434,128]{2,1,0:T(8,128)(2,1)S(1)} %pad_maximum_fusion.refs_8_), channel_id=1, source_target_pairs={{0,1},{1,0},{2,3},{3,2},{4,5},{5,4},{6,7},{7,6},{8,9},{9,8},{10,11... | collective-permute-start | bytes 1333256 | tf_op jit(solution)/shard_map/ppermute | solution.py:393
  26.6 6.4 %collective-permute-start.8 = (bf16[4,434,128]{2,1,0:T(8,128)(2,1)S(1)}, bf16[4,434,128]{2,1,0:T(8,128)(2,1)}, u32[]{:S(2)}, u32[]{:S(2)}) collective-permute-start(bf16[4,434,128]{2,1,0:T(8,128)(2,1)S(1)} %collective-permute-done.6.refs_5_), channel_id=1, source_target_pairs={{0,1},{1,0},{2,3},{3,2},{4,5},{5,4},{6,7},{7,6},{8,9},{9,8},{10,11... | collective-permute-start | bytes 1333256 | tf_op jit(solution)/shard_map/ppermute | solution.py:393
  32.3 1.9 %collective-permute-start.11 = (bf16[4,434,128]{2,1,0:T(8,128)(2,1)S(1)}, bf16[4,434,128]{2,1,0:T(8,128)(2,1)}, u32[]{:S(2)}, u32[]{:S(2)}) collective-permute-start(bf16[4,434,128]{2,1,0:T(8,128)(2,1)S(1)} %collective-permute-done.9.refs_9_), channel_id=1, source_target_pairs={{0,1},{1,0},{2,3},{3,2},{4,5},{5,4},{6,7},{7,6},{8,9},{9,8},{10,11... | collective-permute-start | bytes 1333256 | tf_op jit(solution)/shard_map/ppermute | solution.py:393
  50.6 1.9 %collective-permute-start.14 = (bf16[4,434,128]{2,1,0:T(8,128)(2,1)S(1)}, bf16[4,434,128]{2,1,0:T(8,128)(2,1)S(1)}, u32[]{:S(2)}, u32[]{:S(2)}) collective-permute-start(bf16[4,434,128]{2,1,0:T(8,128)(2,1)S(1)} %get-tuple-element.29), channel_id=1, source_target_pairs={{0,1},{1,0},{2,3},{3,2},{4,5},{5,4},{6,7},{7,6},{8,9},{9,8},{10,11... | collective-permute-start | bytes 1333256 | tf_op jit(solution)/shard_map/ppermute | solution.py:393
  50.8 3.5 %collective-permute-start.17 = (bf16[4,434,128]{2,1,0:T(8,128)(2,1)S(1)}, bf16[4,434,128]{2,1,0:T(8,128)(2,1)S(1)}, u32[]{:S(2)}, u32[]{:S(2)}) collective-permute-start(bf16[4,434,128]{2,1,0:T(8,128)(2,1)S(1)} %get-tuple-element.31), channel_id=1, source_target_pairs={{0,1},{1,0},{2,3},{3,2},{4,5},{5,4},{6,7},{7,6},{8,9},{9,8},{10,11... | collective-permute-start | bytes 1333256 | tf_op jit(solution)/shard_map/ppermute | solution.py:393
  51.2 3.8 %collective-permute-start.13 = (bf16[4,434,128]{2,1,0:T(8,128)(2,1)S(1)}, bf16[4,434,128]{2,1,0:T(8,128)(2,1)S(1)}, u32[]{:S(2)}, u32[]{:S(2)}) collective-permute-start(bf16[4,434,128]{2,1,0:T(8,128)(2,1)S(1)} %get-tuple-element.27), channel_id=1, source_target_pairs={{0,1},{1,0},{2,3},{3,2},{4,5},{5,4},{6,7},{7,6},{8,9},{9,8},{10,11... | collective-permute-start | bytes 1333256 | tf_op jit(solution)/shard_map/ppermute | solution.py:393
  52.6 8.5 %collective-permute-start.15 = (bf16[4,434,128]{2,1,0:T(8,128)(2,1)S(1)}, bf16[4,434,128]{2,1,0:T(8,128)(2,1)S(1)}, u32[]{:S(2)}, u32[]{:S(2)}) collective-permute-start(bf16[4,434,128]{2,1,0:T(8,128)(2,1)S(1)} %add_convert_fusion.1), channel_id=1, source_target_pairs={{0,4},{1,3},{2,6},{3,1},{4,0},{5,7},{6,2},{7,5},{8,12},{9,11},{10,... | collective-permute-start | bytes 1333256 | tf_op jit(solution)/shard_map/ppermute | solution.py:393
  54.4 13.9 %collective-permute-start.18 = (bf16[4,434,128]{2,1,0:T(8,128)(2,1)S(1)}, bf16[4,434,128]{2,1,0:T(8,128)(2,1)S(1)}, u32[]{:S(2)}, u32[]{:S(2)}) collective-permute-start(bf16[4,434,128]{2,1,0:T(8,128)(2,1)S(1)} %add_convert_fusion), channel_id=1, source_target_pairs={{0,4},{1,3},{2,6},{3,1},{4,0},{5,7},{6,2},{7,5},{8,12},{9,11},{10,... | collective-permute-start | bytes 1333256 | tf_op jit(solution)/shard_map/ppermute | solution.py:393
  61.2 7.0 %collective-permute-start.16 = (bf16[2,434,128]{2,1,0:T(8,128)(2,1)S(1)}, bf16[2,434,128]{2,1,0:T(8,128)(2,1)S(1)}, u32[]{:S(2)}, u32[]{:S(2)}) collective-permute-start(bf16[2,434,128]{2,1,0:T(8,128)(2,1)S(1)} %slice.66), channel_id=1, source_target_pairs={{0,2},{1,5},{2,0},{3,7},{4,6},{5,1},{6,4},{7,3},{8,10},{9,13},{10,... | collective-permute-start | bytes 666632 | tf_op jit(solution)/shard_map/ppermute | solution.py:393
  62.9 6.0 %collective-permute-start.12 = (bf16[4,434,128]{2,1,0:T(8,128)(2,1)S(1)}, bf16[4,434,128]{2,1,0:T(8,128)(2,1)S(1)}, u32[]{:S(2)}, u32[]{:S(2)}) collective-permute-start(bf16[4,434,128]{2,1,0:T(8,128)(2,1)S(1)} %get-tuple-element.25), channel_id=1, source_target_pairs={{0,1},{1,0},{2,3},{3,2},{4,5},{5,4},{6,7},{7,6},{8,9},{9,8},{10,11... | collective-permute-start | bytes 1333256 | tf_op jit(solution)/shard_map/ppermute | solution.py:393
  68.3 5.0 %collective-permute-start.21 = (bf16[434,128]{1,0:T(8,128)(2,1)S(1)}, bf16[434,128]{1,0:T(8,128)(2,1)S(1)}, u32[]{:S(2)}, u32[]{:S(2)}) collective-permute-start(bf16[434,128]{1,0:T(8,128)(2,1)S(1)} %fusion.6), channel_id=1, source_target_pairs={{0,8},{1,9},{2,10},{3,11},{4,12},{5,13},{6,14},{7,15},{8,0},{9,1},... | collective-permute-start | bytes 333320 | tf_op jit(solution)/shard_map/ppermute | solution.py:393
  69.1 6.5 %collective-permute-start.19 = (bf16[2,434,128]{2,1,0:T(8,128)(2,1)S(1)}, bf16[2,434,128]{2,1,0:T(8,128)(2,1)S(1)}, u32[]{:S(2)}, u32[]{:S(2)}) collective-permute-start(bf16[2,434,128]{2,1,0:T(8,128)(2,1)S(1)} %slice.65), channel_id=1, source_target_pairs={{0,2},{1,5},{2,0},{3,7},{4,6},{5,1},{6,4},{7,3},{8,10},{9,13},{10,... | collective-permute-start | bytes 666632 | tf_op jit(solution)/shard_map/ppermute | solution.py:393
  73.4 7.5 %collective-permute-start.22 = (bf16[434,128]{1,0:T(8,128)(2,1)S(1)}, bf16[434,128]{1,0:T(8,128)(2,1)S(1)}, u32[]{:S(2)}, u32[]{:S(2)}) collective-permute-start(bf16[434,128]{1,0:T(8,128)(2,1)S(1)} %fusion.1), channel_id=1, source_target_pairs={{0,16},{1,17},{2,18},{3,19},{4,20},{5,21},{6,22},{7,23},{8,24},{9,... | collective-permute-start | bytes 333320 | tf_op jit(solution)/shard_map/ppermute | solution.py:393
  75.7 6.1 %collective-permute-start.20 = (bf16[434,128]{1,0:T(8,128)(2,1)S(1)}, bf16[434,128]{1,0:T(8,128)(2,1)S(1)}, u32[]{:S(2)}, u32[]{:S(2)}) collective-permute-start(bf16[434,128]{1,0:T(8,128)(2,1)S(1)} %fusion.5), channel_id=1, source_target_pairs={{0,8},{1,9},{2,10},{3,11},{4,12},{5,13},{6,14},{7,15},{8,0},{9,1},... | collective-permute-start | bytes 333320 | tf_op jit(solution)/shard_map/ppermute | solution.py:393
